TPU v7x, 32 devices: a whole 2x2x4 slice. The times are simulated.
32 devices in a mesh: dp: 2 (over x), row: 4 (over y, core), col: 4 (over z).
Axes of the slice: x: 2, y: 2, z: 4, core: 2. Of those that a mesh axis runs over, the one named last changes fastest.
Arguments:
- tokens: bfloat16 [8, 64, 64, 768], P('dp', 'row', 'col'), may hold values from -6 to 6
- cls_token: bfloat16 [8, 768], P('dp'), may hold values from -6 to 6
- patch_mask: int32 [8, 64, 64], P('dp', 'row', 'col'), may hold values from 0 to 1, as said below
- loss_mask: int32 [8, 64, 64], P('dp', 'row', 'col'), may hold values 0 or 1
- mask_emb: float32 [768], replicated, may hold values from -5 to 5
- ln1_gain: float32 [768], replicated, may hold values from 0.5 to 1.5
- ln1_bias: float32 [768], replicated, may hold values from -1.5 to 1.5
- w_qkv: bfloat16 [768, 2304], replicated, may hold values from -0.21875 to 0.21875
- q_bias: float32 [768], replicated, may hold values from -2.5 to 2.5
- v_bias: float32 [768], replicated, may hold values from -2.5 to 2.5
- rel_table: float32 [12, 50], replicated, may hold values from -4 to 4
- w_out: bfloat16 [768, 768], replicated, may hold values from -0.875 to 0.875
- out_bias: float32 [768], replicated, may hold values from -1.5 to 1.5
- scale_attn: float32 [768], replicated, may hold values from 0.25 to 1.75
- ln2_gain: float32 [768], replicated, may hold values from 0.5 to 1.5
- ln2_bias: float32 [768], replicated, may hold values from -1.5 to 1.5
- w_up: bfloat16 [768, 3072], replicated, may hold values from -0.21875 to 0.21875
- up_bias: float32 [3072], replicated, may hold values from -2.5 to 2.5
- w_down: bfloat16 [3072, 768], replicated, may hold values from -0.109375 to 0.109375
- down_bias: float32 [768], replicated, may hold values from -1.5 to 1.5
- scale_mlp: float32 [768], replicated, may hold values from 0.25 to 1.75
- out_grad: bfloat16 [8, 64, 64, 768], P('dp', 'row', 'col'), may hold values from -6 to 6
Outputs:
- out: bfloat16 [8, 64, 64, 768], P('dp', 'row', 'col')
- out_cls: bfloat16 [8, 768], P('dp')
- d_tokens: float32 [8, 64, 64, 768], P('dp', 'row', 'col')
- d_cls: float32 [8, 768], P('dp')
- d_w_qkv: float32 [768, 2304], P(('row', 'col'), 'dp')
- d_w_out: float32 [768, 768], P(('row', 'col'), 'dp')
- d_w_up: float32 [768, 3072], P(('row', 'col'), 'dp')
- d_w_down: float32 [3072, 768], P(('row', 'col'), 'dp')
- d_mask_emb: float32 [768], replicated
- d_ln1_gain: float32 [768], replicated
- d_ln1_bias: float32 [768], replicated
- d_q_bias: float32 [768], replicated
- d_v_bias: float32 [768], replicated
- d_rel_table: float32 [12, 50], replicated
- d_out_bias: float32 [768], replicated
- d_scale_attn: float32 [768], replicated
- d_ln2_gain: float32 [768], replicated
- d_ln2_bias: float32 [768], replicated
- d_up_bias: float32 [3072], replicated
- d_down_bias: float32 [768], replicated
- d_scale_mlp: float32 [768], replicated
Inputs may be any that keep to these rules, and one draw needn't show every extreme that they name: `patch_mask`: 1 marks a patch that is replaced by the mask embedding. Each page draws its own rate of ones, from 20 to 60 percent. `loss_mask`: 1 marks a patch whose loss counts where it is masked.
All inputs are finite; a program needn't handle non-finite values. No bound on the sum of `loss_mask` on one device may be relied on, other than what follows from the above.
Results may differ from a plain program's by a relative error of at most 0.012.
Values may be sent and summed in bfloat16 or wider, within the bound.
No kernel may reach another device: no remote copies, remote signals or barrier semaphores. Data moves between devices by JAX's collectives and lax.ppermute only.
A program may use at most 832 MiB of HBM per device.

v0:
```python
import functools
import math

import jax
import jax.numpy as jnp
import numpy as np
from jax import lax
from jax.experimental import pallas as pl
from jax.experimental.pallas import tpu as pltpu
from jax.sharding import PartitionSpec as P

F32 = jnp.float32
BF16 = jnp.bfloat16
NEG = -1e30
REACH = 3
SPAN = 7
BAND = 4
SIDE = 8
LANES = 128
FLAG = 1024.0
ROOM, LESS = 56, 28
EPS = 1e-06
MIB = 1 << 20


def dot(a, b):
    return jnp.dot(a, b, preferred_element_type=F32)


def dot_t(a, b):
    return lax.dot_general(a, b, (((1,), (1,)), ((), ())), preferred_element_type=F32)


def dot_0(a, b):
    return lax.dot_general(a, b, (((0,), (0,)), ((), ())), preferred_element_type=F32)


def split3(x):
    hi = x.astype(BF16)
    rest = x - hi.astype(F32)
    mid = rest.astype(BF16)
    low = (rest - mid.astype(F32)).astype(BF16)
    return hi, mid, low


def norm_parts(x):
    c = x - jnp.mean(x, axis=-1, keepdims=True)
    inv = lax.rsqrt(jnp.mean(c * c, axis=-1, keepdims=True) + EPS)
    return c * inv, inv


def norm_pull(e, unit, inv):
    return inv * (
        e
        - jnp.mean(e, axis=-1, keepdims=True)
        - unit * jnp.mean(e * unit, axis=-1, keepdims=True)
    )


def unmask(x, emb):
    return jnp.where(x > FLAG / 2, emb, x)


class Geometry:
    def __init__(self, pages, rows, cols, width, heads):
        self.pages, self.rows, self.cols = pages, rows, cols
        self.width, self.heads = width, heads
        self.head = width // heads
        self.lanes = 256
        self.stack = self.lanes // self.head
        self.groups = width // self.lanes
        self.own = rows * cols
        self.edge = REACH * cols
        self.side = (rows + 2 * REACH) * SIDE
        self.halo = 2 * self.edge + self.side + 16
        self.bands = rows // BAND
        self.band = BAND * cols
        self.main = (BAND + 2 * REACH) * cols
        self.flank = (BAND + 2 * REACH) * SIDE
        self.slots = self.main + self.flank + 16
        self.cls_at = self.main + self.flank
        slot = np.arange(self.slots)
        r = np.where(slot < self.main, slot // cols, (slot - self.main) // SIDE)
        s = (slot - self.main) % SIDE
        c = np.where(
            slot < self.main,
            slot % cols,
            np.where(s < REACH, s - REACH, np.where(s < 2 * REACH, cols + s - REACH, -1000)),
        )
        is_cls = slot >= self.cls_at
        r = np.where(is_cls, -1000, r)
        c = np.where(is_cls, -1000, c)
        self.slot_row, self.slot_col = r, c
        q = np.arange(self.band)
        a = r[None, :] - (q // cols)[:, None]
        b = c[None, :] - (q % cols)[:, None] + REACH
        ok = (a >= 0) & (a < SPAN) & (b >= 0) & (b < SPAN)
        offset = np.where(ok, a * SPAN + b, -1)
        mirror = np.where(ok, SPAN * SPAN - 1 - offset, -1)
        offset[:, self.cls_at] = SPAN * SPAN
        self.offset = offset.astype(np.int32)
        self.mirror = mirror.astype(np.int32)
        fold = np.full((cols, self.slots), -1, np.int32)
        for i in range(cols):
            for lane in range(SPAN * cols):
                d = lane % cols - i + REACH
                if 0 <= d < SPAN:
                    fold[i, lane] = lane // cols * SPAN + d
            for lane in range(SPAN * SIDE):
                s1 = lane % SIDE
                if s1 < 2 * REACH:
                    col = s1 - REACH if s1 < REACH else cols + s1 - REACH
                    d = col - i + REACH
                    if 0 <= d < SPAN:
                        fold[i, self.main + lane] = lane // SIDE * SPAN + d
            fold[i, self.cls_at] = SPAN * SPAN
        self.fold = fold.T.copy()
        lane = np.arange(self.lanes) // self.head
        self.head_mask = (np.arange(16)[:, None] == lane[None, :]).astype(np.float32)
        stat = np.zeros((self.groups, 8, LANES), np.float32)
        every = np.zeros((32, LANES), np.float32)
        for h in range(heads):
            g, k = divmod(h, self.stack)
            for part in range(3):
                stat[g, k, 48 + 16 * part + h] = -1.0
                every[h, 16 * part + h] = -1.0
                every[16 + h, 48 + 16 * part + h] = -1.0
        self.stat_mask = stat
        self.stat_all = every
        self.to_head = (np.arange(width)[:, None] // self.head == np.arange(LANES)[None, :]).astype(
            np.float32
        )
        self.head_rows = self.to_head.T[:16].copy()
        base = np.full((2, cols, self.slots), -1, np.int32)
        for i in range(cols):
            for lane in range(self.slots):
                o = fold[i, lane]
                base[0, i, lane] = o
                base[1, i, lane] = SPAN * SPAN - 1 - o if 0 <= o < SPAN * SPAN else -1
        self.base = base
        tall = rows + 2 * REACH
        self.strip = -(-REACH * tall // 8) * 8
        flank = np.zeros((2, self.side, self.strip), np.float32)
        for r in range(tall):
            for i in range(REACH):
                flank[0, r * SIDE + i, r * REACH + i] = 1.0
                flank[1, r * SIDE + REACH + i, r * REACH + i] = 1.0
        self.flank_of = flank

    def block(self, own, halo, b):
        lo, hi = b * self.band, b * self.band + self.main
        e, o = self.edge, self.own
        parts = []
        if lo < e:
            parts.append(halo[lo : min(hi, e)])
        parts.append(own[max(lo - e, 0) : min(hi - e, o)])
        if hi > e + o:
            parts.append(halo[e + max(lo - e - o, 0) : e + hi - e - o])
        at = 2 * e + b * BAND * SIDE
        parts.append(halo[at : at + self.flank])
        parts.append(halo[2 * e + self.side : 2 * e + self.side + 16])
        return jnp.concatenate(parts, axis=0)

    def around(self, top, bottom, left, right, flank, last):
        side = dot(flank[0], left) + dot(flank[1], right)
        return jnp.concatenate([top, bottom, side.astype(BF16), last], axis=0)

    def stacked(self, x, mask):
        return jnp.concatenate([x * mask[h : h + 1] for h in range(self.stack)], axis=0)

    def unstacked(self, r):
        rows = r.shape[0] // self.stack
        lane = lax.broadcasted_iota(jnp.int32, (rows, self.lanes), 1) // self.head
        out = r[(self.stack - 1) * rows :]
        for h in range(self.stack - 1):
            out = jnp.where(lane == h, r[h * rows : (h + 1) * rows], out)
        return out


def full(shape):
    return pl.BlockSpec(shape, lambda *_: (0,) * len(shape))


def hold(shape):
    return pl.BlockSpec(shape, lambda *_: (0,) * len(shape), pipeline_mode=pl.Buffered(1))


def params(limit, sem=1):
    return pltpu.CompilerParams(
        dimension_semantics=("arbitrary",) * sem, vmem_limit_bytes=limit * MIB
    )


def bias_body(geo, table, index_ref, out_ref):
    lane = lax.broadcasted_iota(jnp.int32, (geo.cols, geo.slots), 1)
    low = jnp.full((geo.cols, geo.slots), NEG, F32)
    index = index_ref[...]
    pair = 2

    def head(i, carry):
        acc = [low] * (2 * pair)
        for o in range(SPAN * SPAN + 1):
            hit = index == o
            for j in range(pair):
                at = 2 * j + o % 2
                acc[at] = jnp.where(hit, table[i * pair + j, o], acc[at])
        for j in range(pair):
            both = jnp.maximum(acc[2 * j], acc[2 * j + 1])
            main = jnp.where(lane < geo.main, both, low)
            side = jnp.where((lane >= geo.main) & (lane < geo.cls_at), both, low)
            last = jnp.where(lane >= geo.cls_at, both, low)
            h = i * pair + j
            for r in range(BAND):
                if r:
                    both = jnp.maximum(
                        pltpu.roll(main, r * geo.cols, 1), pltpu.roll(side, r * SIDE, 1)
                    )
                else:
                    both = jnp.maximum(main, side)
                at = pl.multiple_of(h % geo.stack * geo.band + r * geo.cols, 8)
                out_ref[h // geo.stack, pl.ds(at, geo.cols), :] = jnp.maximum(both, last)
        return carry

    lax.fori_loop(0, geo.heads // pair, head, 0)


def bias_table(geo, rel_table, which):
    return pl.pallas_call(
        functools.partial(bias_body, geo),
        out_shape=jax.ShapeDtypeStruct((geo.groups, geo.stack * geo.band, geo.slots), F32),
        in_specs=[
            pl.BlockSpec(memory_space=pltpu.SMEM),
            pl.BlockSpec(memory_space=pltpu.VMEM),
        ],
        out_specs=pl.BlockSpec(memory_space=pltpu.VMEM),
        compiler_params=pltpu.CompilerParams(vmem_limit_bytes=ROOM * MIB),
        name="bias_table",
    )(rel_table, jnp.asarray(geo.base[which]))


def qkv_rows(pages, w_ref, vec_ref, o_ref):
    d = pages[0].shape[1]

    def normed(raw):
        unit, _ = norm_parts(unmask(raw.astype(F32), vec_ref[0:1]))
        return (unit * vec_ref[1:2] + vec_ref[2:3]).astype(BF16)

    now = normed(pages[0])
    for k in range(len(pages)):
        rows = dot(now, w_ref[...])
        if k + 1 < len(pages):
            now = normed(pages[k + 1])
        for i in range(3):
            cols = slice(i * d, (i + 1) * d)
            o_ref[k, :, cols] = (rows[:, cols] + vec_ref[9 + i : 10 + i]).astype(BF16)


def qkv_own_body(x_ref, w_ref, vec_ref, o_ref):
    span = x_ref.shape[0]
    qkv_rows([x_ref[k] for k in range(span)], w_ref, vec_ref, o_ref)


def qkv_halo_body(geo, top_ref, bottom_ref, left_ref, right_ref, last_ref, flank_ref, w_ref, vec_ref, o_ref):
    span = top_ref.shape[0]
    raw = [
        geo.around(
            top_ref[k], bottom_ref[k], left_ref[k], right_ref[k], flank_ref[...], last_ref[k]
        )
        for k in range(span)
    ]
    qkv_rows(raw, w_ref, vec_ref, o_ref)


def by_page(a, span=1):
    return pl.BlockSpec((span,) + a.shape[1:], lambda p: (p,) + (0,) * (len(a.shape) - 1))


def qkv_call(body, rows, paged, whole, name):
    pages, _, d = paged[0].shape
    span = 2 if pages % 2 == 0 else 1
    n = pages * rows
    return pl.pallas_call(
        body,
        out_shape=jax.ShapeDtypeStruct((pages, rows, 3 * d), BF16),
        grid=(pages // span,),
        in_specs=[by_page(a, span) for a in paged] + [hold(a.shape) for a in whole],
        out_specs=pl.BlockSpec((span, rows, 3 * d), lambda p: (p, 0, 0)),
        compiler_params=params(ROOM),
        cost_estimate=pl.CostEstimate(
            flops=6 * n * d * d, transcendentals=n, bytes_accessed=2 * (4 * n * d + 3 * d * d)
        ),
        name=name,
    )(*paged, *whole)


def strips_body(geo, x_ref, top_ref, bottom_ref, right_ref, left_ref, tall, near):
    e, o = geo.edge, geo.own
    near[...] = jnp.zeros_like(near)

    def page(p, carry):
        tall[0:e, :] = top_ref[p].astype(F32)
        tall[e : e + o, :] = x_ref[p].astype(F32)
        tall[e + o :, :] = bottom_ref[p].astype(F32)
        for r in range(geo.rows + 2 * REACH):
            to, at = r * REACH, r * geo.cols
            near[0, to : to + REACH, :] = tall[at + geo.cols - REACH : at + geo.cols, :]
            near[1, to : to + REACH, :] = tall[at : at + REACH, :]
        right_ref[p] = near[0].astype(BF16)
        left_ref[p] = near[1].astype(BF16)
        return carry

    lax.fori_loop(0, geo.pages, page, 0)


def strips_call(geo, x, top, bottom):
    width = x.shape[2]
    shape = jax.ShapeDtypeStruct((geo.pages, geo.strip, width), BF16)
    return pl.pallas_call(
        functools.partial(strips_body, geo),
        out_shape=(shape, shape),
        scratch_shapes=[
            pltpu.VMEM((2 * geo.edge + geo.own, width), F32),
            pltpu.VMEM((2, geo.strip, width), F32),
        ],
        compiler_params=pltpu.CompilerParams(vmem_limit_bytes=ROOM * MIB),
        name="strips",
    )(x, top, bottom)


def class_part(geo, own_ref, halo_ref, hr_ref, hrf_ref, o_ref):
    page, d, at = pl.program_id(0), geo.width, geo.halo - 16

    @pl.when(page == 0)
    def _():
        o_ref[...] = jnp.zeros_like(o_ref)

    scale = BF16(1.0 / math.sqrt(geo.head))
    hr, hrf = hr_ref[...], hrf_ref[...]
    qc = jnp.broadcast_to(halo_ref[0, at : at + 1, 0:d] * scale, (16, d)) * hr
    s = dot_t(qc, own_ref[0, :, d : 2 * d])
    top = jnp.max(s, axis=-1, keepdims=True)
    e = jnp.exp(s - top)
    total = jnp.sum(e, axis=-1, keepdims=True)
    acc = dot(jnp.concatenate(split3(e), axis=0), own_ref[0, :, 2 * d : 3 * d])
    acc = acc[0:16] + acc[16:32] + acc[32:48]
    o_ref[pl.ds(page, 1), :] = jnp.sum(acc * hrf, axis=0, keepdims=True)
    row = lax.broadcasted_iota(jnp.int32, (16, LANES), 0)
    diag = row == lax.broadcasted_iota(jnp.int32, (16, LANES), 1)
    stats = [jnp.sum(jnp.where(diag, a, 0.0), axis=0, keepdims=True) for a in (top, total)]
    stats.append(jnp.zeros((1, d - 2 * LANES), F32))
    o_ref[pl.ds(geo.pages + page, 1), :] = jnp.concatenate(stats, axis=1)


def attend_body(
    geo, own_ref, halo_ref, bias_ref, ok_ref, hm_ref, hr_ref, hrf_ref, o_ref, lse_ref, p_ref, c_ref
):
    scale = BF16(1.0 / math.sqrt(geo.head))
    hm = hm_ref[...]
    lane = lax.broadcasted_iota(jnp.int32, (geo.band, LANES), 1)
    bands = range(geo.bands)
    at = [slice(b * geo.band, (b + 1) * geo.band) for b in bands]
    lses = [jnp.zeros((geo.band, LANES), F32) for _ in bands]

    def part(ref, which, g):
        lo = which * geo.width + g * geo.lanes
        return ref[0, :, lo : lo + geo.lanes]

    def score(g):
        q, k, hk = part(own_ref, 0, g), part(own_ref, 1, g), part(halo_ref, 1, g)
        return [
            dot_t(geo.stacked(q[at[b]] * scale, hm), geo.block(k, hk, b))
            + bias_ref[g]
            + ok_ref[b : b + 1]
            for b in bands
        ]

    def soften(g, scores):
        probs = []
        for b in bands:
            top = jnp.max(scores[b], axis=-1, keepdims=True)
            e = jnp.exp(scores[b] - top)
            total = jnp.sum(e, axis=-1, keepdims=True)
            lse = top + jnp.log(total)
            for h in range(geo.stack):
                rows = slice(h * geo.band, (h + 1) * geo.band)
                lses[b] = jnp.where(lane == g * geo.stack + h, lse[rows], lses[b])
            p = (e * (1.0 / total)).astype(BF16)
            p_ref[0, g, b] = p
            probs.append(p)
        return probs

    def mix(g, probs):
        v, hv = part(own_ref, 2, g), part(halo_ref, 2, g)
        for b in bands:
            rows = geo.unstacked(dot(probs[b], geo.block(v, hv, b)))
            o_ref[0, at[b], g * geo.lanes : (g + 1) * geo.lanes] = rows.astype(BF16)

    class_part(geo, own_ref, halo_ref, hr_ref, hrf_ref, c_ref)
    scores = score(0)
    for g in range(geo.groups):
        probs = soften(g, scores)
        if g + 1 < geo.groups:
            scores = score(g + 1)
        mix(g, probs)
    for b in bands:
        lse_ref[0, at[b], :] = lses[b]


def attend_call(geo, own, halo, bias, ok, hm, hr, hrf):
    G = geo.groups
    mm = 2 * geo.pages * G * geo.bands * 256 * 256 * 256
    outs = (
        jax.ShapeDtypeStruct((geo.pages, geo.own, geo.width), BF16),
        jax.ShapeDtypeStruct((geo.pages, geo.own, LANES), F32),
        jax.ShapeDtypeStruct((geo.pages, G, geo.bands, geo.lanes, geo.slots), BF16),
        jax.ShapeDtypeStruct((2 * geo.pages, geo.width), F32),
    )
    return pl.pallas_call(
        functools.partial(attend_body, geo),
        out_shape=outs,
        grid=(geo.pages,),
        in_specs=[by_page(own), by_page(halo)] + [hold(a.shape) for a in (bias, ok, hm, hr, hrf)],
        out_specs=[by_page(a) for a in outs[:3]] + [hold((2 * geo.pages, geo.width))],
        compiler_params=params(ROOM),
        cost_estimate=pl.CostEstimate(
            flops=2 * mm, transcendentals=geo.pages * G * geo.bands * 65536, bytes_accessed=16 * MIB
        ),
        name="attend",
    )(own, halo, bias, ok, hm, hr, hrf)


def mlp_body(
    tile, steps, att_ref, x_ref, og_ref, lse_ref, wout_ref, vec_ref, toh_ref, wup_ref, wdn_ref,
    out_ref, gmx_ref, gres_ref, gb_ref, dw_ref, vg_ref, dub_ref,
    n2, n2t, gm, res, branch, mlp, gn, act, dh, up_buf, dn_buf, out_buf, gmx_buf, gres_buf, gb_buf,
    sems, out_sems,
):
    step = pl.program_id(0)
    n, d = n2.shape
    row = lambda i: vec_ref[i : i + 1]
    tiles, few, rows_dn = n // tile, dn_buf.shape[0], dn_buf.shape[1]
    rows_up = up_buf.shape[1]
    span = lambda t: pl.ds(pl.multiple_of(t * tile, tile), tile)

    @pl.when(step == 0)
    def _():
        def one(t, carry):
            rows = span(t)
            x = unmask(x_ref[rows, :].astype(F32), row(0))
            br = dot(att_ref[rows, :], wout_ref[...]) + row(3)
            r = x + row(4) * br
            branch[rows, :] = br
            res[rows, :] = r
            unit, _ = norm_parts(r)
            n2[rows, :] = (unit * row(5) + row(6)).astype(BF16)
            gm[rows, :] = (row(8) * og_ref[rows, :].astype(F32)).astype(BF16)
            mlp[rows, :] = jnp.zeros((tile, d), F32)
            gn[rows, :] = jnp.zeros((tile, d), F32)
            return carry

        lax.fori_loop(0, tiles, one, 0)
        n2t[...] = n2[...].T
        vg_ref[...] = jnp.zeros_like(vg_ref)

    wup, wdn = wup_ref[...], wdn_ref[...]
    upb = vec_ref[pl.ds(12 + step, 1), :]
    dub_ref[...] = jnp.zeros_like(dub_ref)

    def one(t, carry):
        rows = pl.ds(pl.multiple_of(t * 2 * tile, 2 * tile), 2 * tile)
        h = dot(n2[rows, :], wup) + upb
        da = dot_t(gm[rows, :], wdn)
        cdf = 0.5 * (1.0 + lax.erf(h * math.sqrt(0.5)))
        pdf = jnp.exp(-0.5 * h * h) * (1.0 / math.sqrt(2.0 * math.pi))
        a = (h * cdf).astype(BF16)
        g = (da * (cdf + h * pdf)).astype(BF16)
        act[rows, :] = a
        dh[rows, :] = g
        mlp[rows, :] += dot(a, wdn)
        gn[rows, :] += dot_t(g, wup)
        dub_ref[0:1] += jnp.sum(g.astype(F32), axis=0, keepdims=True)
        return carry

    lax.fori_loop(0, tiles // 2, one, 0)

    def copies(c):
        at = pl.multiple_of(c * rows_up, 8)
        return (
            pltpu.make_async_copy(up_buf, dw_ref.at[:, pl.ds(at, rows_up), :], sems.at[0]),
            pltpu.make_async_copy(
                dn_buf,
                dw_ref.at[pl.ds(c * few, few), steps * rows_up : steps * rows_up + rows_dn, :],
                sems.at[1],
            ),
        )

    @pl.when(step > 0)
    def _():
        for copy in copies(step - 1):
            copy.wait()

    up_buf[...] = dot(n2t[...], dh[...]).astype(BF16).reshape(up_buf.shape)
    dn_buf[...] = dot_0(act[...], gm[...]).astype(BF16).reshape(dn_buf.shape)
    for copy in copies(step):
        copy.start()

    @pl.when(step == steps - 1)
    def _():
        outs = ((out_buf, out_ref), (gmx_buf, gmx_ref), (gres_buf, gres_ref), (gb_buf, gb_ref))

        def sends(t, slot):
            return [
                pltpu.make_async_copy(buf.at[slot], ref.at[span(t), :], out_sems.at[slot, i])
                for i, (buf, ref) in enumerate(outs)
            ]

        def add(i, v):
            vg_ref[i : i + 1] += jnp.sum(v, axis=0, keepdims=True)

        def one(t, carry):
            rows, slot = span(t), lax.rem(t, 2)

            @pl.when(t >= 2)
            def _():
                for copy in sends(t - 2, slot):
                    copy.wait()

            r, br, att = res[rows, :], branch[rows, :], att_ref[rows, :]
            og = og_ref[rows, :].astype(F32)
            mo = mlp[rows, :] + row(7)
            out_buf[slot] = (r + row(8) * mo).astype(BF16)
            add(0, og * mo)
            add(1, gm[rows, :].astype(F32))
            unit, inv = norm_parts(r)
            grad = gn[rows, :]
            add(2, grad * unit)
            add(3, grad)
            gr = og + norm_pull(grad * row(5), unit, inv)
            gres_buf[slot] = gr
            add(4, gr * br)
            gb = (row(4) * gr).astype(BF16)
            add(5, gb.astype(F32))
            gb_buf[slot] = gb
            mix = dot_t(gb, wout_ref[...]).astype(BF16)
            prod = mix.astype(F32) * att.astype(F32)
            delta = sum(dot(part, toh_ref[...]) for part in split3(prod))
            packed = jnp.zeros(delta.shape, F32)
            for i, part in enumerate(split3(lse_ref[rows, :]) + split3(delta)):
                part = part.astype(F32)
                packed += part if i == 0 else pltpu.roll(part, 16 * i, 1)
            gmx_buf[slot, :, 0:d] = mix
            gmx_buf[slot, :, d : d + LANES] = packed.astype(BF16)
            for copy in sends(t, slot):
                copy.start()
            return carry

        lax.fori_loop(0, tiles, one, 0)
        for t in (tiles - 2, tiles - 1):
            for copy in sends(t, t % 2):
                copy.wait()
        for copy in copies(step):
            copy.wait()


def mlp_call(att, x, og, lse, w_out, vec, to_head, w_up, w_down, dests, tile=256):
    n, d = x.shape
    ff = w_up.shape[1]
    steps = ff // d
    rows_up, rows_dn = d // dests, ff // dests
    anywhere = pl.BlockSpec(memory_space=pl.ANY)
    return pl.pallas_call(
        functools.partial(mlp_body, tile, steps),
        out_shape=(
            jax.ShapeDtypeStruct((n, d), BF16),
            jax.ShapeDtypeStruct((n, d + LANES), BF16),
            jax.ShapeDtypeStruct((n, d), F32),
            jax.ShapeDtypeStruct((n, d), BF16),
            jax.ShapeDtypeStruct((dests, steps * rows_up + rows_dn, d), BF16),
            jax.ShapeDtypeStruct((8, d), F32),
            jax.ShapeDtypeStruct((8, ff), F32),
        ),
        grid=(steps,),
        in_specs=[hold(a.shape) for a in (att, x, og, lse, w_out, vec, to_head)]
        + [pl.BlockSpec((d, d), lambda c: (0, c)), pl.BlockSpec((d, d), lambda c: (c, 0))],
        out_specs=[anywhere] * 5 + [hold((8, d)), pl.BlockSpec((8, d), lambda c: (0, c))],
        scratch_shapes=[
            pltpu.VMEM((n, d), BF16),
            pltpu.VMEM((d, n), BF16),
            pltpu.VMEM((n, d), BF16),
            pltpu.VMEM((n, d), F32),
            pltpu.VMEM((n, d), F32),
            pltpu.VMEM((n, d), F32),
            pltpu.VMEM((n, d), F32),
            pltpu.VMEM((n, d), BF16),
            pltpu.VMEM((n, d), BF16),
            pltpu.VMEM((dests, rows_up, d), BF16),
            pltpu.VMEM((dests // steps, rows_dn, d), BF16),
            pltpu.VMEM((2, tile, d), BF16),
            pltpu.VMEM((2, tile, d + LANES), BF16),
            pltpu.VMEM((2, tile, d), F32),
            pltpu.VMEM((2, tile, d), BF16),
            pltpu.SemaphoreType.DMA((2,)),
            pltpu.SemaphoreType.DMA((2, 4)),
        ],
        compiler_params=params(ROOM),
        cost_estimate=pl.CostEstimate(
            flops=2 * n * d * (6 * ff + 2 * d),
            transcendentals=2 * n * ff,
            bytes_accessed=2 * (4 * d * ff + 8 * n * d),
        ),
        name="mlp",
    )(att, x, og, lse, w_out, vec, to_head, w_up, w_down)


def table_sums(geo, acc_ref, fold_ref, o_ref):
    lane = lax.broadcasted_iota(jnp.int32, (geo.cols, geo.slots), 1)
    heads = []
    for g in range(geo.groups):
        for h in range(geo.stack):
            x = acc_ref[g, h * geo.band : (h + 1) * geo.band, :]
            parts = [x[i * geo.cols : (i + 1) * geo.cols] for i in range(BAND)]
            main, side, plain = parts[0], parts[0], parts[0]
            for i in range(1, BAND):
                main = main + pltpu.roll(parts[i], geo.slots - i * geo.cols, 1)
                side = side + pltpu.roll(parts[i], geo.slots - i * SIDE, 1)
                plain = plain + parts[i]
            z = jnp.where(lane < SPAN * geo.cols, main, jnp.where(lane < geo.cls_at, side, plain))
            heads.append(z)
    pad = [jnp.zeros((geo.cols, geo.slots), F32)] * (16 - geo.heads)
    z = jnp.stack(heads + pad, axis=0)
    total = jnp.zeros((16, LANES), F32)
    which = lax.broadcasted_iota(jnp.int32, (geo.slots, LANES), 1)
    for i in range(geo.cols):
        pick = jnp.where(fold_ref[:, i : i + 1] == which, 1.0, 0.0).astype(BF16)
        for part in split3(z[:, i, :]):
            total += dot(part, pick)
    o_ref[...] = total


def query_grad_body(
    geo, p_ref, own_ref, halo_ref, gm_ref, hm_ref, sm_ref, fold_ref, dq_ref, table_ref, rel_ref
):
    scale = 1.0 / math.sqrt(geo.head)
    hm = hm_ref[...]
    bands = range(geo.bands)
    at = [slice(b * geo.band, (b + 1) * geo.band) for b in bands]
    ones = jnp.ones((geo.slots, LANES), BF16)
    join = lambda a, b: jnp.concatenate([a, b], axis=1)
    st = gm_ref[0, :, geo.width :]

    @pl.when(pl.program_id(0) == 0)
    def _():
        rel_ref[...] = jnp.zeros_like(rel_ref)

    def part(ref, which, g):
        lo = which * geo.width + g * geo.lanes
        return ref[0, :, lo : lo + geo.lanes]

    def pull(g):
        gm, v, hv = part(gm_ref, 0, g), part(own_ref, 2, g), part(halo_ref, 2, g)
        sm = sm_ref[g]
        return [
            dot_t(
                join(geo.stacked(gm[at[b]], hm), geo.stacked(st[at[b]], sm)),
                join(geo.block(v, hv, b), ones),
            )
            for b in bands
        ]

    dp = pull(0)
    for g in range(geo.groups):
        ds = [p_ref[0, g, b].astype(F32) * dp[b] for b in bands]
        if g + 1 < geo.groups:
            dp = pull(g + 1)
        total = ds[0]
        for d in ds[1:]:
            total = total + d
        rel_ref[g] += total
        k, hk = part(own_ref, 1, g), part(halo_ref, 1, g)
        for b in bands:
            rows = geo.unstacked(dot((ds[b] * scale).astype(BF16), geo.block(k, hk, b)))
            dq_ref[0, at[b], g * geo.lanes : (g + 1) * geo.lanes] = rows.astype(BF16)

    @pl.when(pl.program_id(0) == geo.pages - 1)
    def _():
        table_sums(geo, rel_ref, fold_ref, table_ref)


def query_grad_call(geo, probs, own, halo, gmx, hm, sm):
    G = geo.groups
    mm = 2 * geo.pages * G * geo.bands * 256 * 256 * 256
    dq = jax.ShapeDtypeStruct((geo.pages, geo.own, geo.width), BF16)
    table = jax.ShapeDtypeStruct((16, LANES), F32)
    fold = jnp.asarray(geo.fold)
    return pl.pallas_call(
        functools.partial(query_grad_body, geo),
        out_shape=(dq, table),
        grid=(geo.pages,),
        in_specs=[by_page(a) for a in (probs, own, halo, gmx)]
        + [hold(a.shape) for a in (hm, sm, fold)],
        out_specs=[by_page(dq), hold(table.shape)],
        scratch_shapes=[pltpu.VMEM((geo.groups, geo.stack * geo.band, geo.slots), F32)],
        compiler_params=params(ROOM),
        cost_estimate=pl.CostEstimate(
            flops=2 * mm, transcendentals=0, bytes_accessed=20 * MIB
        ),
        name="query_grad",
    )(probs, own, halo, gmx, hm, sm, fold)


def class_grad(geo, own_ref, halo_ref, gm_ref, hr_ref, hrf_ref, sa_ref, cb_ref, o_ref, acc):
    page, d, at = pl.program_id(0), geo.width, geo.halo - 16

    @pl.when(page == 0)
    def _():
        acc[...] = jnp.zeros_like(acc)

    scale = 1.0 / math.sqrt(geo.head)
    hr, hrf, sa = hr_ref[...], hrf_ref[...], sa_ref[...]
    q, gm, st = own_ref[0, :, 0:d], gm_ref[0, :, 0:d], gm_ref[0, :, d:]
    kc = jnp.broadcast_to(halo_ref[0, at : at + 1, d : 2 * d] * BF16(scale), (16, d)) * hr
    vc = jnp.broadcast_to(halo_ref[0, at : at + 1, 2 * d : 3 * d], (16, d)) * hr
    prob = jnp.exp(dot_t(kc, q) + dot_t(sa[0:16], st) + cb_ref[...])
    ds = prob * (dot_t(vc, gm) + dot_t(sa[16:32], st))
    row = pl.ds(page, 1)
    dk = dot((ds * scale).astype(BF16), q)
    dv = dot(prob.astype(BF16), gm)
    acc[row, 0:d] = jnp.sum(dk * hrf, axis=0, keepdims=True)
    acc[row, d : 2 * d] = jnp.sum(dv * hrf, axis=0, keepdims=True)

    @pl.when(page == geo.pages - 1)
    def _():
        o_ref[...] = acc[...].astype(BF16)


def key_grad_body(
    geo, own_ref, halo_ref, gm_ref, top_ref, bottom_ref, left_ref, right_ref,
    bias_ref, ok_ref, hm_ref, sa_ref, flank_ref, hr_ref, hrf_ref, cb_ref, dk_ref, dv_ref, c_ref,
    hgm, rowstat, acc,
):
    scale = 1.0 / math.sqrt(geo.head)
    hm = hm_ref[...]
    bands = range(geo.bands)
    at = [slice(b * geo.band, (b + 1) * geo.band) for b in bands]
    last = jnp.zeros((16, gm_ref.shape[2]), BF16)
    hgm[...] = geo.around(
        top_ref[0], bottom_ref[0], left_ref[0], right_ref[0], flank_ref[...], last
    )
    stats, own = hgm[:, geo.width :], gm_ref[0, :, geo.width :]
    row = lax.broadcasted_iota(jnp.int32, (32, geo.slots), 0)
    for b in bands:
        r = dot_t(sa_ref[...], geo.block(own, stats, b))
        rowstat[b] = r + jnp.where(row < 16, ok_ref[b : b + 1], 0.0)

    def part(ref, which, g):
        lo = which * geo.width + g * geo.lanes
        return ref[0, :, lo : lo + geo.lanes]

    def spread(g, b, first):
        at = first + g * geo.stack
        return jnp.concatenate(
            [
                jnp.broadcast_to(rowstat[b, at + h : at + h + 1, :], (geo.band, geo.slots))
                for h in range(geo.stack)
            ],
            axis=0,
        )

    def first(g):
        q, k, v = (part(own_ref, i, g) for i in range(3))
        hq, gm = part(halo_ref, 0, g), part(gm_ref, 0, g)
        hg = hgm[:, g * geo.lanes : (g + 1) * geo.lanes]
        qb = [geo.block(q, hq, b) for b in bands]
        gb = [geo.block(gm, hg, b) for b in bands]
        s = [dot_t(geo.stacked(k[at[b]] * BF16(scale), hm), qb[b]) for b in bands]
        dp = [dot_t(geo.stacked(v[at[b]], hm), gb[b]) for b in bands]
        return qb, gb, s, dp

    class_grad(geo, own_ref, halo_ref, gm_ref, hr_ref, hrf_ref, sa_ref, cb_ref, c_ref, acc)
    now = first(0)
    for g in range(geo.groups):
        qb, gb, s, dp = now
        p = [jnp.exp(s[b] + bias_ref[g] + spread(g, b, 0)) for b in bands]
        ds = [(p[b] * (dp[b] + spread(g, b, 16)) * scale).astype(BF16) for b in bands]
        if g + 1 < geo.groups:
            now = first(g + 1)
        lanes = slice(g * geo.lanes, (g + 1) * geo.lanes)
        for b in bands:
            dv_ref[0, at[b], lanes] = geo.unstacked(dot(p[b].astype(BF16), gb[b])).astype(BF16)
            dk_ref[0, at[b], lanes] = geo.unstacked(dot(ds[b], qb[b])).astype(BF16)


def key_grad_call(geo, own, halo, gmx, pieces, *whole):
    G = geo.groups
    mm = 2 * geo.pages * G * geo.bands * 256 * 256 * 256
    out = jax.ShapeDtypeStruct((geo.pages, geo.own, geo.width), BF16)
    return pl.pallas_call(
        functools.partial(key_grad_body, geo),
        out_shape=(out, out, jax.ShapeDtypeStruct((16, 2 * geo.width), BF16)),
        grid=(geo.pages,),
        in_specs=[by_page(a) for a in (own, halo, gmx) + pieces]
        + [hold(a.shape) for a in whole],
        out_specs=[by_page(out)] * 2 + [hold((16, 2 * geo.width))],
        scratch_shapes=[
            pltpu.VMEM((geo.halo, geo.width + LANES), BF16),
            pltpu.VMEM((geo.bands, 32, geo.slots), F32),
            pltpu.VMEM((16, 2 * geo.width), F32),
        ],
        compiler_params=params(ROOM),
        cost_estimate=pl.CostEstimate(
            flops=4 * mm, transcendentals=geo.pages * G * geo.bands * 65536, bytes_accessed=20 * MIB
        ),
        name="key_grad",
    )(own, halo, gmx, *pieces, *whole)


def class_close_body(
    geo, mine_ref, parts_ref, cls_ref, x_ref, toh_ref, wout_ref, vec_ref, wup_ref, wdn_ref,
    out_ref, res, n2, acc,
):
    step = pl.program_id(0)
    d, pages = geo.width, geo.pages
    row = lambda i: vec_ref[i : i + 1]
    places = parts_ref.shape[0]

    @pl.when(step == 0)
    def _():
        mine = mine_ref[0]
        q = jnp.concatenate([cls_ref[p, 0:1, 0:d] for p in range(pages)], axis=0).astype(F32)
        k = jnp.concatenate([cls_ref[p, 0:1, d : 2 * d] for p in range(pages)], axis=0).astype(F32)
        v = jnp.concatenate([cls_ref[p, 0:1, 2 * d :] for p in range(pages)], axis=0).astype(F32)
        toh = toh_ref[...]
        own = sum(dot(part, toh) for part in split3(q * k)) * (1.0 / math.sqrt(geo.head))
        tops = [parts_ref[code ^ mine, pages:, 0:LANES] for code in range(places)]
        top = own
        for value in tops:
            top = jnp.maximum(top, value)
        weights = [jnp.exp(value - top) for value in tops] + [jnp.exp(own - top)]
        total = weights[-1]
        for code in range(places):
            total = total + weights[code] * parts_ref[code ^ mine, pages:, LANES : 2 * LANES]
        spread = jnp.concatenate([w / total for w in weights], axis=0)
        spread = sum(dot_t(part, toh) for part in split3(spread))
        mixed = spread[places * pages :] * v
        for code in range(places):
            rows = spread[code * pages : (code + 1) * pages]
            mixed = mixed + rows * parts_ref[code ^ mine, 0:pages, :]
        mixed = mixed.astype(BF16)
        mixed = jnp.concatenate([mixed, jnp.zeros((16 - pages, d), BF16)], axis=0)
        r = x_ref[...].astype(F32) + row(4) * (dot(mixed, wout_ref[...]) + row(3))
        res[...] = r
        unit, _ = norm_parts(r)
        n2[...] = (unit * row(5) + row(6)).astype(BF16)
        acc[...] = jnp.zeros_like(acc)

    h = dot(n2[...], wup_ref[...]) + vec_ref[pl.ds(12 + step, 1), :]
    a = (h * 0.5 * (1.0 + lax.erf(h * math.sqrt(0.5)))).astype(BF16)
    acc[...] += dot(a, wdn_ref[...])

    @pl.when(step == pl.num_programs(0) - 1)
    def _():
        out_ref[...] = (res[...] + row(8) * (acc[...] + row(7))).astype(BF16)


def class_close_call(geo, mine, parts, halo, x, to_head, w_out, vec, w_up, w_down):
    d = geo.width
    ff = w_up.shape[1]
    return pl.pallas_call(
        functools.partial(class_close_body, geo),
        out_shape=jax.ShapeDtypeStruct((16, d), BF16),
        grid=(ff // d,),
        in_specs=[pl.BlockSpec(memory_space=pltpu.SMEM)]
        + [
            full(parts.shape),
            pl.BlockSpec((geo.pages, 16, 3 * d), lambda c: (0, geo.halo // 16 - 1, 0)),
        ]
        + [full(a.shape) for a in (x, to_head, w_out, vec)]
        + [
            pl.BlockSpec((d, d), lambda c: (0, c)),
            pl.BlockSpec((d, d), lambda c: (c, 0)),
        ],
        out_specs=full((16, d)),
        scratch_shapes=[
            pltpu.VMEM((16, d), F32),
            pltpu.VMEM((16, d), BF16),
            pltpu.VMEM((16, d), F32),
        ],
        compiler_params=params(ROOM),
        cost_estimate=pl.CostEstimate(
            flops=64 * d * (2 * ff + d), transcendentals=16 * ff, bytes_accessed=12 * MIB
        ),
        name="class_close",
    )(mine, parts, halo, x, to_head, w_out, vec, w_up, w_down)


def by_place(dw, cols, core, half, column, keep_ref, send_ref):
    slab = dw.shape[0] // (4 * cols)
    for mine in range(2):

        @pl.when(core == mine)
        def _():
            for dest in range(4 * cols):
                y, b, c = dest // (2 * cols), dest // cols % 2, dest % cols
                place = (y ^ half) * cols + (c ^ column)
                ref = keep_ref if b == mine else send_ref
                ref[place] = dw[dest * slab : (dest + 1) * slab]


def early_weight_body(
    tile, cols, at_ref, x_ref, att_ref, dq_ref, gb_ref, vec_ref, keep_ref, send_ref, nt_ref, sum_ref,
    left, grad,
):
    step = pl.program_id(0)
    n, d = x_ref.shape

    @pl.when(step == 0)
    def _():
        def one(t, carry):
            rows = pl.ds(pl.multiple_of(t * tile, tile), tile)
            unit, _ = norm_parts(unmask(x_ref[rows, :].astype(F32), vec_ref[0:1]))
            grad[rows, :] = (unit * vec_ref[1:2] + vec_ref[2:3]).astype(BF16)
            return carry

        lax.fori_loop(0, n // tile, one, 0)
        left[...] = grad[...].T
        nt_ref[...] = left[...]
        grad[...] = dq_ref[...]
        total = jnp.sum(dq_ref[...].astype(F32), axis=0, keepdims=True)
        sum_ref[...] = jnp.broadcast_to(total, sum_ref.shape)

    @pl.when(step == 1)
    def _():
        left[...] = att_ref[...].T
        grad[...] = gb_ref[...]

    dw = dot(left[...], grad[...]).astype(BF16)
    by_place(dw, cols, at_ref[0], at_ref[1], at_ref[2], keep_ref, send_ref)


def late_weight_body(
    cols, at_ref, nt_ref, dk_ref, dv_ref, c_ref, cg_ref, vec_ref, keep_ref, send_ref, sum_ref, grad
):
    step = pl.program_id(0)
    extra = cg_ref[...]

    @pl.when(step == 0)
    def _():
        grad[...] = dk_ref[...]

    @pl.when(step == 1)
    def _():
        grad[...] = dv_ref[...]
        total = jnp.sum(dv_ref[...].astype(F32), axis=0, keepdims=True)
        total = total + jnp.sum(extra.astype(F32), axis=0, keepdims=True)
        sum_ref[...] = jnp.broadcast_to(total, sum_ref.shape)

    unit, _ = norm_parts(c_ref[...].astype(F32))
    left = (unit * vec_ref[1:2] + vec_ref[2:3]).astype(BF16)
    dw = (dot(nt_ref[...], grad[...]) + dot_0(left, extra)).astype(BF16)
    by_place(dw, cols, at_ref[0], at_ref[1], at_ref[2], keep_ref, send_ref)


def weight_call(body, where, cols, ins, in_specs, n, d, more, more_specs, scratch, name):
    slab = d // (4 * cols)
    out = jax.ShapeDtypeStruct((2 * cols, slab, 2 * d), BF16)
    block = pl.BlockSpec((2 * cols, slab, d), lambda i, p: (0, 0, i))
    return pl.pallas_call(
        body,
        out_shape=(out, out) + more,
        grid_spec=pltpu.PrefetchScalarGridSpec(
            num_scalar_prefetch=1,
            grid=(2,),
            in_specs=in_specs,
            out_specs=[block, block] + more_specs,
            scratch_shapes=scratch,
        ),
        compiler_params=params(ROOM),
        cost_estimate=pl.CostEstimate(
            flops=4 * n * d * d, transcendentals=n, bytes_accessed=2 * (5 * n * d + 2 * d * d)
        ),
        name=name,
    )(where, *ins)


def early_weight_call(where, cols, x, att, dq, gb, vec, tile=256):
    n, d = x.shape
    return weight_call(
        functools.partial(early_weight_body, tile, cols), where, cols, (x, att, dq, gb, vec),
        [hold(a.shape) for a in (x, att, dq, gb, vec)], n, d,
        (jax.ShapeDtypeStruct((d, n), BF16), jax.ShapeDtypeStruct((8, d), F32)),
        [hold((d, n)), hold((8, d))],
        [pltpu.VMEM((d, n), BF16), pltpu.VMEM((n, d), BF16)],
        "early_weight",
    )


def late_weight_call(where, cols, nt, dk, dv, cls_rows, cls_grad, vec):
    n, d = dk.shape
    ins = (nt, dk, dv, cls_rows)
    return weight_call(
        functools.partial(late_weight_body, cols), where, cols, ins + (cls_grad, vec),
        [hold(a.shape) for a in ins]
        + [pl.BlockSpec((16, d), lambda i, p: (0, i)), hold(vec.shape)],
        n, d, (jax.ShapeDtypeStruct((8, d), F32),), [hold((8, d))],
        [pltpu.VMEM((n, d), BF16)],
        "late_weight",
    )


def fold_body(cols, at_ref, k1_ref, r1_ref, k2_ref, r2_ref, own_ref, x_ref, y_ref, far_ref):
    d = k1_ref.shape[2] // 2
    add = lambda a, b, lo, hi: (a[:, :, lo:hi].astype(F32) + b[:, :, lo:hi].astype(F32)).astype(BF16)
    one = lambda lo, hi: add(k1_ref, r1_ref, lo, hi)
    two = lambda lo, hi: add(k2_ref, r2_ref, lo, hi)
    h = d // 2
    for page in range(2):

        @pl.when(at_ref[3] == page)
        def _():
            for near, far, half in ((own_ref, y_ref, page), (x_ref, far_ref, 1 - page)):
                if half == 0:
                    parts = ((one(0, d), 0), (two(0, h), d), (one(d, d + h), d + h))
                else:
                    parts = ((two(h, 2 * d), 0), (one(d + h, 2 * d), d + h))
                for value, lo in parts:
                    hi = lo + value.shape[2]
                    near[:, :, lo:hi] = value[:cols]
                    far[:, :, lo:hi] = value[cols:]


def fold_call(where, cols, keep1, got1, keep2, got2):
    _, slab, d2 = keep1.shape
    out = jax.ShapeDtypeStruct((cols, slab, d2), BF16)
    rows = slab // 3
    spec = lambda k: pl.BlockSpec((k, rows, d2), lambda i, p: (0, i, 0))
    return pl.pallas_call(
        functools.partial(fold_body, cols),
        out_shape=(out,) * 4,
        grid_spec=pltpu.PrefetchScalarGridSpec(
            num_scalar_prefetch=1,
            grid=(3,),
            in_specs=[spec(2 * cols)] * 4,
            out_specs=[spec(cols)] * 4,
        ),
        compiler_params=params(LESS),
        name="fold",
    )(where, keep1, got1, keep2, got2)


def token_grad_body(
    pages, heads, x_ref, dq_ref, dk_ref, dv_ref, gres_ref, w_ref, c_ref, cg_ref, vec_ref, part_ref,
    mlp_ref, up_ref, table_ref, sq_ref, sv_ref, dt_ref, o_ref,
):
    d = x_ref.shape[1]
    wq, wk, wv = w_ref[:, 0:d], w_ref[:, d : 2 * d], w_ref[:, 2 * d : 3 * d]
    gain = vec_ref[1:2]
    lead = 2 * pages
    at = lead + pages

    @pl.when(pl.program_id(0) == 0)
    def _():
        o_ref[...] = jnp.zeros_like(o_ref)
        unit, inv = norm_parts(c_ref[...].astype(F32))
        gn = dot_t(cg_ref[:, 0:d], wk) + dot_t(cg_ref[:, d : 2 * d], wv)
        o_ref[0:lead] = part_ref[...]
        o_ref[lead:at] = norm_pull(gn * gain, unit, inv)[0:pages]
        o_ref[at + 1 : at + 2] = jnp.sum(gn * unit, axis=0, keepdims=True)
        o_ref[at + 2 : at + 3] = jnp.sum(gn, axis=0, keepdims=True)
        o_ref[at + 3 : at + 4] = sq_ref[0:1]
        o_ref[at + 4 : at + 5] = sv_ref[0:1]
        o_ref[at + 5 : at + 11] = mlp_ref[0:6]
        ups = up_ref.shape[1] // d
        for i in range(ups):
            o_ref[at + 11 + i : at + 12 + i] = up_ref[0:1, i * d : (i + 1) * d]
        for h in range(heads):
            r, c = divmod(h * LANES, d)
            o_ref[at + 11 + ups + r : at + 12 + ups + r, c : c + LANES] = table_ref[h : h + 1]

    raw = x_ref[...].astype(F32)
    masked = raw > FLAG / 2
    unit, inv = norm_parts(jnp.where(masked, vec_ref[0:1], raw))
    gn = dot_t(dq_ref[...], wq) + dot_t(dk_ref[...], wk) + dot_t(dv_ref[...], wv)
    gs = gres_ref[...] + norm_pull(gn * gain, unit, inv)
    dt_ref[...] = jnp.where(masked, 0.0, gs)
    o_ref[at : at + 1] += jnp.sum(jnp.where(masked, gs, 0.0), axis=0, keepdims=True)
    o_ref[at + 1 : at + 2] += jnp.sum(gn * unit, axis=0, keepdims=True)
    o_ref[at + 2 : at + 3] += jnp.sum(gn, axis=0, keepdims=True)


def token_grad_call(pages, heads, rows_in, whole, tile=256):
    n, d = rows_in[0].shape
    up = whole[6]
    count = 3 * pages + 11 + up.shape[1] // d - (-heads * LANES // d)
    height = -(-count // 8) * 8
    rows = pl.BlockSpec((tile, d), lambda i: (i, 0))
    return pl.pallas_call(
        functools.partial(token_grad_body, pages, heads),
        out_shape=(jax.ShapeDtypeStruct((n, d), F32), jax.ShapeDtypeStruct((height, d), F32)),
        grid=(n // tile,),
        in_specs=[rows] * 5 + [hold(a.shape) for a in whole],
        out_specs=[rows, hold((height, d))],
        compiler_params=params(ROOM),
        cost_estimate=pl.CostEstimate(
            flops=2 * n * d * 3 * d, transcendentals=n, bytes_accessed=2 * (8 * n * d + 3 * d * d)
        ),
        name="token_grad",
    )(*rows_in, *whole)


def passed_along(value, axis, steps):
    count = lax.axis_size(axis)
    first, last = max(0, -steps), min(count, count - steps)
    return lax.ppermute(value, axis, [(i, i + steps) for i in range(first, last)])


def swap(value, axis, bit):
    return lax.ppermute(value, axis, [(i, i ^ bit) for i in range(lax.axis_size(axis))])


def halo_pieces(geo, x):
    top = passed_along(x[:, geo.own - geo.edge :], "row", 1)
    bottom = passed_along(x[:, : geo.edge], "row", -1)
    to_right, to_left = strips_call(geo, x, top, bottom)
    return top, bottom, passed_along(to_right, "col", 1), passed_along(to_left, "col", -1)


def page_sum(part, by):
    return lax.psum_scatter(part, "dp", scatter_dimension=by, tiled=True)


def spread_sum(grad):
    part = lax.psum_scatter(grad, ("row", "col"), scatter_dimension=0, tiled=True)
    return page_sum(part, 1).astype(F32)


def join(values):
    return lax.optimization_barrier(values)


def shards(
    tokens, cls_token, patch_mask, loss_mask, mask_emb, ln1_gain, ln1_bias, w_qkv, q_bias, v_bias,
    rel_table, w_out, out_bias, scale_attn, ln2_gain, ln2_bias, w_up, up_bias, w_down, down_bias,
    scale_mlp, out_grad,
):
    pages, rows, cols, width = tokens.shape
    heads = rel_table.shape[0]
    geo = Geometry(pages, rows, cols, width, heads)
    count = pages * rows * cols
    row_peers, col_peers = lax.axis_size("row"), lax.axis_size("col")
    grid_rows, grid_cols = rows * row_peers, cols * col_peers
    row_at, col_at, page_at = (lax.axis_index(a) for a in ("row", "col", "dp"))

    ups = w_up.shape[1] // width
    vec = jnp.concatenate(
        [
            mask_emb, ln1_gain, ln1_bias, out_bias, scale_attn, ln2_gain, ln2_bias, down_bias,
            scale_mlp, q_bias, jnp.zeros((width,), F32), v_bias, up_bias,
        ]
    ).reshape(12 + ups, width)
    hm = jnp.asarray(geo.head_mask, BF16)
    hr, hrf = jnp.asarray(geo.head_rows, BF16), jnp.asarray(geo.head_rows, F32)
    sm, sa = jnp.asarray(geo.stat_mask, BF16), jnp.asarray(geo.stat_all, BF16)
    to_head, flank = jnp.asarray(geo.to_head, BF16), jnp.asarray(geo.flank_of, BF16)

    at_row = row_at * rows + BAND * np.arange(8)[:, None] - REACH + geo.slot_row[None, :]
    at_col = col_at * cols + geo.slot_col[None, :]
    inside = (at_row >= 0) & (at_row < grid_rows) & (at_col >= 0) & (at_col < grid_cols)
    inside = inside | (np.arange(geo.slots) >= geo.cls_at)[None, :]
    ok = jnp.where(inside, 0.0, NEG).astype(F32)

    masked = (patch_mask == 1)[..., None]
    x = jnp.where(masked, jnp.asarray(FLAG, BF16), tokens).reshape(pages, geo.own, width)
    pieces = halo_pieces(geo, x)
    bias_a = bias_table(geo, rel_table, 0)
    own = qkv_call(qkv_own_body, geo.own, (x,), (w_qkv, vec), "qkv_own")
    first = np.arange(16)[:, None] == 0
    cls_block = jnp.where(first, cls_token[:, None, :], jnp.zeros((), BF16))
    halo = qkv_call(
        functools.partial(qkv_halo_body, geo), geo.halo, pieces + (cls_block,),
        (flank, w_qkv, vec), "qkv_halo",
    )
    att, lse, probs, cls_part = attend_call(geo, own, halo, bias_a, ok, hm, hr, hrf)
    att, lse, x = att.reshape(count, width), lse.reshape(count, LANES), x.reshape(count, width)
    counted = (patch_mask * loss_mask == 1)[..., None]
    out_g = jnp.where(counted, out_grad, jnp.zeros((), BF16)).reshape(count, width)
    out, gmx, gres, gb, d_mlp, vg_mlp, d_upb = mlp_call(
        att, x, out_g, lse, w_out, vec, to_head, w_up, w_down, row_peers * col_peers
    )
    d_mlp = lax.psum_scatter(d_mlp, ("row", "col"), scatter_dimension=0, tiled=True)[0]
    gmx = gmx.reshape(pages, geo.own, width + LANES)
    pieces = halo_pieces(geo, gmx)
    bias_b = bias_table(geo, rel_table, 1)
    dq, d_table = query_grad_call(geo, probs, own, halo, gmx, hm, sm)
    class_bias = jnp.concatenate([rel_table[:, SPAN * SPAN], jnp.zeros((16 - heads,), F32)])
    class_bias = jnp.broadcast_to(class_bias[:, None], (16, geo.own))
    cls_rows = jnp.concatenate([cls_token, jnp.zeros((16 - pages, width), BF16)], axis=0)
    direct = (lax.axis_size("dp"), row_peers, col_peers) == (2, 4, 4)
    if direct:
        where = jnp.stack([row_at % 2, row_at // 2, col_at, page_at]).astype(jnp.int32)
    else:
        where = jnp.zeros((4,), jnp.int32)
    dq = dq.reshape(count, width)
    keep1, send1, nt, sum_q = early_weight_call(where, col_peers, x, att, dq, gb, vec)
    pieces, bias_b, nt = join((pieces, bias_b, nt))
    if direct:
        got1 = swap(send1, "row", 1)
    dk, dv, cls_low = key_grad_call(
        geo, own, halo, gmx, pieces, bias_b, ok, hm, sa, flank, hr, hrf, class_bias
    )
    dk, dv = dk.reshape(count, width), dv.reshape(count, width)
    keep2, send2, sum_v = late_weight_call(where, col_peers, nt, dk, dv, cls_rows, cls_low, vec)
    wide = lambda a: a.astype(F32)
    if direct:
        got2 = swap(send2, "row", 1)
        mine, to_x, to_y, to_far = fold_call(where, col_peers, keep1, got1, keep2, got2)
        mine, dq = join((mine, dq))
        near_x = swap(to_x, "dp", 1)
        near_y = swap(to_y, "row", 2)
        far = lax.ppermute(
            to_far,
            ("dp", "row"),
            [(4 * i + j, 4 * (i ^ 1) + (j ^ 2)) for i in range(2) for j in range(4)],
        )
    d_tok, block = token_grad_call(
        pages, heads, (x, dq, dk, dv, gres),
        (w_qkv, cls_rows, cls_low, vec, cls_part, vg_mlp, d_upb, d_table, sum_q, sum_v),
    )
    slab = width // (row_peers * col_peers)
    if direct:
        near_x, near_y, far, block = join((near_x, near_y, far, block))
        late = (wide(mine) + wide(near_x) + wide(near_y) + wide(far)).astype(BF16)
        beside = [swap(late[step], "col", step) for step in range(1, col_peers)]
        up, down = d_mlp[: ups * slab], d_mlp[ups * slab :]
        cut_up, cut_down = ups * slab // 2, width // 2

        def halves(place):
            return jnp.concatenate(
                [
                    lax.dynamic_slice_in_dim(up, place * cut_up, cut_up, 0),
                    lax.dynamic_slice_in_dim(down, place * cut_down, cut_down, 1).reshape(
                        -1, width
                    ),
                ],
                axis=0,
            )

        other = swap(halves(1 - page_at), "dp", 1)

    lead = 2 * pages
    vectors = block[lead:]
    parts, mine_at, place = block[:lead], jnp.zeros((), jnp.int32), 1
    sent = block
    for axis in ("col", "row"):
        peers, rows_in = lax.axis_size(axis), parts.shape[0]
        got = [swap(sent, axis, bit) for bit in range(1, peers)]
        level = [vectors] + [g[rows_in:] for g in got]
        while len(level) > 1:
            level = [a + b for a, b in zip(level[0::2], level[1::2])]
        vectors = level[0]
        parts = jnp.concatenate([parts] + [g[:rows_in] for g in got], axis=0)
        mine_at = mine_at + place * lax.axis_index(axis).astype(jnp.int32)
        place = place * peers
        sent = jnp.concatenate([parts, vectors], axis=0)

    d_cls, v = vectors[:pages], vectors[pages:]
    bit = 1
    while bit < lax.axis_size("dp"):
        v, bit = v + swap(v, "dp", bit), 2 * bit
    out_cls = class_close_call(
        geo, mine_at[None], parts.reshape(-1, 2 * pages, width), halo, cls_rows, to_head, w_out, vec, w_up,
        w_down,
    )[:pages]

    half = 3 * width // 2
    if direct:
        beside, other, v, out_cls = join((beside, other, v, out_cls))
        late = wide(late[0])
        for part in beside:
            late = late + wide(part)
        d_qkv, d_wout = late[:, :half], late[:, half:]
        both = wide(halves(page_at)) + wide(other)
        d_up = jnp.transpose(both[:cut_up].reshape(-1, slab, width), (1, 0, 2)).reshape(slab, -1)
        d_down = both[cut_up:].reshape(-1, cut_down)
    else:
        def whole(keep, send):
            both = jnp.stack([keep, send]).reshape(2, 2, col_peers, slab, 2 * width)
            return jnp.transpose(both, (1, 0, 2, 3, 4)).reshape(width, 2 * width)

        early, late = whole(keep1, send1), whole(keep2, send2)
        d_qkv = spread_sum(jnp.concatenate([early[:, :width], late], axis=1))
        d_wout = spread_sum(early[:, width:])
        d_up = jnp.transpose(d_mlp[: ups * slab].reshape(ups, slab, width), (1, 0, 2))
        d_up = page_sum(d_up.reshape(slab, ups * width), 1).astype(F32)
        d_down = page_sum(d_mlp[ups * slab :], 1).astype(F32)

    d_rel = v[11 + ups : 13 + ups].reshape(-1)[: heads * LANES].reshape(heads, LANES)[:, : SPAN * SPAN + 1]
    return (
        out.reshape(tokens.shape),
        out_cls,
        d_tok.reshape(tokens.shape),
        d_cls,
        d_qkv,
        d_wout,
        d_up,
        d_down,
        v[0],
        v[1],
        v[2],
        v[3],
        v[4],
        d_rel,
        v[10],
        v[9],
        v[7],
        v[8],
        v[11 : 11 + ups].reshape(-1),
        v[6],
        v[5],
    )


def solution(mesh):
    tile = P("dp", "row", "col", None)
    flat = P("dp", "row", "col")
    weights = P(("row", "col"), "dp")
    return jax.shard_map(
        shards,
        mesh=mesh,
        in_specs=(tile, P("dp", None), flat, flat) + (P(),) * 17 + (tile,),
        out_specs=(tile, P("dp", None), tile, P("dp", None)) + (weights,) * 4 + (P(),) * 13,
        check_vma=False,
    )
```

profile of v0, /device:TPU:0, one launch (start us, length us, event | category | flops | bytes accessed | tf_op | source)
XLA Modules:
  0.0 282.4 jit_solution(884039232466141518)
XLA Ops:
  8.2 3.0 %broadcast_select_fusion = (bf16[4,16,16,768]{3,2,1,0:T(8,128)(2,1)}, bf16[4,16,16,768]{3,2,1,0:T(8,128)(2,1)S(1)}) fusion(bf16[4,16,16,768]{3,2,1,0:T(8,128)(2,1)} %param.58, pred[4,16,16]{2,1,0:T(8,128)(4,1)S(1)} %get-tuple-element.161, bf16[4,16,16,768]{3,2,1,0:T(8,128)(2,1)} %param.37, pred[4,16,16]{2,1,0:T(8,128)(4,1)S(1)} %get-tuple-element.162), kind=kLoop, calls=%fused_computation | loop fusion | flops 1572864 | bytes 6293504 | tf_op jit(solution)/shard_map/jit(_where)/select_n | solution.py:1185
  11.3 2.4 collective-permute-start
  16.7 2.5 collective-permute-done.1.bottom_ref
  20.0 3.3 %strips.2 = (bf16[4,72,768]{2,1,0:T(8,128)(2,1)}, bf16[4,72,768]{2,1,0:T(8,128)(2,1)}) custom-call(bf16[4,256,768]{2,1,0:T(8,128)(2,1)} %bitcast.45, bf16[4,48,768]{2,1,0:T(8,128)(2,1)} %copy-done.7, bf16[4,48,768]{2,1,0:T(8,128)(2,1)} %copy-done.8), custom_call_target="tpu_custom_call" | custom-call | tf_op jit(solution)/shard_map/strips/pallas_call | solution.py:318
  23.3 3.5 %collective-permute-start.2 = (bf16[4,72,768]{2,1,0:T(8,128)(2,1)}, bf16[4,72,768]{2,1,0:T(8,128)(2,1)S(1)}, u32[]{:S(2)}, u32[]{:S(2)}) collective-permute-start(bf16[4,72,768]{2,1,0:T(8,128)(2,1)} %get-tuple-element.72), channel_id=1, source_target_pairs={{0,1},{1,2},{2,3},{4,5},{5,6},{6,7},{8,9},{9,10},{10,11},{12,13},{... | collective-permute-start | bytes 1327112 | tf_op jit(solution)/shard_map/ppermute | solution.py:1113
  28.7 3.0 %bias_table.2.bias_ref = f32[3,256,256]{2,1,0:T(8,128)} custom-call(f32[12,50]{1,0:T(8,128)} %table.3, s32[16,256]{1,0:T(8,128)} %constant.116.clone.index_ref), custom_call_target="tpu_custom_call" | custom-call | tf_op jit(solution)/shard_map/bias_table/pallas_call | solution.py:228
  31.7 8.2 %qkv_own.1.own_ref = bf16[4,256,2304]{2,1,0:T(8,128)(2,1)} custom-call(bf16[4,256,768]{2,1,0:T(8,128)(2,1)} %bitcast.46, bf16[768,2304]{1,0:T(8,128)(2,1)} %w_ref.5, f32[16,768]{1,0:T(8,128)} %reshape.112.vec_ref), custom_call_target="tpu_custom_call" | custom-call | flops 3623878656 | bytes 9830400 | tf_op jit(solution)/shard_map/qkv_own/pallas_call | solution.py:282
  41.5 9.7 %qkv_halo.1.halo_ref.cls_ref = bf16[4,288,2304]{2,1,0:T(8,128)(2,1)} custom-call(bf16[4,48,768]{2,1,0:T(8,128)(2,1)} %copy-done.7, bf16[4,48,768]{2,1,0:T(8,128)(2,1)} %copy-done.8, bf16[4,72,768]{2,1,0:T(8,128)(2,1)} %copy-done.30, bf16[4,72,768]{2,1,0:T(8,128)(2,1)} %copy-done.31, bf16[4,16,768]{2,1,0:T(8,128)(2,1)} %broadcast_select_fusion.2.last_ref, ...), custom_call_target="tpu_custom_call" | custom-call | flops 4076863488 | bytes 10616832 | tf_op jit(solution)/shard_map/qkv_halo/pallas_call | solution.py:282
  51.1 11.7 %attend.1 = (bf16[4,256,768]{2,1,0:T(8,128)(2,1)}, f32[4,256,128]{2,1,0:T(8,128)}, bf16[4,3,4,256,256]{4,3,2,1,0:T(8,128)(2,1)}, f32[8,768]{1,0:T(8,128)}) custom-call(bf16[4,256,2304]{2,1,0:T(8,128)(2,1)} %qkv_own.1.own_ref, bf16[4,288,2304]{2,1,0:T(8,128)(2,1)} %qkv_halo.1.halo_ref.cls_ref, f32[3,256,256]{2,1,0:T(8,128)} %bias_table.2.bias_ref, ...), custom_call_target="tpu_custom_call" | custom-call | flops 3221225472 | bytes 16777216 | tf_op jit(solution)/shard_map/attend/pallas_call | solution.py:418
  62.8 49.3 %mlp.1 = (bf16[1024,768]{1,0:T(8,128)(2,1)}, bf16[1024,896]{1,0:T(8,128)(2,1)}, f32[1024,768]{1,0:T(8,128)}, bf16[1024,768]{1,0:T(8,128)(2,1)}, bf16[16,384,768]...) custom-call(bf16[1024,768]{1,0:T(8,128)(2,1)} %bitcast.59, bf16[1024,768]{1,0:T(8,128)(2,1)} %bitcast.47, ...), custom_call_target="tpu_custom_call" | custom-call | flops 31406948352 | bytes 31457280 | tf_op jit(solution)/shard_map/mlp/pallas_call | solution.py:571
  113.4 6.7 %collective-permute-start.5 = (bf16[4,48,896]{2,1,0:T(8,128)(2,1)S(1)}, bf16[4,48,896]{2,1,0:T(8,128)(2,1)S(1)}, u32[]{:S(2)}, u32[]{:S(2)}) collective-permute-start(bf16[4,48,896]{2,1,0:T(8,128)(2,1)S(1)} %get-tuple-element.139), channel_id=1, source_target_pairs={{0,4},{4,8},{8,12},{1,5},{5,9},{9,13},{2,6},{6,10},{10,14},{3,7},{... | collective-permute-start | bytes 1032200 | tf_op jit(solution)/shard_map/ppermute | solution.py:1113
  121.4 3.0 %bias_table.3.bias_ref = f32[3,256,256]{2,1,0:T(8,128)} custom-call(f32[12,50]{1,0:T(8,128)} %table.3, s32[16,256]{1,0:T(8,128)} %constant.118.clone.index_ref), custom_call_target="tpu_custom_call" | custom-call | tf_op jit(solution)/shard_map/bias_table/pallas_call | solution.py:228
  127.3 3.9 %strips.3 = (bf16[4,72,896]{2,1,0:T(8,128)(2,1)}, bf16[4,72,896]{2,1,0:T(8,128)(2,1)}) custom-call(bf16[4,256,896]{2,1,0:T(8,128)(2,1)} %bitcast.41, bf16[4,48,896]{2,1,0:T(8,128)(2,1)} %copy-done.5, bf16[4,48,896]{2,1,0:T(8,128)(2,1)} %copy-done.6), custom_call_target="tpu_custom_call" | custom-call | tf_op jit(solution)/shard_map/strips/pallas_call | solution.py:318
  131.2 4.2 %collective-permute-start.7 = (bf16[4,72,896]{2,1,0:T(8,128)(2,1)}, bf16[4,72,896]{2,1,0:T(8,128)(2,1)S(1)}, u32[]{:S(2)}, u32[]{:S(2)}) collective-permute-start(bf16[4,72,896]{2,1,0:T(8,128)(2,1)} %get-tuple-element.83), channel_id=1, source_target_pairs={{0,1},{1,2},{2,3},{4,5},{5,6},{6,7},{8,9},{9,10},{10,11},{12,13},{... | collective-permute-start | bytes 1548296 | tf_op jit(solution)/shard_map/ppermute | solution.py:1113
  136.7 12.7 %query_grad.1 = (bf16[4,256,768]{2,1,0:T(8,128)(2,1)}, f32[16,128]{1,0:T(8,128)}) custom-call(bf16[4,3,4,256,256]{4,3,2,1,0:T(8,128)(2,1)} %get-tuple-element.77.p_ref, bf16[4,256,2304]{2,1,0:T(8,128)(2,1)} %qkv_own.1.own_ref, bf16[4,288,2304]{2,1,0:T(8,128)(2,1)} %qkv_halo.1.halo_ref.cls_ref, bf16[4,256,896]{2,1,0:T(8,128)(2,1)} %bitcast.42, ...), custom_call_target="tpu_custom_call" | custom-call | flops 3221225472 | bytes 20971520 | tf_op jit(solution)/shard_map/query_grad/pallas_call | solution.py:695
  149.4 10.9 %early_weight.1 = (bf16[8,48,1536]{2,1,0:T(8,128)(2,1)}, bf16[8,48,1536]{2,1,0:T(8,128)(2,1)}, bf16[768,1024]{1,0:T(8,128)(2,1)}, f32[8,768]{1,0:T(8,128)}) custom-call(s32[4]{0:T(128)} %pad_add_fusion.at_ref, bf16[1024,768]{1,0:T(8,128)(2,1)} %bitcast.48, bf16[1024,768]{1,0:T(8,128)(2,1)} %bitcast.60, bf16[1024,768]{1,0:T(8,128)(2,1)} %bitcast.55, ...), custom_call_target="tpu_custom_call" | custom-call | flops 2415919104 | bytes 10223616 | tf_op jit(solution)/shard_map/early_weight/pallas_call | solution.py:967
  160.4 1.8 collective-permute-start.4
  163.2 16.6 %key_grad.1 = (bf16[4,256,768]{2,1,0:T(8,128)(2,1)}, bf16[4,256,768]{2,1,0:T(8,128)(2,1)}, bf16[16,1536]{1,0:T(8,128)(2,1)}) custom-call(bf16[4,256,2304]{2,1,0:T(8,128)(2,1)} %qkv_own.1.own_ref, bf16[4,288,2304]{2,1,0:T(8,128)(2,1)} %qkv_halo.1.halo_ref.cls_ref, bf16[4,256,896]{2,1,0:T(8,128)(2,1)} %bitcast.43, bf16[4,48,896]{2,1,0:T(8,128)(2,1)} %copy-done.5, ...), custom_call_target="tpu_custom_call" | custom-call | flops 6442450944 | bytes 20971520 | tf_op jit(solution)/shard_map/key_grad/pallas_call | solution.py:797
  179.9 8.8 %late_weight.1 = (bf16[8,48,1536]{2,1,0:T(8,128)(2,1)}, bf16[8,48,1536]{2,1,0:T(8,128)(2,1)}, f32[8,768]{1,0:T(8,128)}) custom-call(s32[4]{0:T(128)} %pad_add_fusion.at_ref, bf16[768,1024]{1,0:T(8,128)(2,1)} %get-tuple-element.86.nt_ref, bf16[1024,768]{1,0:T(8,128)(2,1)} %bitcast.61, bf16[1024,768]{1,0:T(8,128)(2,1)} %bitcast.63, ...), custom_call_target="tpu_custom_call" | custom-call | flops 2415919104 | bytes 10223616 | tf_op jit(solution)/shard_map/late_weight/pallas_call | solution.py:967
  188.7 3.0 %collective-permute-done.9.r2_ref = bf16[8,48,1536]{2,1,0:T(8,128)(2,1)S(1)} collective-permute-done((bf16[8,48,1536]{2,1,0:T(8,128)(2,1)}, bf16[8,48,1536]{2,1,0:T(8,128)(2,1)S(1)}, u32[]{:S(2)}, u32[]{:S(2)}) %collective-permute-start.9) | collective-permute-done | bytes 1179680 | tf_op jit(solution)/shard_map/ppermute | solution.py:1117
  193.0 1.7 fold.1
  198.3 12.7 %token_grad.1 = (f32[1024,768]{1,0:T(8,128)}, f32[32,768]{1,0:T(8,128)}) custom-call(bf16[1024,768]{1,0:T(8,128)(2,1)} %bitcast.49, bf16[1024,768]{1,0:T(8,128)(2,1)} %bitcast.56, bf16[1024,768]{1,0:T(8,128)(2,1)} %bitcast.62, bf16[1024,768]{1,0:T(8,128)(2,1)} %bitcast.64, f32[1024,768]{1,0:T(8,128)} %get-tuple-element.103.gres_ref, ...), custom_call_target="tpu_custom_call" | custom-call | flops 3623878656 | bytes 16121856 | tf_op jit(solution)/shard_map/token_grad/pallas_call | solution.py:1096
  211.0 16.5 %collective-permute-done.11 = bf16[4,48,1536]{2,1,0:T(8,128)(2,1)S(1)} collective-permute-done((bf16[4,48,1536]{2,1,0:T(8,128)(2,1)S(1)}, bf16[4,48,1536]{2,1,0:T(8,128)(2,1)S(1)}, u32[]{:S(2)}, u32[]{:S(2)}) %collective-permute-start.11) | collective-permute-done | bytes 589856 | tf_op jit(solution)/shard_map/ppermute | solution.py:1117
  227.5 3.0 %collective-permute-start.17 = (f32[32,768]{1,0:T(8,128)}, f32[32,768]{1,0:T(8,128)S(1)}, u32[]{:S(2)}, u32[]{:S(2)}) collective-permute-start(f32[32,768]{1,0:T(8,128)} %get-tuple-element.115), channel_id=1, source_target_pairs={{0,1},{1,0},{2,3},{3,2},{4,5},{5,4},{6,7},{7,6},{8,9},{9,8},{10,11... | collective-permute-start | bytes 294920 | tf_op jit(solution)/shard_map/ppermute | solution.py:1117
  230.5 2.6 collective-permute-start.18
  234.4 3.7 %collective-permute-done.17 = f32[32,768]{1,0:T(8,128)S(1)} collective-permute-done((f32[32,768]{1,0:T(8,128)}, f32[32,768]{1,0:T(8,128)S(1)}, u32[]{:S(2)}, u32[]{:S(2)}) %collective-permute-start.17) | collective-permute-done | bytes 98336 | tf_op jit(solution)/shard_map/ppermute | solution.py:1117
  238.2 8.1 %collective-permute-done.18 = f32[32,768]{1,0:T(8,128)S(1)} collective-permute-done((f32[32,768]{1,0:T(8,128)}, f32[32,768]{1,0:T(8,128)S(1)}, u32[]{:S(2)}, u32[]{:S(2)}) %collective-permute-start.18) | collective-permute-done | bytes 98336 | tf_op jit(solution)/shard_map/ppermute | solution.py:1117
  246.4 2.1 collective-permute-start.21
  248.5 4.4 %collective-permute-start.13 = (bf16[48,1536]{1,0:T(8,128)(2,1)S(1)}, bf16[48,1536]{1,0:T(8,128)(2,1)S(1)}, u32[]{:S(2)}, u32[]{:S(2)}) collective-permute-start(bf16[48,1536]{1,0:T(8,128)(2,1)S(1)} %get-tuple-element.148), channel_id=1, source_target_pairs={{0,1},{1,0},{2,3},{3,2},{4,5},{5,4},{6,7},{7,6},{8,9},{9,8},{10,11... | collective-permute-start | bytes 442376 | tf_op jit(solution)/shard_map/ppermute | solution.py:1117
  253.2 2.6 collective-permute-start.15
  258.7 2.1 collective-permute-start.16
  261.6 7.5 %class_close.1 = bf16[16,768]{1,0:T(8,128)(2,1)} custom-call(s32[1]{0:T(128)} %bitcast.19.mine_ref, f32[16,8,768]{2,1,0:T(8,128)} %bitcast.52, bf16[4,288,2304]{2,1,0:T(8,128)(2,1)} %qkv_halo.1.halo_ref.cls_ref, bf16[16,768]{1,0:T(8,128)(2,1)} %concatenate.26.c_ref.x_ref, bf16[768,128]{1,0:T(8,128)(2,1)} %constant.110.clone.toh_ref, ...), custom_call_target="tpu_custom_call" | custom-call | flops 339738624 | bytes 12582912 | tf_op jit(solution)/shard_map/class_close/pallas_call | solution.py:868
  (161 shorter events, 32.1 us)
Async XLA Ops:
  7.2 250.3 %reduce-scatter.2.cloned.1.call-start = ((), (), s32[]{:S(2)}) async-start(), calls=%async_computation.1 | async-start | bytes 10027008 | tf_op jit(solution)/shard_map/reduce_scatter | solution.py:1189
  8.2 7.8 %copy-start.23 = (f32[768]{0:T(1024)S(1)}, f32[768]{0:T(1024)}, u32[]{:S(2)}) copy-start(f32[768]{0:T(1024)} %param.46) | copy-start | bytes 9220
  11.2 8.0 %copy-start.3 = (bf16[4,16,16,768]{3,2,1,0:T(8,128)(2,1)}, bf16[4,16,16,768]{3,2,1,0:T(8,128)(2,1)S(1)}, u32[]{:S(2)}) copy-start(bf16[4,16,16,768]{3,2,1,0:T(8,128)(2,1)S(1)} %get-tuple-element.164) | copy-start | bytes 4718596
  11.2 16.8 %copy-start.12 = (f32[3072]{0:T(1024)S(1)}, f32[3072]{0:T(1024)}, u32[]{:S(2)}) copy-start(f32[3072]{0:T(1024)} %param.54) | copy-start | bytes 36868
  11.3 5.4 %collective-permute-start = (bf16[4,48,768]{2,1,0:T(8,128)(2,1)S(1)}, bf16[4,48,768]{2,1,0:T(8,128)(2,1)S(1)}, u32[]{:S(2)}, u32[]{:S(2)}) collective-permute-start(bf16[4,48,768]{2,1,0:T(8,128)(2,1)S(1)} %get-tuple-element.141), channel_id=1, source_target_pairs={{0,4},{4,8},{8,12},{1,5},{5,9},{9,13},{2,6},{6,10},{10,14},{3,7},{... | collective-permute-start | bytes 884744 | tf_op jit(solution)/shard_map/ppermute | solution.py:1113
  13.7 5.6 %collective-permute-start.1 = (bf16[4,48,768]{2,1,0:T(8,128)(2,1)S(1)}, bf16[4,48,768]{2,1,0:T(8,128)(2,1)S(1)}, u32[]{:S(2)}, u32[]{:S(2)}) collective-permute-start(bf16[4,48,768]{2,1,0:T(8,128)(2,1)S(1)} %get-tuple-element.140), channel_id=1, source_target_pairs={{4,0},{8,4},{12,8},{5,1},{9,5},{13,9},{6,2},{10,6},{14,10},{7,3},{... | collective-permute-start | bytes 884744 | tf_op jit(solution)/shard_map/ppermute | solution.py:1113
  23.3 16.7 %collective-permute-start.2 = (bf16[4,72,768]{2,1,0:T(8,128)(2,1)}, bf16[4,72,768]{2,1,0:T(8,128)(2,1)S(1)}, u32[]{:S(2)}, u32[]{:S(2)}) collective-permute-start(bf16[4,72,768]{2,1,0:T(8,128)(2,1)} %get-tuple-element.72), channel_id=1, source_target_pairs={{0,1},{1,2},{2,3},{4,5},{5,6},{6,7},{8,9},{9,10},{10,11},{12,13},{... | collective-permute-start | bytes 1327112 | tf_op jit(solution)/shard_map/ppermute | solution.py:1113
  26.8 13.2 %collective-permute-start.3 = (bf16[4,72,768]{2,1,0:T(8,128)(2,1)}, bf16[4,72,768]{2,1,0:T(8,128)(2,1)S(1)}, u32[]{:S(2)}, u32[]{:S(2)}) collective-permute-start(bf16[4,72,768]{2,1,0:T(8,128)(2,1)} %get-tuple-element.73), channel_id=1, source_target_pairs={{1,0},{2,1},{3,2},{5,4},{6,5},{7,6},{9,8},{10,9},{11,10},{13,12},{... | collective-permute-start | bytes 1327112 | tf_op jit(solution)/shard_map/ppermute | solution.py:1113
  112.2 12.9 %copy-start.10 = (f32[12,50]{1,0:T(8,128)S(1)}, f32[12,50]{1,0:T(8,128)}, u32[]{:S(2)}) copy-start(f32[12,50]{1,0:T(8,128)} %table.3) | copy-start | bytes 7204
  113.4 12.5 %collective-permute-start.5 = (bf16[4,48,896]{2,1,0:T(8,128)(2,1)S(1)}, bf16[4,48,896]{2,1,0:T(8,128)(2,1)S(1)}, u32[]{:S(2)}, u32[]{:S(2)}) collective-permute-start(bf16[4,48,896]{2,1,0:T(8,128)(2,1)S(1)} %get-tuple-element.139), channel_id=1, source_target_pairs={{0,4},{4,8},{8,12},{1,5},{5,9},{9,13},{2,6},{6,10},{10,14},{3,7},{... | collective-permute-start | bytes 1032200 | tf_op jit(solution)/shard_map/ppermute | solution.py:1113
  120.1 5.8 %collective-permute-start.6 = (bf16[4,48,896]{2,1,0:T(8,128)(2,1)S(1)}, bf16[4,48,896]{2,1,0:T(8,128)(2,1)S(1)}, u32[]{:S(2)}, u32[]{:S(2)}) collective-permute-start(bf16[4,48,896]{2,1,0:T(8,128)(2,1)S(1)} %get-tuple-element.138), channel_id=1, source_target_pairs={{4,0},{8,4},{12,8},{5,1},{9,5},{13,9},{6,2},{10,6},{14,10},{7,3},{... | collective-permute-start | bytes 1032200 | tf_op jit(solution)/shard_map/ppermute | solution.py:1113
  131.2 31.0 %collective-permute-start.7 = (bf16[4,72,896]{2,1,0:T(8,128)(2,1)}, bf16[4,72,896]{2,1,0:T(8,128)(2,1)S(1)}, u32[]{:S(2)}, u32[]{:S(2)}) collective-permute-start(bf16[4,72,896]{2,1,0:T(8,128)(2,1)} %get-tuple-element.83), channel_id=1, source_target_pairs={{0,1},{1,2},{2,3},{4,5},{5,6},{6,7},{8,9},{9,10},{10,11},{12,13},{... | collective-permute-start | bytes 1548296 | tf_op jit(solution)/shard_map/ppermute | solution.py:1113
  135.4 26.8 %collective-permute-start.8 = (bf16[4,72,896]{2,1,0:T(8,128)(2,1)}, bf16[4,72,896]{2,1,0:T(8,128)(2,1)S(1)}, u32[]{:S(2)}, u32[]{:S(2)}) collective-permute-start(bf16[4,72,896]{2,1,0:T(8,128)(2,1)} %get-tuple-element.84), channel_id=1, source_target_pairs={{1,0},{2,1},{3,2},{5,4},{6,5},{7,6},{9,8},{10,9},{11,10},{13,12},{... | collective-permute-start | bytes 1548296 | tf_op jit(solution)/shard_map/ppermute | solution.py:1113
  160.4 28.3 %collective-permute-start.4 = (bf16[8,48,1536]{2,1,0:T(8,128)(2,1)}, bf16[8,48,1536]{2,1,0:T(8,128)(2,1)S(1)}, u32[]{:S(2)}, u32[]{:S(2)}) collective-permute-start(bf16[8,48,1536]{2,1,0:T(8,128)(2,1)} %get-tuple-element.82), channel_id=1, source_target_pairs={{0,4},{4,0},{8,12},{12,8},{1,5},{5,1},{9,13},{13,9},{2,6},{6,2},{1... | collective-permute-start | bytes 3538952 | tf_op jit(solution)/shard_map/ppermute | solution.py:1117
  179.8 11.9 %copy-start = (bf16[8,48,1536]{2,1,0:T(8,128)(2,1)S(1)}, bf16[8,48,1536]{2,1,0:T(8,128)(2,1)}, u32[]{:S(2)}) copy-start(bf16[8,48,1536]{2,1,0:T(8,128)(2,1)} %get-tuple-element.81.k1_ref) | copy-start | bytes 3538948
  179.8 11.9 %copy-start.2 = (s32[4]{0:T(128)S(1)}, s32[4]{0:T(128)}, u32[]{:S(2)}) copy-start(s32[4]{0:T(128)} %pad_add_fusion.at_ref) | copy-start | bytes 52
  188.7 3.1 %collective-permute-start.9 = (bf16[8,48,1536]{2,1,0:T(8,128)(2,1)}, bf16[8,48,1536]{2,1,0:T(8,128)(2,1)S(1)}, u32[]{:S(2)}, u32[]{:S(2)}) collective-permute-start(bf16[8,48,1536]{2,1,0:T(8,128)(2,1)} %get-tuple-element.96), channel_id=1, source_target_pairs={{0,4},{4,0},{8,12},{12,8},{1,5},{5,1},{9,13},{13,9},{2,6},{6,2},{1... | collective-permute-start | bytes 3538952 | tf_op jit(solution)/shard_map/ppermute | solution.py:1117
  194.8 16.2 %collective-permute-start.10 = (bf16[4,48,1536]{2,1,0:T(8,128)(2,1)S(1)}, bf16[4,48,1536]{2,1,0:T(8,128)(2,1)S(1)}, u32[]{:S(2)}, u32[]{:S(2)}) collective-permute-start(bf16[4,48,1536]{2,1,0:T(8,128)(2,1)S(1)} %get-tuple-element.99), channel_id=1, source_target_pairs={{0,16},{16,0},{1,17},{17,1},{2,18},{18,2},{3,19},{19,3},{4,20},{20... | collective-permute-start | bytes 1769480 | tf_op jit(solution)/shard_map/ppermute | solution.py:1117
  196.4 31.1 %collective-permute-start.11 = (bf16[4,48,1536]{2,1,0:T(8,128)(2,1)S(1)}, bf16[4,48,1536]{2,1,0:T(8,128)(2,1)S(1)}, u32[]{:S(2)}, u32[]{:S(2)}) collective-permute-start(bf16[4,48,1536]{2,1,0:T(8,128)(2,1)S(1)} %get-tuple-element.100), channel_id=1, source_target_pairs={{0,8},{4,12},{8,0},{12,4},{1,9},{5,13},{9,1},{13,5},{2,10},{6,14},... | collective-permute-start | bytes 1769480 | tf_op jit(solution)/shard_map/ppermute | solution.py:1117
  197.1 30.4 %collective-permute-start.12 = (bf16[4,48,1536]{2,1,0:T(8,128)(2,1)S(1)}, bf16[4,48,1536]{2,1,0:T(8,128)(2,1)}, u32[]{:S(2)}, u32[]{:S(2)}) collective-permute-start(bf16[4,48,1536]{2,1,0:T(8,128)(2,1)S(1)} %get-tuple-element.101), channel_id=1, source_target_pairs={{0,24},{4,28},{8,16},{12,20},{16,8},{20,12},{24,0},{28,4},{1,25},{... | collective-permute-start | bytes 1769480 | tf_op jit(solution)/shard_map/ppermute | solution.py:1219
  211.0 23.4 %copy-start.9 = (f32[32,768]{1,0:T(8,128)S(1)}, f32[32,768]{1,0:T(8,128)}, u32[]{:S(2)}) copy-start(f32[32,768]{1,0:T(8,128)} %get-tuple-element.115) | copy-start | bytes 294916
  227.5 10.7 %collective-permute-start.17 = (f32[32,768]{1,0:T(8,128)}, f32[32,768]{1,0:T(8,128)S(1)}, u32[]{:S(2)}, u32[]{:S(2)}) collective-permute-start(f32[32,768]{1,0:T(8,128)} %get-tuple-element.115), channel_id=1, source_target_pairs={{0,1},{1,0},{2,3},{3,2},{4,5},{5,4},{6,7},{7,6},{8,9},{9,8},{10,11... | collective-permute-start | bytes 294920 | tf_op jit(solution)/shard_map/ppermute | solution.py:1117
  230.5 15.8 %collective-permute-start.18 = (f32[32,768]{1,0:T(8,128)}, f32[32,768]{1,0:T(8,128)S(1)}, u32[]{:S(2)}, u32[]{:S(2)}) collective-permute-start(f32[32,768]{1,0:T(8,128)} %get-tuple-element.115), channel_id=1, source_target_pairs={{0,2},{1,3},{2,0},{3,1},{4,6},{5,7},{6,4},{7,5},{8,10},{9,11},{10,... | collective-permute-start | bytes 294920 | tf_op jit(solution)/shard_map/ppermute | solution.py:1117
  233.1 13.2 %collective-permute-start.19 = (f32[32,768]{1,0:T(8,128)}, f32[32,768]{1,0:T(8,128)S(1)}, u32[]{:S(2)}, u32[]{:S(2)}) collective-permute-start(f32[32,768]{1,0:T(8,128)} %get-tuple-element.115), channel_id=1, source_target_pairs={{0,3},{1,2},{2,1},{3,0},{4,7},{5,6},{6,5},{7,4},{8,11},{9,10},{10,... | collective-permute-start | bytes 294920 | tf_op jit(solution)/shard_map/ppermute | solution.py:1117
  246.3 6.9 %collective-permute-start.22 = (f32[56,768]{1,0:T(8,128)S(1)}, f32[56,768]{1,0:T(8,128)S(1)}, u32[]{:S(2)}, u32[]{:S(2)}) collective-permute-start(f32[56,768]{1,0:T(8,128)S(1)} %get-tuple-element.136), channel_id=1, source_target_pairs={{0,12},{4,8},{8,4},{12,0},{1,13},{5,9},{9,5},{13,1},{2,14},{6,10},... | collective-permute-start | bytes 516104 | tf_op jit(solution)/shard_map/ppermute | solution.py:1117
  246.4 10.3 %collective-permute-start.21 = (f32[56,768]{1,0:T(8,128)S(1)}, f32[56,768]{1,0:T(8,128)S(1)}, u32[]{:S(2)}, u32[]{:S(2)}) collective-permute-start(f32[56,768]{1,0:T(8,128)S(1)} %get-tuple-element.136), channel_id=1, source_target_pairs={{0,8},{4,12},{8,0},{12,4},{1,9},{5,13},{9,1},{13,5},{2,10},{6,14},... | collective-permute-start | bytes 516104 | tf_op jit(solution)/shard_map/ppermute | solution.py:1117
  248.5 8.3 %collective-permute-start.20 = (f32[56,768]{1,0:T(8,128)S(1)}, f32[56,768]{1,0:T(8,128)S(1)}, u32[]{:S(2)}, u32[]{:S(2)}) collective-permute-start(f32[56,768]{1,0:T(8,128)S(1)} %get-tuple-element.136), channel_id=1, source_target_pairs={{0,4},{4,0},{8,12},{12,8},{1,5},{5,1},{9,13},{13,9},{2,6},{6,2},{1... | collective-permute-start | bytes 516104 | tf_op jit(solution)/shard_map/ppermute | solution.py:1117
  248.5 22.0 %collective-permute-start.13 = (bf16[48,1536]{1,0:T(8,128)(2,1)S(1)}, bf16[48,1536]{1,0:T(8,128)(2,1)S(1)}, u32[]{:S(2)}, u32[]{:S(2)}) collective-permute-start(bf16[48,1536]{1,0:T(8,128)(2,1)S(1)} %get-tuple-element.148), channel_id=1, source_target_pairs={{0,1},{1,0},{2,3},{3,2},{4,5},{5,4},{6,7},{7,6},{8,9},{9,8},{10,11... | collective-permute-start | bytes 442376 | tf_op jit(solution)/shard_map/ppermute | solution.py:1117
  253.0 17.6 %collective-permute-start.14 = (bf16[48,1536]{1,0:T(8,128)(2,1)S(1)}, bf16[48,1536]{1,0:T(8,128)(2,1)S(1)}, u32[]{:S(2)}, u32[]{:S(2)}) collective-permute-start(bf16[48,1536]{1,0:T(8,128)(2,1)S(1)} %get-tuple-element.147), channel_id=1, source_target_pairs={{0,2},{1,3},{2,0},{3,1},{4,6},{5,7},{6,4},{7,5},{8,10},{9,11},{10,... | collective-permute-start | bytes 442376 | tf_op jit(solution)/shard_map/ppermute | solution.py:1117
  253.2 17.4 %collective-permute-start.15 = (bf16[48,1536]{1,0:T(8,128)(2,1)S(1)}, bf16[48,1536]{1,0:T(8,128)(2,1)S(1)}, u32[]{:S(2)}, u32[]{:S(2)}) collective-permute-start(bf16[48,1536]{1,0:T(8,128)(2,1)S(1)} %get-tuple-element.146), channel_id=1, source_target_pairs={{0,3},{1,2},{2,1},{3,0},{4,7},{5,6},{6,5},{7,4},{8,11},{9,10},{10,... | collective-permute-start | bytes 442376 | tf_op jit(solution)/shard_map/ppermute | solution.py:1117
  257.4 13.1 %collective-permute-start.23 = (f32[20,768]{1,0:T(8,128)}, f32[20,768]{1,0:T(8,128)S(1)}, u32[]{:S(2)}, u32[]{:S(2)}) collective-permute-start(f32[20,768]{1,0:T(8,128)} %slice.204), channel_id=1, source_target_pairs={{0,16},{16,0},{1,17},{17,1},{2,18},{18,2},{3,19},{19,3},{4,20},{20... | collective-permute-start | bytes 184328 | tf_op jit(solution)/shard_map/ppermute | solution.py:1117
  258.7 11.8 %collective-permute-start.16 = (bf16[192,768]{1,0:T(8,128)(2,1)S(1)}, bf16[192,768]{1,0:T(8,128)(2,1)S(1)}, u32[]{:S(2)}, u32[]{:S(2)}) collective-permute-start(bf16[192,768]{1,0:T(8,128)(2,1)S(1)} %pad_maximum_fusion), channel_id=1, source_target_pairs={{0,16},{16,0},{1,17},{17,1},{2,18},{18,2},{3,19},{19,3},{4,20},{20... | collective-permute-start | bytes 884744 | tf_op jit(solution)/shard_map/ppermute | solution.py:1117
  (26 other events, 124.2 us)
Sparse Core Ops, SparseCore 0:
  112.3 139.1 reduce-scatter.1
where the time goes:
time: 285 us; the launch traced here: 282 us
  Pallas kernels  163 us (57%)
  starting transfers between devices  44.5 us (16%)
  waiting for transfers between devices  34.9 us (12%)
  local copies, waits for them, and re-layouts  17.6 us (6%)
  between operations  14.8 us (5%)
  other arithmetic  7.38 us (3%)
    pallas_call x1, Pallas kernels, mlp_call(): pl.pallas_call(functools.partial(mlp_body, tile, steps), out_shape=(jax.S...  49.3 us
    ppermute x15, waiting for transfers between devices, swap(): lax.ppermute(value, axis, [(i, i ^ bit) for i in range(lax.axis_size(axis...  32.3 us
    ppermute x8, starting transfers between devices, passed_along(): lax.ppermute(value, axis, [(i, i + steps) for i in range(first, last)])  22 us
    ppermute x15, starting transfers between devices, swap(): lax.ppermute(value, axis, [(i, i ^ bit) for i in range(lax.axis_size(axis...  21.3 us
    pallas_call x2, Pallas kernels, weight_call(): pl.pallas_call(body, out_shape=(out, out) + more, grid_spec=pltpu.Prefetc...  19.8 us
    pallas_call x2, Pallas kernels, qkv_call(): pl.pallas_call(body, out_shape=jax.ShapeDtypeStruct((pages, rows, 3 * d),...  17.9 us
    pallas_call x1, Pallas kernels, key_grad_call(): pl.pallas_call(functools.partial(key_grad_body, geo), out_shape=(out, out...  16.6 us
    pallas_call x1, Pallas kernels, query_grad_call(): pl.pallas_call(functools.partial(query_grad_body, geo), out_shape=(dq, ta...  12.7 us
  transfers between devices with their start and end apart: 25, of which 6 were waited for; matrix products, arithmetic and copies ran while one was open for 4% of the time, Pallas kernels for 32%

commit v1 on v0

--- a/solution.py
+++ b/solution.py
@@ -21,6 +21,7 @@
 ROOM, LESS = 56, 28
 EPS = 1e-06
 MIB = 1 << 20
+ANYWHERE = pl.BlockSpec(memory_space=pl.ANY)
 
 
 def dot(a, b):
@@ -271,6 +272,11 @@
     qkv_rows(raw, w_ref, vec_ref, o_ref)
 
 
+def part_of(a, i, d, rows=None):
+    rows = rows or a.shape[1]
+    return pl.BlockSpec((1, rows, d), lambda p: (p, a.shape[1] // rows - 1, i))
+
+
 def by_page(a, span=1):
     return pl.BlockSpec((span,) + a.shape[1:], lambda p: (p,) + (0,) * (len(a.shape) - 1))
 
@@ -327,8 +333,8 @@
     )(x, top, bottom)
 
 
-def class_part(geo, own_ref, halo_ref, hr_ref, hrf_ref, o_ref):
-    page, d, at = pl.program_id(0), geo.width, geo.halo - 16
+def class_part(geo, own_ref, cq_ref, hr_ref, hrf_ref, o_ref):
+    page, d = pl.program_id(0), geo.width
 
     @pl.when(page == 0)
     def _():
@@ -336,7 +342,7 @@
 
     scale = BF16(1.0 / math.sqrt(geo.head))
     hr, hrf = hr_ref[...], hrf_ref[...]
-    qc = jnp.broadcast_to(halo_ref[0, at : at + 1, 0:d] * scale, (16, d)) * hr
+    qc = jnp.broadcast_to(cq_ref[0, 0:1, :] * scale, (16, d)) * hr
     s = dot_t(qc, own_ref[0, :, d : 2 * d])
     top = jnp.max(s, axis=-1, keepdims=True)
     e = jnp.exp(s - top)
@@ -352,7 +358,8 @@
 
 
 def attend_body(
-    geo, own_ref, halo_ref, bias_ref, ok_ref, hm_ref, hr_ref, hrf_ref, o_ref, lse_ref, p_ref, c_ref
+    geo, own_ref, hk_ref, hv_ref, cq_ref, bias_ref, ok_ref, hm_ref, hr_ref, hrf_ref, o_ref, lse_ref,
+    p_ref, c_ref,
 ):
     scale = BF16(1.0 / math.sqrt(geo.head))
     hm = hm_ref[...]
@@ -366,7 +373,7 @@
         return ref[0, :, lo : lo + geo.lanes]
 
     def score(g):
-        q, k, hk = part(own_ref, 0, g), part(own_ref, 1, g), part(halo_ref, 1, g)
+        q, k, hk = part(own_ref, 0, g), part(own_ref, 1, g), part(hk_ref, 0, g)
         return [
             dot_t(geo.stacked(q[at[b]] * scale, hm), geo.block(k, hk, b))
             + bias_ref[g]
@@ -390,12 +397,12 @@
         return probs
 
     def mix(g, probs):
-        v, hv = part(own_ref, 2, g), part(halo_ref, 2, g)
+        v, hv = part(own_ref, 2, g), part(hv_ref, 0, g)
         for b in bands:
             rows = geo.unstacked(dot(probs[b], geo.block(v, hv, b)))
             o_ref[0, at[b], g * geo.lanes : (g + 1) * geo.lanes] = rows.astype(BF16)
 
-    class_part(geo, own_ref, halo_ref, hr_ref, hrf_ref, c_ref)
+    class_part(geo, own_ref, cq_ref, hr_ref, hrf_ref, c_ref)
     scores = score(0)
     for g in range(geo.groups):
         probs = soften(g, scores)
@@ -419,21 +426,24 @@
         functools.partial(attend_body, geo),
         out_shape=outs,
         grid=(geo.pages,),
-        in_specs=[by_page(own), by_page(halo)] + [hold(a.shape) for a in (bias, ok, hm, hr, hrf)],
+        in_specs=[by_page(own)]
+        + [part_of(halo, i, geo.width) for i in (1, 2)]
+        + [part_of(halo, 0, geo.width, 16)]
+        + [hold(a.shape) for a in (bias, ok, hm, hr, hrf)],
         out_specs=[by_page(a) for a in outs[:3]] + [hold((2 * geo.pages, geo.width))],
         compiler_params=params(ROOM),
         cost_estimate=pl.CostEstimate(
             flops=2 * mm, transcendentals=geo.pages * G * geo.bands * 65536, bytes_accessed=16 * MIB
         ),
         name="attend",
-    )(own, halo, bias, ok, hm, hr, hrf)
+    )(own, halo, halo, halo, bias, ok, hm, hr, hrf)
 
 
 def mlp_body(
     tile, steps, att_ref, x_ref, og_ref, lse_ref, wout_ref, vec_ref, toh_ref, wup_ref, wdn_ref,
     out_ref, gmx_ref, gres_ref, gb_ref, dw_ref, vg_ref, dub_ref,
     n2, n2t, gm, res, branch, mlp, gn, act, dh, up_buf, dn_buf, out_buf, gmx_buf, gres_buf, gb_buf,
-    sems, out_sems,
+    og_buf, lse_buf, wup_buf, wdn_buf, sems, out_sems, in_sems, w_sems,
 ):
     step = pl.program_id(0)
     n, d = n2.shape
@@ -441,9 +451,24 @@
     tiles, few, rows_dn = n // tile, dn_buf.shape[0], dn_buf.shape[1]
     rows_up = up_buf.shape[1]
     span = lambda t: pl.ds(pl.multiple_of(t * tile, tile), tile)
+    late = (
+        pltpu.make_async_copy(og_ref, og_buf, in_sems.at[0]),
+        pltpu.make_async_copy(lse_ref, lse_buf, in_sems.at[1]),
+    )
+
+    def weights(c):
+        slot = lax.rem(c, 2)
+        at = pl.ds(pl.multiple_of(c * d, d), d)
+        return (
+            pltpu.make_async_copy(wup_ref.at[:, at], wup_buf.at[slot], w_sems.at[slot, 0]),
+            pltpu.make_async_copy(wdn_ref.at[at, :], wdn_buf.at[slot], w_sems.at[slot, 1]),
+        )
 
     @pl.when(step == 0)
     def _():
+        for copy in late + weights(0):
+            copy.start()
+
         def one(t, carry):
             rows = span(t)
             x = unmask(x_ref[rows, :].astype(F32), row(0))
@@ -453,7 +478,6 @@
             res[rows, :] = r
             unit, _ = norm_parts(r)
             n2[rows, :] = (unit * row(5) + row(6)).astype(BF16)
-            gm[rows, :] = (row(8) * og_ref[rows, :].astype(F32)).astype(BF16)
             mlp[rows, :] = jnp.zeros((tile, d), F32)
             gn[rows, :] = jnp.zeros((tile, d), F32)
             return carry
@@ -461,8 +485,25 @@
         lax.fori_loop(0, tiles, one, 0)
         n2t[...] = n2[...].T
         vg_ref[...] = jnp.zeros_like(vg_ref)
-
-    wup, wdn = wup_ref[...], wdn_ref[...]
+        for copy in late:
+            copy.wait()
+
+        def two(t, carry):
+            rows = span(t)
+            gm[rows, :] = (row(8) * og_buf[rows, :].astype(F32)).astype(BF16)
+            return carry
+
+        lax.fori_loop(0, tiles, two, 0)
+
+    for copy in weights(step):
+        copy.wait()
+
+    @pl.when(step + 1 < steps)
+    def _():
+        for copy in weights(step + 1):
+            copy.start()
+
+    wup, wdn = wup_buf[lax.rem(step, 2)], wdn_buf[lax.rem(step, 2)]
     upb = vec_ref[pl.ds(12 + step, 1), :]
     dub_ref[...] = jnp.zeros_like(dub_ref)
 
@@ -526,7 +567,7 @@
                     copy.wait()
 
             r, br, att = res[rows, :], branch[rows, :], att_ref[rows, :]
-            og = og_ref[rows, :].astype(F32)
+            og = og_buf[rows, :].astype(F32)
             mo = mlp[rows, :] + row(7)
             out_buf[slot] = (r + row(8) * mo).astype(BF16)
             add(0, og * mo)
@@ -545,7 +586,7 @@
             prod = mix.astype(F32) * att.astype(F32)
             delta = sum(dot(part, toh_ref[...]) for part in split3(prod))
             packed = jnp.zeros(delta.shape, F32)
-            for i, part in enumerate(split3(lse_ref[rows, :]) + split3(delta)):
+            for i, part in enumerate(split3(lse_buf[rows, :]) + split3(delta)):
                 part = part.astype(F32)
                 packed += part if i == 0 else pltpu.roll(part, 16 * i, 1)
             gmx_buf[slot, :, 0:d] = mix
@@ -580,8 +621,9 @@
             jax.ShapeDtypeStruct((8, ff), F32),
         ),
         grid=(steps,),
-        in_specs=[hold(a.shape) for a in (att, x, og, lse, w_out, vec, to_head)]
-        + [pl.BlockSpec((d, d), lambda c: (0, c)), pl.BlockSpec((d, d), lambda c: (c, 0))],
+        in_specs=[hold(att.shape), hold(x.shape), anywhere, anywhere]
+        + [hold(a.shape) for a in (w_out, vec, to_head)]
+        + [anywhere, anywhere],
         out_specs=[anywhere] * 5 + [hold((8, d)), pl.BlockSpec((8, d), lambda c: (0, c))],
         scratch_shapes=[
             pltpu.VMEM((n, d), BF16),
@@ -599,8 +641,14 @@
             pltpu.VMEM((2, tile, d + LANES), BF16),
             pltpu.VMEM((2, tile, d), F32),
             pltpu.VMEM((2, tile, d), BF16),
+            pltpu.VMEM((n, d), BF16),
+            pltpu.VMEM((n, LANES), F32),
+            pltpu.VMEM((2, d, d), BF16),
+            pltpu.VMEM((2, d, d), BF16),
             pltpu.SemaphoreType.DMA((2,)),
             pltpu.SemaphoreType.DMA((2, 4)),
+            pltpu.SemaphoreType.DMA((2,)),
+            pltpu.SemaphoreType.DMA((2, 2)),
         ],
         compiler_params=params(ROOM),
         cost_estimate=pl.CostEstimate(
@@ -638,7 +686,8 @@
 
 
 def query_grad_body(
-    geo, p_ref, own_ref, halo_ref, gm_ref, hm_ref, sm_ref, fold_ref, dq_ref, table_ref, rel_ref
+    geo, p_ref, k_ref, v_ref, hk_ref, hv_ref, gm_ref, hm_ref, sm_ref, fold_ref, dq_ref, table_ref,
+    rel_ref,
 ):
     scale = 1.0 / math.sqrt(geo.head)
     hm = hm_ref[...]
@@ -657,7 +706,7 @@
         return ref[0, :, lo : lo + geo.lanes]
 
     def pull(g):
-        gm, v, hv = part(gm_ref, 0, g), part(own_ref, 2, g), part(halo_ref, 2, g)
+        gm, v, hv = part(gm_ref, 0, g), part(v_ref, 0, g), part(hv_ref, 0, g)
         sm = sm_ref[g]
         return [
             dot_t(
@@ -676,7 +725,7 @@
         for d in ds[1:]:
             total = total + d
         rel_ref[g] += total
-        k, hk = part(own_ref, 1, g), part(halo_ref, 1, g)
+        k, hk = part(k_ref, 0, g), part(hk_ref, 0, g)
         for b in bands:
             rows = geo.unstacked(dot((ds[b] * scale).astype(BF16), geo.block(k, hk, b)))
             dq_ref[0, at[b], g * geo.lanes : (g + 1) * geo.lanes] = rows.astype(BF16)
@@ -696,7 +745,9 @@
         functools.partial(query_grad_body, geo),
         out_shape=(dq, table),
         grid=(geo.pages,),
-        in_specs=[by_page(a) for a in (probs, own, halo, gmx)]
+        in_specs=[by_page(probs)]
+        + [part_of(a, i, geo.width) for a in (own, halo) for i in (1, 2)]
+        + [by_page(gmx)]
         + [hold(a.shape) for a in (hm, sm, fold)],
         out_specs=[by_page(dq), hold(table.shape)],
         scratch_shapes=[pltpu.VMEM((geo.groups, geo.stack * geo.band, geo.slots), F32)],
@@ -705,11 +756,11 @@
             flops=2 * mm, transcendentals=0, bytes_accessed=20 * MIB
         ),
         name="query_grad",
-    )(probs, own, halo, gmx, hm, sm, fold)
-
-
-def class_grad(geo, own_ref, halo_ref, gm_ref, hr_ref, hrf_ref, sa_ref, cb_ref, o_ref, acc):
-    page, d, at = pl.program_id(0), geo.width, geo.halo - 16
+    )(probs, own, own, halo, halo, gmx, hm, sm, fold)
+
+
+def class_grad(geo, own_ref, cls_ref, gm_ref, hr_ref, hrf_ref, sa_ref, cb_ref, o_ref, acc):
+    page, d = pl.program_id(0), geo.width
 
     @pl.when(page == 0)
     def _():
@@ -718,8 +769,8 @@
     scale = 1.0 / math.sqrt(geo.head)
     hr, hrf, sa = hr_ref[...], hrf_ref[...], sa_ref[...]
     q, gm, st = own_ref[0, :, 0:d], gm_ref[0, :, 0:d], gm_ref[0, :, d:]
-    kc = jnp.broadcast_to(halo_ref[0, at : at + 1, d : 2 * d] * BF16(scale), (16, d)) * hr
-    vc = jnp.broadcast_to(halo_ref[0, at : at + 1, 2 * d : 3 * d], (16, d)) * hr
+    kc = jnp.broadcast_to(cls_ref[0, 0:1, d : 2 * d] * BF16(scale), (16, d)) * hr
+    vc = jnp.broadcast_to(cls_ref[0, 0:1, 2 * d : 3 * d], (16, d)) * hr
     prob = jnp.exp(dot_t(kc, q) + dot_t(sa[0:16], st) + cb_ref[...])
     ds = prob * (dot_t(vc, gm) + dot_t(sa[16:32], st))
     row = pl.ds(page, 1)
@@ -734,7 +785,7 @@
 
 
 def key_grad_body(
-    geo, own_ref, halo_ref, gm_ref, top_ref, bottom_ref, left_ref, right_ref,
+    geo, own_ref, hq_ref, cls_ref, gm_ref, top_ref, bottom_ref, left_ref, right_ref,
     bias_ref, ok_ref, hm_ref, sa_ref, flank_ref, hr_ref, hrf_ref, cb_ref, dk_ref, dv_ref, c_ref,
     hgm, rowstat, acc,
 ):
@@ -768,7 +819,7 @@
 
     def first(g):
         q, k, v = (part(own_ref, i, g) for i in range(3))
-        hq, gm = part(halo_ref, 0, g), part(gm_ref, 0, g)
+        hq, gm = part(hq_ref, 0, g), part(gm_ref, 0, g)
         hg = hgm[:, g * geo.lanes : (g + 1) * geo.lanes]
         qb = [geo.block(q, hq, b) for b in bands]
         gb = [geo.block(gm, hg, b) for b in bands]
@@ -776,7 +827,7 @@
         dp = [dot_t(geo.stacked(v[at[b]], hm), gb[b]) for b in bands]
         return qb, gb, s, dp
 
-    class_grad(geo, own_ref, halo_ref, gm_ref, hr_ref, hrf_ref, sa_ref, cb_ref, c_ref, acc)
+    class_grad(geo, own_ref, cls_ref, gm_ref, hr_ref, hrf_ref, sa_ref, cb_ref, c_ref, acc)
     now = first(0)
     for g in range(geo.groups):
         qb, gb, s, dp = now
@@ -798,7 +849,8 @@
         functools.partial(key_grad_body, geo),
         out_shape=(out, out, jax.ShapeDtypeStruct((16, 2 * geo.width), BF16)),
         grid=(geo.pages,),
-        in_specs=[by_page(a) for a in (own, halo, gmx) + pieces]
+        in_specs=[by_page(own), part_of(halo, 0, geo.width), part_of(halo, 0, 3 * geo.width, 16)]
+        + [by_page(a) for a in (gmx,) + pieces]
         + [hold(a.shape) for a in whole],
         out_specs=[by_page(out)] * 2 + [hold((16, 2 * geo.width))],
         scratch_shapes=[
@@ -811,7 +863,7 @@
             flops=4 * mm, transcendentals=geo.pages * G * geo.bands * 65536, bytes_accessed=20 * MIB
         ),
         name="key_grad",
-    )(own, halo, gmx, *pieces, *whole)
+    )(own, halo, halo, gmx, *pieces, *whole)
 
 
 def class_close_body(
@@ -859,7 +911,7 @@
 
     @pl.when(step == pl.num_programs(0) - 1)
     def _():
-        out_ref[...] = (res[...] + row(8) * (acc[...] + row(7))).astype(BF16)
+        out_ref[...] = (res[...] + row(8) * (acc[...] + row(7))).astype(BF16)[0:pages]
 
 
 def class_close_call(geo, mine, parts, halo, x, to_head, w_out, vec, w_up, w_down):
@@ -867,7 +919,7 @@
     ff = w_up.shape[1]
     return pl.pallas_call(
         functools.partial(class_close_body, geo),
-        out_shape=jax.ShapeDtypeStruct((16, d), BF16),
+        out_shape=jax.ShapeDtypeStruct((geo.pages, d), BF16),
         grid=(ff // d,),
         in_specs=[pl.BlockSpec(memory_space=pltpu.SMEM)]
         + [
@@ -879,7 +931,7 @@
             pl.BlockSpec((d, d), lambda c: (0, c)),
             pl.BlockSpec((d, d), lambda c: (c, 0)),
         ],
-        out_specs=full((16, d)),
+        out_specs=full((geo.pages, d)),
         scratch_shapes=[
             pltpu.VMEM((16, d), F32),
             pltpu.VMEM((16, d), BF16),
@@ -908,13 +960,20 @@
 
 def early_weight_body(
     tile, cols, at_ref, x_ref, att_ref, dq_ref, gb_ref, vec_ref, keep_ref, send_ref, nt_ref, sum_ref,
-    left, grad,
+    left, grad, att, gb, sems,
 ):
     step = pl.program_id(0)
     n, d = x_ref.shape
+    copies = (
+        pltpu.make_async_copy(att_ref, att, sems.at[0]),
+        pltpu.make_async_copy(gb_ref, gb, sems.at[1]),
+    )
 
     @pl.when(step == 0)
     def _():
+        for copy in copies:
+            copy.start()
+
         def one(t, carry):
             rows = pl.ds(pl.multiple_of(t * tile, tile), tile)
             unit, _ = norm_parts(unmask(x_ref[rows, :].astype(F32), vec_ref[0:1]))
@@ -930,33 +989,38 @@
 
     @pl.when(step == 1)
     def _():
-        left[...] = att_ref[...].T
-        grad[...] = gb_ref[...]
+        for copy in copies:
+            copy.wait()
+        left[...] = att[...].T
+        grad[...] = gb[...]
 
     dw = dot(left[...], grad[...]).astype(BF16)
     by_place(dw, cols, at_ref[0], at_ref[1], at_ref[2], keep_ref, send_ref)
 
 
 def late_weight_body(
-    cols, at_ref, nt_ref, dk_ref, dv_ref, c_ref, cg_ref, vec_ref, keep_ref, send_ref, sum_ref, grad
+    cols, at_ref, nt_ref, dk_ref, dv_ref, c_ref, cg_ref, vec_ref, keep_ref, send_ref, sum_ref, grad,
+    sem,
 ):
     step = pl.program_id(0)
+    copy = pltpu.make_async_copy(dv_ref, grad.at[1], sem)
     extra = cg_ref[...]
 
     @pl.when(step == 0)
     def _():
-        grad[...] = dk_ref[...]
+        copy.start()
+        grad[0] = dk_ref[...]
 
     @pl.when(step == 1)
     def _():
-        grad[...] = dv_ref[...]
-        total = jnp.sum(dv_ref[...].astype(F32), axis=0, keepdims=True)
+        copy.wait()
+        total = jnp.sum(grad[1].astype(F32), axis=0, keepdims=True)
         total = total + jnp.sum(extra.astype(F32), axis=0, keepdims=True)
         sum_ref[...] = jnp.broadcast_to(total, sum_ref.shape)
 
     unit, _ = norm_parts(c_ref[...].astype(F32))
     left = (unit * vec_ref[1:2] + vec_ref[2:3]).astype(BF16)
-    dw = (dot(nt_ref[...], grad[...]) + dot_0(left, extra)).astype(BF16)
+    dw = (dot(nt_ref[...], grad[step]) + dot_0(left, extra)).astype(BF16)
     by_place(dw, cols, at_ref[0], at_ref[1], at_ref[2], keep_ref, send_ref)
 
 
@@ -986,10 +1050,12 @@
     n, d = x.shape
     return weight_call(
         functools.partial(early_weight_body, tile, cols), where, cols, (x, att, dq, gb, vec),
-        [hold(a.shape) for a in (x, att, dq, gb, vec)], n, d,
+        [hold(x.shape), ANYWHERE, hold(dq.shape), ANYWHERE, hold(vec.shape)], n, d,
         (jax.ShapeDtypeStruct((d, n), BF16), jax.ShapeDtypeStruct((8, d), F32)),
         [hold((d, n)), hold((8, d))],
-        [pltpu.VMEM((d, n), BF16), pltpu.VMEM((n, d), BF16)],
+        [pltpu.VMEM((d, n), BF16)]
+        + [pltpu.VMEM((n, d), BF16)] * 3
+        + [pltpu.SemaphoreType.DMA((2,))],
         "early_weight",
     )
 
@@ -999,48 +1065,59 @@
     ins = (nt, dk, dv, cls_rows)
     return weight_call(
         functools.partial(late_weight_body, cols), where, cols, ins + (cls_grad, vec),
-        [hold(a.shape) for a in ins]
+        [hold(nt.shape), hold(dk.shape), ANYWHERE, hold(cls_rows.shape)]
         + [pl.BlockSpec((16, d), lambda i, p: (0, i)), hold(vec.shape)],
         n, d, (jax.ShapeDtypeStruct((8, d), F32),), [hold((8, d))],
-        [pltpu.VMEM((n, d), BF16)],
+        [pltpu.VMEM((2, n, d), BF16), pltpu.SemaphoreType.DMA(())],
         "late_weight",
     )
 
 
-def fold_body(cols, at_ref, k1_ref, r1_ref, k2_ref, r2_ref, own_ref, x_ref, y_ref, far_ref):
+def fold_body(
+    cols, at_ref, k1_ref, r1_ref, k2_ref, r2_ref, own_ref, to_x_ref, to_y_ref, held_x_ref, held_y_ref
+):
     d = k1_ref.shape[2] // 2
     add = lambda a, b, lo, hi: (a[:, :, lo:hi].astype(F32) + b[:, :, lo:hi].astype(F32)).astype(BF16)
     one = lambda lo, hi: add(k1_ref, r1_ref, lo, hi)
     two = lambda lo, hi: add(k2_ref, r2_ref, lo, hi)
-    h = d // 2
+    h, n = d // 2, cols // 2
     for page in range(2):
 
         @pl.when(at_ref[3] == page)
         def _():
-            for near, far, half in ((own_ref, y_ref, page), (x_ref, far_ref, 1 - page)):
-                if half == 0:
+            for mine in (True, False):
+                if (page == 0) == mine:
                     parts = ((one(0, d), 0), (two(0, h), d), (one(d, d + h), d + h))
                 else:
                     parts = ((two(h, 2 * d), 0), (one(d + h, 2 * d), d + h))
                 for value, lo in parts:
-                    hi = lo + value.shape[2]
-                    near[:, :, lo:hi] = value[:cols]
-                    far[:, :, lo:hi] = value[cols:]
+                    at = slice(lo, lo + value.shape[2])
+                    near, far = value[:cols], value[cols:]
+                    if mine:
+                        own_ref[:, :, at] = near
+                        to_y_ref[:n, :, at] = far[:n]
+                        held_y_ref[:, :, at] = far[n:]
+                    else:
+                        held_x_ref[:, :, at] = near[:n]
+                        to_x_ref[:n, :, at] = near[n:]
+                        to_y_ref[n:, :, at] = far[:n]
+                        to_x_ref[n:, :, at] = far[n:]
 
 
 def fold_call(where, cols, keep1, got1, keep2, got2):
     _, slab, d2 = keep1.shape
-    out = jax.ShapeDtypeStruct((cols, slab, d2), BF16)
+    out = lambda k: jax.ShapeDtypeStruct((k, slab, d2), BF16)
+    sizes = (cols, cols, cols, cols // 2, cols // 2)
     rows = slab // 3
     spec = lambda k: pl.BlockSpec((k, rows, d2), lambda i, p: (0, i, 0))
     return pl.pallas_call(
         functools.partial(fold_body, cols),
-        out_shape=(out,) * 4,
+        out_shape=tuple(out(k) for k in sizes),
         grid_spec=pltpu.PrefetchScalarGridSpec(
             num_scalar_prefetch=1,
             grid=(3,),
             in_specs=[spec(2 * cols)] * 4,
-            out_specs=[spec(cols)] * 4,
+            out_specs=[spec(k) for k in sizes],
         ),
         compiler_params=params(LESS),
         name="fold",
@@ -1117,11 +1194,14 @@
     return lax.ppermute(value, axis, [(i, i ^ bit) for i in range(lax.axis_size(axis))])
 
 
-def halo_pieces(geo, x):
+def halo_pieces(geo, x, filler):
     top = passed_along(x[:, geo.own - geo.edge :], "row", 1)
     bottom = passed_along(x[:, : geo.edge], "row", -1)
+    if filler is not None:
+        top, bottom, filler = join((top, bottom, filler))
     to_right, to_left = strips_call(geo, x, top, bottom)
-    return top, bottom, passed_along(to_right, "col", 1), passed_along(to_left, "col", -1)
+    pieces = top, bottom, passed_along(to_right, "col", 1), passed_along(to_left, "col", -1)
+    return pieces, filler
 
 
 def page_sum(part, by):
@@ -1170,7 +1250,7 @@
 
     masked = (patch_mask == 1)[..., None]
     x = jnp.where(masked, jnp.asarray(FLAG, BF16), tokens).reshape(pages, geo.own, width)
-    pieces = halo_pieces(geo, x)
+    pieces, _ = halo_pieces(geo, x, None)
     bias_a = bias_table(geo, rel_table, 0)
     own = qkv_call(qkv_own_body, geo.own, (x,), (w_qkv, vec), "qkv_own")
     first = np.arange(16)[:, None] == 0
@@ -1188,8 +1268,8 @@
     )
     d_mlp = lax.psum_scatter(d_mlp, ("row", "col"), scatter_dimension=0, tiled=True)[0]
     gmx = gmx.reshape(pages, geo.own, width + LANES)
-    pieces = halo_pieces(geo, gmx)
-    bias_b = bias_table(geo, rel_table, 1)
+    rel_late, _ = join((rel_table, gb))
+    pieces, bias_b = halo_pieces(geo, gmx, bias_table(geo, rel_late, 1))
     dq, d_table = query_grad_call(geo, probs, own, halo, gmx, hm, sm)
     class_bias = jnp.concatenate([rel_table[:, SPAN * SPAN], jnp.zeros((16 - heads,), F32)])
     class_bias = jnp.broadcast_to(class_bias[:, None], (16, geo.own))
@@ -1212,24 +1292,25 @@
     wide = lambda a: a.astype(F32)
     if direct:
         got2 = swap(send2, "row", 1)
-        mine, to_x, to_y, to_far = fold_call(where, col_peers, keep1, got1, keep2, got2)
+        mine, to_x, to_y, held_x, held_y = fold_call(where, col_peers, keep1, got1, keep2, got2)
         mine, dq = join((mine, dq))
         near_x = swap(to_x, "dp", 1)
         near_y = swap(to_y, "row", 2)
-        far = lax.ppermute(
-            to_far,
-            ("dp", "row"),
-            [(4 * i + j, 4 * (i ^ 1) + (j ^ 2)) for i in range(2) for j in range(4)],
-        )
     d_tok, block = token_grad_call(
         pages, heads, (x, dq, dk, dv, gres),
         (w_qkv, cls_rows, cls_low, vec, cls_part, vg_mlp, d_upb, d_table, sum_q, sum_v),
     )
     slab = width // (row_peers * col_peers)
     if direct:
-        near_x, near_y, far, block = join((near_x, near_y, far, block))
-        late = (wide(mine) + wide(near_x) + wide(near_y) + wide(far)).astype(BF16)
-        beside = [swap(late[step], "col", step) for step in range(1, col_peers)]
+        near_x, near_y, block = join((near_x, near_y, block))
+        n = col_peers // 2
+        last_x = swap((wide(held_x) + wide(near_y[n:])).astype(BF16), "dp", 1)
+        last_y = swap((wide(held_y) + wide(near_x[n:])).astype(BF16), "row", 2)
+        late = [
+            (wide(mine[:n]) + wide(near_y[:n]) + wide(last_x)).astype(BF16),
+            (wide(mine[n:]) + wide(near_x[:n]) + wide(last_y)).astype(BF16),
+        ]
+        late = [a[i] for a in late for i in range(n)]
         up, down = d_mlp[: ups * slab], d_mlp[ups * slab :]
         cut_up, cut_down = ups * slab // 2, width // 2
 
@@ -1252,6 +1333,9 @@
     sent = block
     for axis in ("col", "row"):
         peers, rows_in = lax.axis_size(axis), parts.shape[0]
+        if direct and axis == "row":
+            sent, *late = join((sent, *late))
+            beside = [swap(late[step], "col", step) for step in range(1, col_peers)]
         got = [swap(sent, axis, bit) for bit in range(1, peers)]
         level = [vectors] + [g[rows_in:] for g in got]
         while len(level) > 1:
@@ -1262,6 +1346,8 @@
         place = place * peers
         sent = jnp.concatenate([parts, vectors], axis=0)
 
+    if direct:
+        beside, parts = join((beside, parts))
     d_cls, v = vectors[:pages], vectors[pages:]
     bit = 1
     while bit < lax.axis_size("dp"):
@@ -1269,11 +1355,11 @@
     out_cls = class_close_call(
         geo, mine_at[None], parts.reshape(-1, 2 * pages, width), halo, cls_rows, to_head, w_out, vec, w_up,
         w_down,
-    )[:pages]
+    )
 
     half = 3 * width // 2
     if direct:
-        beside, other, v, out_cls = join((beside, other, v, out_cls))
+        other, v, out_cls = join((other, v, out_cls))
         late = wide(late[0])
         for part in beside:
             late = late + wide(part)

time: 285 us -> 272 us (0.954)
  waiting for transfers between devices: 34.9 us -> 28.7 us
  Pallas kernels: 163 us -> 159 us
    ppermute x15 -> x17, waiting for transfers between devices: 32.3 us -> 26.2 us  [swap(): lax.ppermute(value, axis, [(i, i ^ bit) for i in range(lax.axis_size(axis...]
    ppermute x15 -> x17, starting transfers between devices: 21.3 us -> 23.8 us  [swap(): lax.ppermute(value, axis, [(i, i ^ bit) for i in range(lax.axis_size(axis...]
  transfers between devices with their start and end apart: 25 -> 26, of which waited for: 6 -> 8; matrix products, arithmetic and copies ran while one was open for 4% -> 4% of each run, Pallas kernels for 32% -> 32%
where the time goes in v1:
time: 272 us; the launch traced here: 271 us
  Pallas kernels  159 us (58%)
  starting transfers between devices  45.9 us (17%)
  waiting for transfers between devices  28.7 us (11%)
  local copies, waits for them, and re-layouts  16.4 us (6%)
  between operations  14.9 us (5%)
  other arithmetic  6.38 us (2%)
    pallas_call x1, Pallas kernels, mlp_call(): pl.pallas_call(functools.partial(mlp_body, tile, steps), out_shape=(jax.S...  47.4 us
    ppermute x17, waiting for transfers between devices, swap(): lax.ppermute(value, axis, [(i, i ^ bit) for i in range(lax.axis_size(axis...  26.2 us
    ppermute x17, starting transfers between devices, swap(): lax.ppermute(value, axis, [(i, i ^ bit) for i in range(lax.axis_size(axis...  23.8 us
    ppermute x8, starting transfers between devices, passed_along(): lax.ppermute(value, axis, [(i, i + steps) for i in range(first, last)])  22 us
    pallas_call x2, Pallas kernels, weight_call(): pl.pallas_call(body, out_shape=(out, out) + more, grid_spec=pltpu.Prefetc...  18.9 us
    pallas_call x2, Pallas kernels, qkv_call(): pl.pallas_call(body, out_shape=jax.ShapeDtypeStruct((pages, rows, 3 * d),...  17.9 us
    pallas_call x1, Pallas kernels, key_grad_call(): pl.pallas_call(functools.partial(key_grad_body, geo), out_shape=(out, out...  16.2 us
    pallas_call x1, Pallas kernels, token_grad_call(): pl.pallas_call(functools.partial(token_grad_body, pages, heads), out_shap...  12.4 us
  transfers between devices with their start and end apart: 26, of which 8 were waited for; matrix products, arithmetic and copies ran while one was open for 4% of the time, Pallas kernels for 32%

profile of v1, /device:TPU:0, one launch (start us, length us, event | category | flops | bytes accessed | tf_op | source)
XLA Modules:
  0.0 271.0 jit_solution(4178562758426807117)
XLA Ops:
  8.2 3.0 %broadcast_select_fusion = (bf16[4,16,16,768]{3,2,1,0:T(8,128)(2,1)}, bf16[4,16,16,768]{3,2,1,0:T(8,128)(2,1)S(1)}) fusion(bf16[4,16,16,768]{3,2,1,0:T(8,128)(2,1)} %param.58, pred[4,16,16]{2,1,0:T(8,128)(4,1)S(1)} %get-tuple-element.184, bf16[4,16,16,768]{3,2,1,0:T(8,128)(2,1)} %param.37, pred[4,16,16]{2,1,0:T(8,128)(4,1)S(1)} %get-tuple-element.185), kind=kLoop, calls=%fused_computation | loop fusion | flops 1572864 | bytes 6293504 | tf_op jit(solution)/shard_map/jit(_where)/select_n | solution.py:1265
  11.3 2.4 collective-permute-start
  16.7 2.5 collective-permute-done.1.bottom_ref
  20.0 3.3 %strips.2 = (bf16[4,72,768]{2,1,0:T(8,128)(2,1)}, bf16[4,72,768]{2,1,0:T(8,128)(2,1)}) custom-call(bf16[4,256,768]{2,1,0:T(8,128)(2,1)} %bitcast.42, bf16[4,48,768]{2,1,0:T(8,128)(2,1)} %copy-done.7, bf16[4,48,768]{2,1,0:T(8,128)(2,1)} %copy-done.8), custom_call_target="tpu_custom_call" | custom-call | tf_op jit(solution)/shard_map/strips/pallas_call | solution.py:324
  23.3 3.5 %collective-permute-start.2 = (bf16[4,72,768]{2,1,0:T(8,128)(2,1)}, bf16[4,72,768]{2,1,0:T(8,128)(2,1)S(1)}, u32[]{:S(2)}, u32[]{:S(2)}) collective-permute-start(bf16[4,72,768]{2,1,0:T(8,128)(2,1)} %get-tuple-element.82), channel_id=1, source_target_pairs={{0,1},{1,2},{2,3},{4,5},{5,6},{6,7},{8,9},{9,10},{10,11},{12,13},{... | collective-permute-start | bytes 1327112 | tf_op jit(solution)/shard_map/ppermute | solution.py:1190
  28.7 3.0 %bias_table.2.bias_ref = f32[3,256,256]{2,1,0:T(8,128)} custom-call(f32[12,50]{1,0:T(8,128)} %table.2, s32[16,256]{1,0:T(8,128)} %constant.116.clone.index_ref), custom_call_target="tpu_custom_call" | custom-call | tf_op jit(solution)/shard_map/bias_table/pallas_call | solution.py:229
  31.7 8.2 %qkv_own.1.own_ref.k_ref.v_ref = bf16[4,256,2304]{2,1,0:T(8,128)(2,1)} custom-call(bf16[4,256,768]{2,1,0:T(8,128)(2,1)} %bitcast.43, bf16[768,2304]{1,0:T(8,128)(2,1)} %w_ref.5, f32[16,768]{1,0:T(8,128)} %reshape.110.vec_ref), custom_call_target="tpu_custom_call" | custom-call | flops 3623878656 | bytes 9830400 | tf_op jit(solution)/shard_map/qkv_own/pallas_call | solution.py:288
  41.5 9.7 %qkv_halo.1.hk_ref.hv_ref.cq_ref.hq_ref.cls_ref = bf16[4,288,2304]{2,1,0:T(8,128)(2,1)} custom-call(bf16[4,48,768]{2,1,0:T(8,128)(2,1)} %copy-done.7, bf16[4,48,768]{2,1,0:T(8,128)(2,1)} %copy-done.8, bf16[4,72,768]{2,1,0:T(8,128)(2,1)} %copy-done.30, bf16[4,72,768]{2,1,0:T(8,128)(2,1)} %copy-done.31, bf16[4,16,768]{2,1,0:T(8,128)(2,1)} %broadcast_select_fusion.2.last_ref, ...), custom_call_target="tpu_custom_call" | custom-call | flops 4076863488 | bytes 10616832 | tf_op jit(solution)/shard_map/qkv_halo/pallas_call | solution.py:288
  51.2 11.5 %attend.1 = (bf16[4,256,768]{2,1,0:T(8,128)(2,1)}, f32[4,256,128]{2,1,0:T(8,128)}, bf16[4,3,4,256,256]{4,3,2,1,0:T(8,128)(2,1)}, f32[8,768]{1,0:T(8,128)}) custom-call(bf16[4,256,2304]{2,1,0:T(8,128)(2,1)} %qkv_own.1.own_ref.k_ref.v_ref, bf16[4,288,2304]{2,1,0:T(8,128)(2,1)} %qkv_halo.1.hk_ref.hv_ref.cq_ref.hq_ref.cls_ref, ...), custom_call_target="tpu_custom_call" | custom-call | flops 3221225472 | bytes 16777216 | tf_op jit(solution)/shard_map/attend/pallas_call | solution.py:425
  62.7 47.4 %mlp.1 = (bf16[1024,768]{1,0:T(8,128)(2,1)}, bf16[1024,896]{1,0:T(8,128)(2,1)}, f32[1024,768]{1,0:T(8,128)}, bf16[1024,768]{1,0:T(8,128)(2,1)}, bf16[16,384,768]...) custom-call(bf16[1024,768]{1,0:T(8,128)(2,1)} %bitcast.52, bf16[1024,768]{1,0:T(8,128)(2,1)} %bitcast.44, ...), custom_call_target="tpu_custom_call" | custom-call | flops 31406948352 | bytes 31457280 | tf_op jit(solution)/shard_map/mlp/pallas_call | solution.py:612
  111.3 6.7 %collective-permute-start.6 = (bf16[4,48,896]{2,1,0:T(8,128)(2,1)S(1)}, bf16[4,48,896]{2,1,0:T(8,128)(2,1)S(1)}, u32[]{:S(2)}, u32[]{:S(2)}) collective-permute-start(bf16[4,48,896]{2,1,0:T(8,128)(2,1)S(1)} %get-tuple-element.159), channel_id=1, source_target_pairs={{0,4},{4,8},{8,12},{1,5},{5,9},{9,13},{2,6},{6,10},{10,14},{3,7},{... | collective-permute-start | bytes 1032200 | tf_op jit(solution)/shard_map/ppermute | solution.py:1190
  120.7 3.0 %bias_table.3.bias_ref = f32[3,256,256]{2,1,0:T(8,128)} custom-call(f32[12,50]{1,0:T(8,128)} %table.2, s32[16,256]{1,0:T(8,128)} %constant.118.clone.index_ref), custom_call_target="tpu_custom_call" | custom-call | tf_op jit(solution)/shard_map/bias_table/pallas_call | solution.py:229
  125.2 3.9 %strips.3 = (bf16[4,72,896]{2,1,0:T(8,128)(2,1)}, bf16[4,72,896]{2,1,0:T(8,128)(2,1)}) custom-call(bf16[4,256,896]{2,1,0:T(8,128)(2,1)} %bitcast.38, bf16[4,48,896]{2,1,0:T(8,128)(2,1)} %copy-done.5, bf16[4,48,896]{2,1,0:T(8,128)(2,1)} %copy-done.6), custom_call_target="tpu_custom_call" | custom-call | tf_op jit(solution)/shard_map/strips/pallas_call | solution.py:324
  129.1 4.3 %collective-permute-start.8 = (bf16[4,72,896]{2,1,0:T(8,128)(2,1)}, bf16[4,72,896]{2,1,0:T(8,128)(2,1)S(1)}, u32[]{:S(2)}, u32[]{:S(2)}) collective-permute-start(bf16[4,72,896]{2,1,0:T(8,128)(2,1)} %get-tuple-element.97), channel_id=1, source_target_pairs={{0,1},{1,2},{2,3},{4,5},{5,6},{6,7},{8,9},{9,10},{10,11},{12,13},{... | collective-permute-start | bytes 1548296 | tf_op jit(solution)/shard_map/ppermute | solution.py:1190
  134.7 12.0 %query_grad.1 = (bf16[4,256,768]{2,1,0:T(8,128)(2,1)}, f32[16,128]{1,0:T(8,128)}) custom-call(bf16[4,3,4,256,256]{4,3,2,1,0:T(8,128)(2,1)} %get-tuple-element.88.p_ref, bf16[4,256,2304]{2,1,0:T(8,128)(2,1)} %qkv_own.1.own_ref.k_ref.v_ref, bf16[4,256,2304]{2,1,0:T(8,128)(2,1)} %qkv_own.1.own_ref.k_ref.v_ref, ...), custom_call_target="tpu_custom_call" | custom-call | flops 3221225472 | bytes 20971520 | tf_op jit(solution)/shard_map/query_grad/pallas_call | solution.py:744
  146.7 10.6 %early_weight.1 = (bf16[8,48,1536]{2,1,0:T(8,128)(2,1)}, bf16[8,48,1536]{2,1,0:T(8,128)(2,1)}, bf16[768,1024]{1,0:T(8,128)(2,1)}, f32[8,768]{1,0:T(8,128)}) custom-call(s32[4]{0:T(128)} %pad_add_fusion.at_ref, bf16[1024,768]{1,0:T(8,128)(2,1)} %bitcast.45, bf16[1024,768]{1,0:T(8,128)(2,1)} %bitcast.53, bf16[1024,768]{1,0:T(8,128)(2,1)} %bitcast.54, ...), custom_call_target="tpu_custom_call" | custom-call | flops 2415919104 | bytes 10223616 | tf_op jit(solution)/shard_map/early_weight/pallas_call | solution.py:1031
  159.7 16.2 %key_grad.1 = (bf16[4,256,768]{2,1,0:T(8,128)(2,1)}, bf16[4,256,768]{2,1,0:T(8,128)(2,1)}, bf16[16,1536]{1,0:T(8,128)(2,1)}) custom-call(bf16[4,256,2304]{2,1,0:T(8,128)(2,1)} %qkv_own.1.own_ref.k_ref.v_ref, bf16[4,288,2304]{2,1,0:T(8,128)(2,1)} %qkv_halo.1.hk_ref.hv_ref.cq_ref.hq_ref.cls_ref, ...), custom_call_target="tpu_custom_call" | custom-call | flops 6442450944 | bytes 20971520 | tf_op jit(solution)/shard_map/key_grad/pallas_call | solution.py:848
  176.0 8.3 %late_weight.1 = (bf16[8,48,1536]{2,1,0:T(8,128)(2,1)}, bf16[8,48,1536]{2,1,0:T(8,128)(2,1)}, f32[8,768]{1,0:T(8,128)}) custom-call(s32[4]{0:T(128)} %pad_add_fusion.at_ref, bf16[768,1024]{1,0:T(8,128)(2,1)} %get-tuple-element.101.nt_ref, bf16[1024,768]{1,0:T(8,128)(2,1)} %bitcast.59, bf16[1024,768]{1,0:T(8,128)(2,1)} %bitcast.61, ...), custom_call_target="tpu_custom_call" | custom-call | flops 2415919104 | bytes 10223616 | tf_op jit(solution)/shard_map/late_weight/pallas_call | solution.py:1031
  184.4 3.0 %collective-permute-done.10.r2_ref = bf16[8,48,1536]{2,1,0:T(8,128)(2,1)S(1)} collective-permute-done((bf16[8,48,1536]{2,1,0:T(8,128)(2,1)}, bf16[8,48,1536]{2,1,0:T(8,128)(2,1)S(1)}, u32[]{:S(2)}, u32[]{:S(2)}) %collective-permute-start.10) | collective-permute-done | bytes 1179680 | tf_op jit(solution)/shard_map/ppermute | solution.py:1194
  188.8 1.7 fold.1
  190.5 1.6 collective-permute-start.11
  192.9 12.4 %token_grad.1 = (f32[1024,768]{1,0:T(8,128)}, f32[32,768]{1,0:T(8,128)}) custom-call(bf16[1024,768]{1,0:T(8,128)(2,1)} %bitcast.46, bf16[1024,768]{1,0:T(8,128)(2,1)} %bitcast.55, bf16[1024,768]{1,0:T(8,128)(2,1)} %bitcast.60, bf16[1024,768]{1,0:T(8,128)(2,1)} %bitcast.62, f32[1024,768]{1,0:T(8,128)} %get-tuple-element.116.gres_ref, ...), custom_call_target="tpu_custom_call" | custom-call | flops 3623878656 | bytes 16121856 | tf_op jit(solution)/shard_map/token_grad/pallas_call | solution.py:1173
  205.9 2.6 collective-permute-done.12
  209.3 2.7 collective-permute-start.14
  214.3 1.5 collective-permute-start.16
  215.8 4.5 %collective-permute-done.13 = f32[32,768]{1,0:T(8,128)S(1)} collective-permute-done((f32[32,768]{1,0:T(8,128)}, f32[32,768]{1,0:T(8,128)S(1)}, u32[]{:S(2)}, u32[]{:S(2)}) %collective-permute-start.13) | collective-permute-done | bytes 98336 | tf_op jit(solution)/shard_map/ppermute | solution.py:1194
  220.3 5.1 %collective-permute-done.14 = f32[32,768]{1,0:T(8,128)S(1)} collective-permute-done((f32[32,768]{1,0:T(8,128)}, f32[32,768]{1,0:T(8,128)S(1)}, u32[]{:S(2)}, u32[]{:S(2)}) %collective-permute-start.14) | collective-permute-done | bytes 98336 | tf_op jit(solution)/shard_map/ppermute | solution.py:1194
  227.7 7.7 %collective-permute-start.22 = (bf16[48,1536]{1,0:T(8,128)(2,1)S(1)}, bf16[48,1536]{1,0:T(8,128)(2,1)S(1)}, u32[]{:S(2)}, u32[]{:S(2)}) collective-permute-start(bf16[48,1536]{1,0:T(8,128)(2,1)S(1)} %get-tuple-element.131), channel_id=1, source_target_pairs={{0,1},{1,0},{2,3},{3,2},{4,5},{5,4},{6,7},{7,6},{8,9},{9,8},{10,11... | collective-permute-start | bytes 442376 | tf_op jit(solution)/shard_map/ppermute | solution.py:1194
  235.8 2.1 collective-permute-start.24
  238.8 3.5 %collective-permute-done.22 = bf16[48,1536]{1,0:T(8,128)(2,1)S(1)} collective-permute-done((bf16[48,1536]{1,0:T(8,128)(2,1)S(1)}, bf16[48,1536]{1,0:T(8,128)(2,1)S(1)}, u32[]{:S(2)}, u32[]{:S(2)}) %collective-permute-start.22) | collective-permute-done | bytes 147488 | tf_op jit(solution)/shard_map/ppermute | solution.py:1194
  242.3 6.8 %collective-permute-done.23 = bf16[48,1536]{1,0:T(8,128)(2,1)S(1)} collective-permute-done((bf16[48,1536]{1,0:T(8,128)(2,1)S(1)}, bf16[48,1536]{1,0:T(8,128)(2,1)S(1)}, u32[]{:S(2)}, u32[]{:S(2)}) %collective-permute-start.23) | collective-permute-done | bytes 147488 | tf_op jit(solution)/shard_map/ppermute | solution.py:1194
  253.0 7.5 %class_close.1 = bf16[4,768]{1,0:T(4,128)(2,1)} custom-call(s32[1]{0:T(128)} %bitcast.20.mine_ref, f32[16,8,768]{2,1,0:T(8,128)} %bitcast.49, bf16[4,288,2304]{2,1,0:T(8,128)(2,1)} %qkv_halo.1.hk_ref.hv_ref.cq_ref.hq_ref.cls_ref, bf16[16,768]{1,0:T(8,128)(2,1)} %concatenate.27.c_ref.x_ref, bf16[768,128]{1,0:T(8,128)(2,1)} %constant.110.clone.toh_ref, ...), custom_call_target="tpu_custom_call" | custom-call | flops 339738624 | bytes 12582912 | tf_op jit(solution)/shard_map/class_close/pallas_call | solution.py:920
  (165 shorter events, 33.9 us)
Async XLA Ops:
  7.2 241.9 %reduce-scatter.2.cloned.1.call-start = ((), (), s32[]{:S(2)}) async-start(), calls=%async_computation.1 | async-start | bytes 10027008 | tf_op jit(solution)/shard_map/reduce_scatter | solution.py:1269
  11.2 16.8 %copy-start.12 = (f32[3072]{0:T(1024)S(1)}, f32[3072]{0:T(1024)}, u32[]{:S(2)}) copy-start(f32[3072]{0:T(1024)} %param.54) | copy-start | bytes 36868
  11.3 5.4 %collective-permute-start = (bf16[4,48,768]{2,1,0:T(8,128)(2,1)S(1)}, bf16[4,48,768]{2,1,0:T(8,128)(2,1)S(1)}, u32[]{:S(2)}, u32[]{:S(2)}) collective-permute-start(bf16[4,48,768]{2,1,0:T(8,128)(2,1)S(1)} %get-tuple-element.161), channel_id=1, source_target_pairs={{0,4},{4,8},{8,12},{1,5},{5,9},{9,13},{2,6},{6,10},{10,14},{3,7},{... | collective-permute-start | bytes 884744 | tf_op jit(solution)/shard_map/ppermute | solution.py:1190
  13.7 5.6 %collective-permute-start.1 = (bf16[4,48,768]{2,1,0:T(8,128)(2,1)S(1)}, bf16[4,48,768]{2,1,0:T(8,128)(2,1)S(1)}, u32[]{:S(2)}, u32[]{:S(2)}) collective-permute-start(bf16[4,48,768]{2,1,0:T(8,128)(2,1)S(1)} %get-tuple-element.160), channel_id=1, source_target_pairs={{4,0},{8,4},{12,8},{5,1},{9,5},{13,9},{6,2},{10,6},{14,10},{7,3},{... | collective-permute-start | bytes 884744 | tf_op jit(solution)/shard_map/ppermute | solution.py:1190
  23.3 16.7 %collective-permute-start.2 = (bf16[4,72,768]{2,1,0:T(8,128)(2,1)}, bf16[4,72,768]{2,1,0:T(8,128)(2,1)S(1)}, u32[]{:S(2)}, u32[]{:S(2)}) collective-permute-start(bf16[4,72,768]{2,1,0:T(8,128)(2,1)} %get-tuple-element.82), channel_id=1, source_target_pairs={{0,1},{1,2},{2,3},{4,5},{5,6},{6,7},{8,9},{9,10},{10,11},{12,13},{... | collective-permute-start | bytes 1327112 | tf_op jit(solution)/shard_map/ppermute | solution.py:1190
  26.8 13.2 %collective-permute-start.3 = (bf16[4,72,768]{2,1,0:T(8,128)(2,1)}, bf16[4,72,768]{2,1,0:T(8,128)(2,1)S(1)}, u32[]{:S(2)}, u32[]{:S(2)}) collective-permute-start(bf16[4,72,768]{2,1,0:T(8,128)(2,1)} %get-tuple-element.83), channel_id=1, source_target_pairs={{1,0},{2,1},{3,2},{5,4},{6,5},{7,6},{9,8},{10,9},{11,10},{13,12},{... | collective-permute-start | bytes 1327112 | tf_op jit(solution)/shard_map/ppermute | solution.py:1190
  110.1 9.8 %copy-start.10 = (f32[12,50]{1,0:T(8,128)S(1)}, f32[12,50]{1,0:T(8,128)}, u32[]{:S(2)}) copy-start(f32[12,50]{1,0:T(8,128)} %table.2) | copy-start | bytes 7204
  111.3 12.5 %collective-permute-start.6 = (bf16[4,48,896]{2,1,0:T(8,128)(2,1)S(1)}, bf16[4,48,896]{2,1,0:T(8,128)(2,1)S(1)}, u32[]{:S(2)}, u32[]{:S(2)}) collective-permute-start(bf16[4,48,896]{2,1,0:T(8,128)(2,1)S(1)} %get-tuple-element.159), channel_id=1, source_target_pairs={{0,4},{4,8},{8,12},{1,5},{5,9},{9,13},{2,6},{6,10},{10,14},{3,7},{... | collective-permute-start | bytes 1032200 | tf_op jit(solution)/shard_map/ppermute | solution.py:1190
  118.0 5.8 %collective-permute-start.7 = (bf16[4,48,896]{2,1,0:T(8,128)(2,1)S(1)}, bf16[4,48,896]{2,1,0:T(8,128)(2,1)S(1)}, u32[]{:S(2)}, u32[]{:S(2)}) collective-permute-start(bf16[4,48,896]{2,1,0:T(8,128)(2,1)S(1)} %get-tuple-element.158), channel_id=1, source_target_pairs={{4,0},{8,4},{12,8},{5,1},{9,5},{13,9},{6,2},{10,6},{14,10},{7,3},{... | collective-permute-start | bytes 1032200 | tf_op jit(solution)/shard_map/ppermute | solution.py:1190
  129.1 29.5 %collective-permute-start.8 = (bf16[4,72,896]{2,1,0:T(8,128)(2,1)}, bf16[4,72,896]{2,1,0:T(8,128)(2,1)S(1)}, u32[]{:S(2)}, u32[]{:S(2)}) collective-permute-start(bf16[4,72,896]{2,1,0:T(8,128)(2,1)} %get-tuple-element.97), channel_id=1, source_target_pairs={{0,1},{1,2},{2,3},{4,5},{5,6},{6,7},{8,9},{9,10},{10,11},{12,13},{... | collective-permute-start | bytes 1548296 | tf_op jit(solution)/shard_map/ppermute | solution.py:1190
  133.4 25.3 %collective-permute-start.9 = (bf16[4,72,896]{2,1,0:T(8,128)(2,1)}, bf16[4,72,896]{2,1,0:T(8,128)(2,1)S(1)}, u32[]{:S(2)}, u32[]{:S(2)}) collective-permute-start(bf16[4,72,896]{2,1,0:T(8,128)(2,1)} %get-tuple-element.98), channel_id=1, source_target_pairs={{1,0},{2,1},{3,2},{5,4},{6,5},{7,6},{9,8},{10,9},{11,10},{13,12},{... | collective-permute-start | bytes 1548296 | tf_op jit(solution)/shard_map/ppermute | solution.py:1190
  157.3 27.1 %collective-permute-start.5 = (bf16[8,48,1536]{2,1,0:T(8,128)(2,1)}, bf16[8,48,1536]{2,1,0:T(8,128)(2,1)S(1)}, u32[]{:S(2)}, u32[]{:S(2)}) collective-permute-start(bf16[8,48,1536]{2,1,0:T(8,128)(2,1)} %get-tuple-element.93), channel_id=1, source_target_pairs={{0,4},{4,0},{8,12},{12,8},{1,5},{5,1},{9,13},{13,9},{2,6},{6,2},{1... | collective-permute-start | bytes 3538952 | tf_op jit(solution)/shard_map/ppermute | solution.py:1194
  176.0 11.5 %copy-start = (bf16[8,48,1536]{2,1,0:T(8,128)(2,1)S(1)}, bf16[8,48,1536]{2,1,0:T(8,128)(2,1)}, u32[]{:S(2)}) copy-start(bf16[8,48,1536]{2,1,0:T(8,128)(2,1)} %get-tuple-element.92.k1_ref) | copy-start | bytes 3538948
  176.0 11.5 %copy-start.2 = (s32[4]{0:T(128)S(1)}, s32[4]{0:T(128)}, u32[]{:S(2)}) copy-start(s32[4]{0:T(128)} %pad_add_fusion.at_ref) | copy-start | bytes 52
  184.3 3.1 %collective-permute-start.10 = (bf16[8,48,1536]{2,1,0:T(8,128)(2,1)}, bf16[8,48,1536]{2,1,0:T(8,128)(2,1)S(1)}, u32[]{:S(2)}, u32[]{:S(2)}) collective-permute-start(bf16[8,48,1536]{2,1,0:T(8,128)(2,1)} %get-tuple-element.111), channel_id=1, source_target_pairs={{0,4},{4,0},{8,12},{12,8},{1,5},{5,1},{9,13},{13,9},{2,6},{6,2},{1... | collective-permute-start | bytes 3538952 | tf_op jit(solution)/shard_map/ppermute | solution.py:1194
  190.5 15.4 %collective-permute-start.11 = (bf16[4,48,1536]{2,1,0:T(8,128)(2,1)S(1)}, bf16[4,48,1536]{2,1,0:T(8,128)(2,1)S(1)}, u32[]{:S(2)}, u32[]{:S(2)}) collective-permute-start(bf16[4,48,1536]{2,1,0:T(8,128)(2,1)S(1)} %get-tuple-element.112), channel_id=1, source_target_pairs={{0,16},{16,0},{1,17},{17,1},{2,18},{18,2},{3,19},{19,3},{4,20},{20... | collective-permute-start | bytes 1769480 | tf_op jit(solution)/shard_map/ppermute | solution.py:1194
  192.1 16.4 %collective-permute-start.12 = (bf16[4,48,1536]{2,1,0:T(8,128)(2,1)S(1)}, bf16[4,48,1536]{2,1,0:T(8,128)(2,1)S(1)}, u32[]{:S(2)}, u32[]{:S(2)}) collective-permute-start(bf16[4,48,1536]{2,1,0:T(8,128)(2,1)S(1)} %get-tuple-element.113), channel_id=1, source_target_pairs={{0,8},{4,12},{8,0},{12,4},{1,9},{5,13},{9,1},{13,5},{2,10},{6,14},... | collective-permute-start | bytes 1769480 | tf_op jit(solution)/shard_map/ppermute | solution.py:1194
  205.2 20.3 %copy-start.9 = (f32[32,768]{1,0:T(8,128)S(1)}, f32[32,768]{1,0:T(8,128)}, u32[]{:S(2)}) copy-start(f32[32,768]{1,0:T(8,128)} %get-tuple-element.124) | copy-start | bytes 294916
  208.5 11.9 %collective-permute-start.13 = (f32[32,768]{1,0:T(8,128)}, f32[32,768]{1,0:T(8,128)S(1)}, u32[]{:S(2)}, u32[]{:S(2)}) collective-permute-start(f32[32,768]{1,0:T(8,128)} %get-tuple-element.124), channel_id=1, source_target_pairs={{0,1},{1,0},{2,3},{3,2},{4,5},{5,4},{6,7},{7,6},{8,9},{9,8},{10,11... | collective-permute-start | bytes 294920 | tf_op jit(solution)/shard_map/ppermute | solution.py:1194
  209.3 16.2 %collective-permute-start.14 = (f32[32,768]{1,0:T(8,128)}, f32[32,768]{1,0:T(8,128)S(1)}, u32[]{:S(2)}, u32[]{:S(2)}) collective-permute-start(f32[32,768]{1,0:T(8,128)} %get-tuple-element.124), channel_id=1, source_target_pairs={{0,2},{1,3},{2,0},{3,1},{4,6},{5,7},{6,4},{7,5},{8,10},{9,11},{10,... | collective-permute-start | bytes 294920 | tf_op jit(solution)/shard_map/ppermute | solution.py:1194
  212.0 13.5 %collective-permute-start.15 = (f32[32,768]{1,0:T(8,128)}, f32[32,768]{1,0:T(8,128)S(1)}, u32[]{:S(2)}, u32[]{:S(2)}) collective-permute-start(f32[32,768]{1,0:T(8,128)} %get-tuple-element.124), channel_id=1, source_target_pairs={{0,3},{1,2},{2,1},{3,0},{4,7},{5,6},{6,5},{7,4},{8,11},{9,10},{10,... | collective-permute-start | bytes 294920 | tf_op jit(solution)/shard_map/ppermute | solution.py:1194
  212.9 12.6 %collective-permute-start.17 = (bf16[2,48,1536]{2,1,0:T(8,128)(2,1)S(1)}, bf16[2,48,1536]{2,1,0:T(8,128)(2,1)S(1)}, u32[]{:S(2)}, u32[]{:S(2)}) collective-permute-start(bf16[2,48,1536]{2,1,0:T(8,128)(2,1)S(1)} %add_convert_fusion.1), channel_id=1, source_target_pairs={{0,8},{4,12},{8,0},{12,4},{1,9},{5,13},{9,1},{13,5},{2,10},{6,14},... | collective-permute-start | bytes 884744 | tf_op jit(solution)/shard_map/ppermute | solution.py:1194
  214.3 11.2 %collective-permute-start.16 = (bf16[2,48,1536]{2,1,0:T(8,128)(2,1)S(1)}, bf16[2,48,1536]{2,1,0:T(8,128)(2,1)S(1)}, u32[]{:S(2)}, u32[]{:S(2)}) collective-permute-start(bf16[2,48,1536]{2,1,0:T(8,128)(2,1)S(1)} %add_convert_fusion.3), channel_id=1, source_target_pairs={{0,16},{16,0},{1,17},{17,1},{2,18},{18,2},{3,19},{19,3},{4,20},{20... | collective-permute-start | bytes 884744 | tf_op jit(solution)/shard_map/ppermute | solution.py:1194
  225.8 10.0 %collective-permute-start.20 = (f32[56,768]{1,0:T(8,128)S(1)}, f32[56,768]{1,0:T(8,128)S(1)}, u32[]{:S(2)}, u32[]{:S(2)}) collective-permute-start(f32[56,768]{1,0:T(8,128)S(1)} %get-tuple-element.130), channel_id=1, source_target_pairs={{0,12},{4,8},{8,4},{12,0},{1,13},{5,9},{9,5},{13,1},{2,14},{6,10},... | collective-permute-start | bytes 516104 | tf_op jit(solution)/shard_map/ppermute | solution.py:1194
  225.9 12.0 %collective-permute-start.19 = (f32[56,768]{1,0:T(8,128)S(1)}, f32[56,768]{1,0:T(8,128)S(1)}, u32[]{:S(2)}, u32[]{:S(2)}) collective-permute-start(f32[56,768]{1,0:T(8,128)S(1)} %get-tuple-element.130), channel_id=1, source_target_pairs={{0,8},{4,12},{8,0},{12,4},{1,9},{5,13},{9,1},{13,5},{2,10},{6,14},... | collective-permute-start | bytes 516104 | tf_op jit(solution)/shard_map/ppermute | solution.py:1194
  227.1 10.8 %collective-permute-start.18 = (f32[56,768]{1,0:T(8,128)S(1)}, f32[56,768]{1,0:T(8,128)S(1)}, u32[]{:S(2)}, u32[]{:S(2)}) collective-permute-start(f32[56,768]{1,0:T(8,128)S(1)} %get-tuple-element.130), channel_id=1, source_target_pairs={{0,4},{4,0},{8,12},{12,8},{1,5},{5,1},{9,13},{13,9},{2,6},{6,2},{1... | collective-permute-start | bytes 516104 | tf_op jit(solution)/shard_map/ppermute | solution.py:1194
  227.7 14.6 %collective-permute-start.22 = (bf16[48,1536]{1,0:T(8,128)(2,1)S(1)}, bf16[48,1536]{1,0:T(8,128)(2,1)S(1)}, u32[]{:S(2)}, u32[]{:S(2)}) collective-permute-start(bf16[48,1536]{1,0:T(8,128)(2,1)S(1)} %get-tuple-element.131), channel_id=1, source_target_pairs={{0,1},{1,0},{2,3},{3,2},{4,5},{5,4},{6,7},{7,6},{8,9},{9,8},{10,11... | collective-permute-start | bytes 442376 | tf_op jit(solution)/shard_map/ppermute | solution.py:1194
  235.5 13.6 %collective-permute-start.23 = (bf16[48,1536]{1,0:T(8,128)(2,1)S(1)}, bf16[48,1536]{1,0:T(8,128)(2,1)S(1)}, u32[]{:S(2)}, u32[]{:S(2)}) collective-permute-start(bf16[48,1536]{1,0:T(8,128)(2,1)S(1)} %get-tuple-element.132), channel_id=1, source_target_pairs={{0,2},{1,3},{2,0},{3,1},{4,6},{5,7},{6,4},{7,5},{8,10},{9,11},{10,... | collective-permute-start | bytes 442376 | tf_op jit(solution)/shard_map/ppermute | solution.py:1194
  235.8 13.3 %collective-permute-start.24 = (bf16[48,1536]{1,0:T(8,128)(2,1)S(1)}, bf16[48,1536]{1,0:T(8,128)(2,1)S(1)}, u32[]{:S(2)}, u32[]{:S(2)}) collective-permute-start(bf16[48,1536]{1,0:T(8,128)(2,1)S(1)} %get-tuple-element.133), channel_id=1, source_target_pairs={{0,3},{1,2},{2,1},{3,0},{4,7},{5,6},{6,5},{7,4},{8,11},{9,10},{10,... | collective-permute-start | bytes 442376 | tf_op jit(solution)/shard_map/ppermute | solution.py:1194
  237.9 22.6 %collective-permute-start.21 = (f32[20,768]{1,0:T(8,128)S(1)}, f32[20,768]{1,0:T(8,128)S(1)}, u32[]{:S(2)}, u32[]{:S(2)}) collective-permute-start(f32[20,768]{1,0:T(8,128)S(1)} %slice.225), channel_id=1, source_target_pairs={{0,16},{16,0},{1,17},{17,1},{2,18},{18,2},{3,19},{19,3},{4,20},{20... | collective-permute-start | bytes 184328 | tf_op jit(solution)/shard_map/ppermute | solution.py:1194
  238.8 11.6 %copy-start.4 = (f32[128,768]{1,0:T(8,128)}, f32[128,768]{1,0:T(8,128)S(1)}, u32[]{:S(2)}) copy-start(f32[128,768]{1,0:T(8,128)S(1)} %slice_dynamic-update-slice_fusion) | copy-start | bytes 1179652
  250.4 10.2 %collective-permute-start.4 = (bf16[192,768]{1,0:T(8,128)(2,1)S(1)}, bf16[192,768]{1,0:T(8,128)(2,1)S(1)}, u32[]{:S(2)}, u32[]{:S(2)}) collective-permute-start(bf16[192,768]{1,0:T(8,128)(2,1)S(1)} %pad_maximum_fusion), channel_id=1, source_target_pairs={{0,16},{16,0},{1,17},{17,1},{2,18},{18,2},{3,19},{19,3},{4,20},{20... | collective-permute-start | bytes 884744 | tf_op jit(solution)/shard_map/ppermute | solution.py:1194
  (27 other events, 139.4 us)
Sparse Core Ops, SparseCore 0:
  110.3 127.6 reduce-scatter.1

commit v2 on v1

--- a/solution.py
+++ b/solution.py
@@ -439,90 +439,46 @@
     )(own, halo, halo, halo, bias, ok, hm, hr, hrf)
 
 
-def mlp_body(
-    tile, steps, att_ref, x_ref, og_ref, lse_ref, wout_ref, vec_ref, toh_ref, wup_ref, wdn_ref,
-    out_ref, gmx_ref, gres_ref, gb_ref, dw_ref, vg_ref, dub_ref,
-    n2, n2t, gm, res, branch, mlp, gn, act, dh, up_buf, dn_buf, out_buf, gmx_buf, gres_buf, gb_buf,
-    og_buf, lse_buf, wup_buf, wdn_buf, sems, out_sems, in_sems, w_sems,
+def hidden_body(
+    tile, steps, att_ref, x_ref, og_ref, wout_ref, vec_ref, wup_ref, wdn_ref,
+    act_ref, dh_ref, dw_ref, dub_ref, n2, n2t, gm, up_buf, dn_buf, sems,
 ):
     step = pl.program_id(0)
     n, d = n2.shape
     row = lambda i: vec_ref[i : i + 1]
-    tiles, few, rows_dn = n // tile, dn_buf.shape[0], dn_buf.shape[1]
-    rows_up = up_buf.shape[1]
-    span = lambda t: pl.ds(pl.multiple_of(t * tile, tile), tile)
-    late = (
-        pltpu.make_async_copy(og_ref, og_buf, in_sems.at[0]),
-        pltpu.make_async_copy(lse_ref, lse_buf, in_sems.at[1]),
-    )
-
-    def weights(c):
-        slot = lax.rem(c, 2)
-        at = pl.ds(pl.multiple_of(c * d, d), d)
-        return (
-            pltpu.make_async_copy(wup_ref.at[:, at], wup_buf.at[slot], w_sems.at[slot, 0]),
-            pltpu.make_async_copy(wdn_ref.at[at, :], wdn_buf.at[slot], w_sems.at[slot, 1]),
-        )
+    tiles = n // tile
+    dests, rows_up, _ = up_buf.shape
+    few, rows_dn, _ = dn_buf.shape
 
     @pl.when(step == 0)
     def _():
-        for copy in late + weights(0):
-            copy.start()
-
         def one(t, carry):
-            rows = span(t)
+            rows = pl.ds(pl.multiple_of(t * tile, tile), tile)
             x = unmask(x_ref[rows, :].astype(F32), row(0))
-            br = dot(att_ref[rows, :], wout_ref[...]) + row(3)
-            r = x + row(4) * br
-            branch[rows, :] = br
-            res[rows, :] = r
-            unit, _ = norm_parts(r)
+            unit, _ = norm_parts(x + row(4) * (dot(att_ref[rows, :], wout_ref[...]) + row(3)))
             n2[rows, :] = (unit * row(5) + row(6)).astype(BF16)
-            mlp[rows, :] = jnp.zeros((tile, d), F32)
-            gn[rows, :] = jnp.zeros((tile, d), F32)
+            gm[rows, :] = (row(8) * og_ref[rows, :].astype(F32)).astype(BF16)
             return carry
 
         lax.fori_loop(0, tiles, one, 0)
         n2t[...] = n2[...].T
-        vg_ref[...] = jnp.zeros_like(vg_ref)
-        for copy in late:
-            copy.wait()
-
-        def two(t, carry):
-            rows = span(t)
-            gm[rows, :] = (row(8) * og_buf[rows, :].astype(F32)).astype(BF16)
-            return carry
-
-        lax.fori_loop(0, tiles, two, 0)
-
-    for copy in weights(step):
-        copy.wait()
-
-    @pl.when(step + 1 < steps)
-    def _():
-        for copy in weights(step + 1):
-            copy.start()
-
-    wup, wdn = wup_buf[lax.rem(step, 2)], wdn_buf[lax.rem(step, 2)]
+
+    wup, wdn = wup_ref[...], wdn_ref[...]
     upb = vec_ref[pl.ds(12 + step, 1), :]
-    dub_ref[...] = jnp.zeros_like(dub_ref)
-
-    def one(t, carry):
-        rows = pl.ds(pl.multiple_of(t * 2 * tile, 2 * tile), 2 * tile)
+
+    def one(t, total):
+        rows = pl.ds(pl.multiple_of(t * tile, tile), tile)
         h = dot(n2[rows, :], wup) + upb
         da = dot_t(gm[rows, :], wdn)
         cdf = 0.5 * (1.0 + lax.erf(h * math.sqrt(0.5)))
         pdf = jnp.exp(-0.5 * h * h) * (1.0 / math.sqrt(2.0 * math.pi))
-        a = (h * cdf).astype(BF16)
+        act_ref[rows, :] = (h * cdf).astype(BF16)
         g = (da * (cdf + h * pdf)).astype(BF16)
-        act[rows, :] = a
-        dh[rows, :] = g
-        mlp[rows, :] += dot(a, wdn)
-        gn[rows, :] += dot_t(g, wup)
-        dub_ref[0:1] += jnp.sum(g.astype(F32), axis=0, keepdims=True)
-        return carry
-
-    lax.fori_loop(0, tiles // 2, one, 0)
+        dh_ref[rows, :] = g
+        return total + jnp.sum(g.astype(F32), axis=0, keepdims=True)
+
+    total = lax.fori_loop(0, tiles, one, jnp.zeros((1, wup.shape[1]), F32))
+    dub_ref[...] = jnp.broadcast_to(total, dub_ref.shape)
 
     def copies(c):
         at = pl.multiple_of(c * rows_up, 8)
@@ -540,124 +496,132 @@
         for copy in copies(step - 1):
             copy.wait()
 
-    up_buf[...] = dot(n2t[...], dh[...]).astype(BF16).reshape(up_buf.shape)
-    dn_buf[...] = dot_0(act[...], gm[...]).astype(BF16).reshape(dn_buf.shape)
+    up_buf[...] = dot(n2t[...], dh_ref[...]).astype(BF16).reshape(up_buf.shape)
+    dn_buf[...] = dot_0(act_ref[...], gm[...]).astype(BF16).reshape(dn_buf.shape)
     for copy in copies(step):
         copy.start()
 
     @pl.when(step == steps - 1)
     def _():
-        outs = ((out_buf, out_ref), (gmx_buf, gmx_ref), (gres_buf, gres_ref), (gb_buf, gb_ref))
-
-        def sends(t, slot):
-            return [
-                pltpu.make_async_copy(buf.at[slot], ref.at[span(t), :], out_sems.at[slot, i])
-                for i, (buf, ref) in enumerate(outs)
-            ]
-
-        def add(i, v):
-            vg_ref[i : i + 1] += jnp.sum(v, axis=0, keepdims=True)
-
-        def one(t, carry):
-            rows, slot = span(t), lax.rem(t, 2)
-
-            @pl.when(t >= 2)
-            def _():
-                for copy in sends(t - 2, slot):
-                    copy.wait()
-
-            r, br, att = res[rows, :], branch[rows, :], att_ref[rows, :]
-            og = og_buf[rows, :].astype(F32)
-            mo = mlp[rows, :] + row(7)
-            out_buf[slot] = (r + row(8) * mo).astype(BF16)
-            add(0, og * mo)
-            add(1, gm[rows, :].astype(F32))
-            unit, inv = norm_parts(r)
-            grad = gn[rows, :]
-            add(2, grad * unit)
-            add(3, grad)
-            gr = og + norm_pull(grad * row(5), unit, inv)
-            gres_buf[slot] = gr
-            add(4, gr * br)
-            gb = (row(4) * gr).astype(BF16)
-            add(5, gb.astype(F32))
-            gb_buf[slot] = gb
-            mix = dot_t(gb, wout_ref[...]).astype(BF16)
-            prod = mix.astype(F32) * att.astype(F32)
-            delta = sum(dot(part, toh_ref[...]) for part in split3(prod))
-            packed = jnp.zeros(delta.shape, F32)
-            for i, part in enumerate(split3(lse_buf[rows, :]) + split3(delta)):
-                part = part.astype(F32)
-                packed += part if i == 0 else pltpu.roll(part, 16 * i, 1)
-            gmx_buf[slot, :, 0:d] = mix
-            gmx_buf[slot, :, d : d + LANES] = packed.astype(BF16)
-            for copy in sends(t, slot):
-                copy.start()
-            return carry
-
-        lax.fori_loop(0, tiles, one, 0)
-        for t in (tiles - 2, tiles - 1):
-            for copy in sends(t, t % 2):
-                copy.wait()
         for copy in copies(step):
             copy.wait()
 
 
-def mlp_call(att, x, og, lse, w_out, vec, to_head, w_up, w_down, dests, tile=256):
+def hidden_call(att, x, og, w_out, vec, w_up, w_down, dests, tile=512):
     n, d = x.shape
     ff = w_up.shape[1]
     steps = ff // d
     rows_up, rows_dn = d // dests, ff // dests
-    anywhere = pl.BlockSpec(memory_space=pl.ANY)
     return pl.pallas_call(
-        functools.partial(mlp_body, tile, steps),
+        functools.partial(hidden_body, tile, steps),
+        out_shape=(
+            jax.ShapeDtypeStruct((n, ff), BF16),
+            jax.ShapeDtypeStruct((n, ff), BF16),
+            jax.ShapeDtypeStruct((dests, steps * rows_up + rows_dn, d), BF16),
+            jax.ShapeDtypeStruct((8, ff), F32),
+        ),
+        grid=(steps,),
+        in_specs=[hold((n, d))] * 3
+        + [
+            hold((d, d)),
+            hold(vec.shape),
+            pl.BlockSpec((d, d), lambda c: (0, c)),
+            pl.BlockSpec((d, d), lambda c: (c, 0)),
+        ],
+        out_specs=[
+            pl.BlockSpec((n, d), lambda c: (0, c)),
+            pl.BlockSpec((n, d), lambda c: (0, c)),
+            pl.BlockSpec(memory_space=pl.ANY),
+            pl.BlockSpec((8, d), lambda c: (0, c)),
+        ],
+        scratch_shapes=[
+            pltpu.VMEM((n, d), BF16),
+            pltpu.VMEM((d, n), BF16),
+            pltpu.VMEM((n, d), BF16),
+            pltpu.VMEM((dests, rows_up, d), BF16),
+            pltpu.VMEM((dests // steps, rows_dn, d), BF16),
+            pltpu.SemaphoreType.DMA((2,)),
+        ],
+        compiler_params=params(ROOM),
+        cost_estimate=pl.CostEstimate(
+            flops=2 * n * d * (4 * ff + d),
+            transcendentals=2 * n * ff,
+            bytes_accessed=2 * (4 * d * ff + 2 * n * ff + 3 * n * d),
+        ),
+        name="hidden",
+    )(att, x, og, w_out, vec, w_up, w_down)
+
+
+def close_body(
+    att_ref, x_ref, og_ref, lse_ref, act_ref, dh_ref, wout_ref, vec_ref, wup_ref, wdn_ref, toh_ref,
+    out_ref, gmx_ref, gres_ref, gb_ref, vg_ref,
+):
+    step = pl.program_id(0)
+    d = x_ref.shape[1]
+    row = lambda i: vec_ref[i : i + 1]
+
+    @pl.when(step == 0)
+    def _():
+        vg_ref[...] = jnp.zeros_like(vg_ref)
+
+    def add(i, v):
+        vg_ref[i : i + 1] += jnp.sum(v, axis=0, keepdims=True)
+
+    att = att_ref[...]
+    br = dot(att, wout_ref[...]) + row(3)
+    res = unmask(x_ref[...].astype(F32), row(0)) + row(4) * br
+    og = og_ref[...].astype(F32)
+    mo = dot(act_ref[...], wdn_ref[...]) + row(7)
+    out_ref[...] = (res + row(8) * mo).astype(BF16)
+    add(0, og * mo)
+    add(1, (row(8) * og).astype(BF16).astype(F32))
+    unit, inv = norm_parts(res)
+    gn = dot_t(dh_ref[...], wup_ref[...])
+    add(2, gn * unit)
+    add(3, gn)
+    gr = og + norm_pull(gn * row(5), unit, inv)
+    gres_ref[...] = gr
+    add(4, gr * br)
+    gb = (row(4) * gr).astype(BF16)
+    add(5, gb.astype(F32))
+    gb_ref[...] = gb
+    mix = dot_t(gb, wout_ref[...]).astype(BF16)
+    gmx_ref[:, 0:d] = mix
+    prod = mix.astype(F32) * att.astype(F32)
+    toh = toh_ref[...]
+    delta = sum(dot(part, toh) for part in split3(prod))
+    packed = jnp.zeros(delta.shape, F32)
+    for i, part in enumerate(split3(lse_ref[...]) + split3(delta)):
+        part = part.astype(F32)
+        packed += part if i == 0 else pltpu.roll(part, 16 * i, 1)
+    gmx_ref[:, d : d + LANES] = packed.astype(BF16)
+
+
+def close_call(att, x, og, lse, act, dh, w_out, vec, w_up, w_down, to_head, tile=256):
+    n, d = x.shape
+    ff = w_up.shape[1]
+    rows = lambda width: pl.BlockSpec((tile, width), lambda i: (i, 0))
+    return pl.pallas_call(
+        close_body,
         out_shape=(
             jax.ShapeDtypeStruct((n, d), BF16),
             jax.ShapeDtypeStruct((n, d + LANES), BF16),
             jax.ShapeDtypeStruct((n, d), F32),
             jax.ShapeDtypeStruct((n, d), BF16),
-            jax.ShapeDtypeStruct((dests, steps * rows_up + rows_dn, d), BF16),
             jax.ShapeDtypeStruct((8, d), F32),
-            jax.ShapeDtypeStruct((8, ff), F32),
         ),
-        grid=(steps,),
-        in_specs=[hold(att.shape), hold(x.shape), anywhere, anywhere]
-        + [hold(a.shape) for a in (w_out, vec, to_head)]
-        + [anywhere, anywhere],
-        out_specs=[anywhere] * 5 + [hold((8, d)), pl.BlockSpec((8, d), lambda c: (0, c))],
-        scratch_shapes=[
-            pltpu.VMEM((n, d), BF16),
-            pltpu.VMEM((d, n), BF16),
-            pltpu.VMEM((n, d), BF16),
-            pltpu.VMEM((n, d), F32),
-            pltpu.VMEM((n, d), F32),
-            pltpu.VMEM((n, d), F32),
-            pltpu.VMEM((n, d), F32),
-            pltpu.VMEM((n, d), BF16),
-            pltpu.VMEM((n, d), BF16),
-            pltpu.VMEM((dests, rows_up, d), BF16),
-            pltpu.VMEM((dests // steps, rows_dn, d), BF16),
-            pltpu.VMEM((2, tile, d), BF16),
-            pltpu.VMEM((2, tile, d + LANES), BF16),
-            pltpu.VMEM((2, tile, d), F32),
-            pltpu.VMEM((2, tile, d), BF16),
-            pltpu.VMEM((n, d), BF16),
-            pltpu.VMEM((n, LANES), F32),
-            pltpu.VMEM((2, d, d), BF16),
-            pltpu.VMEM((2, d, d), BF16),
-            pltpu.SemaphoreType.DMA((2,)),
-            pltpu.SemaphoreType.DMA((2, 4)),
-            pltpu.SemaphoreType.DMA((2,)),
-            pltpu.SemaphoreType.DMA((2, 2)),
-        ],
+        grid=(n // tile,),
+        in_specs=[rows(d), rows(d), rows(d), rows(LANES), rows(ff), rows(ff)]
+        + [hold(a.shape) for a in (w_out, vec, w_up, w_down, to_head)],
+        out_specs=[rows(d), rows(d + LANES), rows(d), rows(d), hold((8, d))],
         compiler_params=params(ROOM),
         cost_estimate=pl.CostEstimate(
-            flops=2 * n * d * (6 * ff + 2 * d),
-            transcendentals=2 * n * ff,
-            bytes_accessed=2 * (4 * d * ff + 8 * n * d),
+            flops=2 * n * d * (2 * ff + 3 * d),
+            transcendentals=n,
+            bytes_accessed=2 * (2 * d * ff + 2 * n * ff + 8 * n * d),
         ),
-        name="mlp",
-    )(att, x, og, lse, w_out, vec, to_head, w_up, w_down)
+        name="close",
+    )(att, x, og, lse, act, dh, w_out, vec, w_up, w_down, to_head)
 
 
 def table_sums(geo, acc_ref, fold_ref, o_ref):
@@ -858,7 +822,7 @@
             pltpu.VMEM((geo.bands, 32, geo.slots), F32),
             pltpu.VMEM((16, 2 * geo.width), F32),
         ],
-        compiler_params=params(ROOM),
+        compiler_params=params(36),
         cost_estimate=pl.CostEstimate(
             flops=4 * mm, transcendentals=geo.pages * G * geo.bands * 65536, bytes_accessed=20 * MIB
         ),
@@ -1038,7 +1002,7 @@
             out_specs=[block, block] + more_specs,
             scratch_shapes=scratch,
         ),
-        compiler_params=params(ROOM),
+        compiler_params=params(LESS),
         cost_estimate=pl.CostEstimate(
             flops=4 * n * d * d, transcendentals=n, bytes_accessed=2 * (5 * n * d + 2 * d * d)
         ),
@@ -1263,10 +1227,13 @@
     att, lse, x = att.reshape(count, width), lse.reshape(count, LANES), x.reshape(count, width)
     counted = (patch_mask * loss_mask == 1)[..., None]
     out_g = jnp.where(counted, out_grad, jnp.zeros((), BF16)).reshape(count, width)
-    out, gmx, gres, gb, d_mlp, vg_mlp, d_upb = mlp_call(
-        att, x, out_g, lse, w_out, vec, to_head, w_up, w_down, row_peers * col_peers
+    act, dh, d_mlp, d_upb = hidden_call(
+        att, x, out_g, w_out, vec, w_up, w_down, row_peers * col_peers
     )
     d_mlp = lax.psum_scatter(d_mlp, ("row", "col"), scatter_dimension=0, tiled=True)[0]
+    out, gmx, gres, gb, vg_mlp = close_call(
+        att, x, out_g, lse, act, dh, w_out, vec, w_up, w_down, to_head
+    )
     gmx = gmx.reshape(pages, geo.own, width + LANES)
     rel_late, _ = join((rel_table, gb))
     pieces, bias_b = halo_pieces(geo, gmx, bias_table(geo, rel_late, 1))

time: 272 us -> 281 us (1.033)
  starting transfers between devices: 45.9 us -> 51.7 us
  local copies, waits for them, and re-layouts: 16.4 us -> 20.9 us
    pallas_call x1 -> x2, Pallas kernels: 47.4 us -> 56.5 us  [the longest x1 32.7 us: hidden_call(): pl.pallas_call(functools.partial(hidden_body, tile, steps), out_shape=(ja...]
    pallas_call x2, Pallas kernels: 18.9 us -> 11.8 us  [weight_call(): pl.pallas_call(body, out_shape=(out, out) + more, grid_spec=pltpu.Prefetc...]
    ppermute x8, waiting for transfers between devices: 2.54 us -> 9.41 us  [passed_along(): lax.ppermute(value, axis, [(i, i + steps) for i in range(first, last)])]
    ppermute x17, waiting for transfers between devices: 26.2 us -> 20.1 us  [swap(): lax.ppermute(value, axis, [(i, i ^ bit) for i in range(lax.axis_size(axis...]
    ppermute x17, starting transfers between devices: 23.8 us -> 29.8 us  [swap(): lax.ppermute(value, axis, [(i, i ^ bit) for i in range(lax.axis_size(axis...]
    unnamed x84 -> x122, local copies, waits for them, and re-layouts: 6.22 us -> 12 us
    pallas_call x1, Pallas kernels: 16.2 us -> 13 us  [key_grad_call(): pl.pallas_call(functools.partial(key_grad_body, geo), out_shape=(out, out...]
  transfers between devices with their start and end apart: 26 -> 26, of which waited for: 8 -> 11; matrix products, arithmetic and copies ran while one was open for 4% -> 3% of each run, Pallas kernels for 32% -> 36%
where the time goes in v2:
time: 281 us; the launch traced here: 280 us
  Pallas kernels  157 us (56%)
  starting transfers between devices  51.7 us (18%)
  waiting for transfers between devices  29.5 us (10%)
  local copies, waits for them, and re-layouts  20.9 us (7%)
  between operations  15.1 us (5%)
  other arithmetic  5.85 us (2%)
    pallas_call x1, Pallas kernels, hidden_call(): pl.pallas_call(functools.partial(hidden_body, tile, steps), out_shape=(ja...  32.7 us
    ppermute x17, starting transfers between devices, swap(): lax.ppermute(value, axis, [(i, i ^ bit) for i in range(lax.axis_size(axis...  29.8 us
    pallas_call x1, Pallas kernels, close_call(): pl.pallas_call(close_body, out_shape=(jax.ShapeDtypeStruct((n, d), BF16),...  23.8 us
    ppermute x8, starting transfers between devices, passed_along(): lax.ppermute(value, axis, [(i, i + steps) for i in range(first, last)])  21.8 us
    ppermute x17, waiting for transfers between devices, swap(): lax.ppermute(value, axis, [(i, i ^ bit) for i in range(lax.axis_size(axis...  20.1 us
    pallas_call x2, Pallas kernels, qkv_call(): pl.pallas_call(body, out_shape=jax.ShapeDtypeStruct((pages, rows, 3 * d),...  17.8 us
    pallas_call x1, Pallas kernels, key_grad_call(): pl.pallas_call(functools.partial(key_grad_body, geo), out_shape=(out, out...  13 us
    pallas_call x1, Pallas kernels, token_grad_call(): pl.pallas_call(functools.partial(token_grad_body, pages, heads), out_shap...  12.3 us
  transfers between devices with their start and end apart: 26, of which 11 were waited for; matrix products, arithmetic and copies ran while one was open for 3% of the time, Pallas kernels for 36%

profile of v2, /device:TPU:0, one launch (start us, length us, event | category | flops | bytes accessed | tf_op | source)
XLA Modules:
  0.0 279.9 jit_solution(15826908382568607698)
XLA Ops:
  8.2 3.0 %broadcast_select_fusion = (bf16[4,16,16,768]{3,2,1,0:T(8,128)(2,1)}, bf16[4,16,16,768]{3,2,1,0:T(8,128)(2,1)S(1)}) fusion(bf16[4,16,16,768]{3,2,1,0:T(8,128)(2,1)} %param.58, pred[4,16,16]{2,1,0:T(8,128)(4,1)S(1)} %get-tuple-element.188, bf16[4,16,16,768]{3,2,1,0:T(8,128)(2,1)} %param.37, pred[4,16,16]{2,1,0:T(8,128)(4,1)S(1)} %get-tuple-element.189), kind=kLoop, calls=%fused_computation | loop fusion | flops 1572864 | bytes 6293504 | tf_op jit(solution)/shard_map/jit(_where)/select_n | solution.py:1229
  11.3 2.4 collective-permute-start
  16.7 2.5 collective-permute-done.1.bottom_ref
  20.0 3.3 %strips.2 = (bf16[4,72,768]{2,1,0:T(8,128)(2,1)}, bf16[4,72,768]{2,1,0:T(8,128)(2,1)}) custom-call(bf16[4,256,768]{2,1,0:T(8,128)(2,1)} %bitcast.44, bf16[4,48,768]{2,1,0:T(8,128)(2,1)} %copy-done.26, bf16[4,48,768]{2,1,0:T(8,128)(2,1)} %copy-done.27), custom_call_target="tpu_custom_call" | custom-call | tf_op jit(solution)/shard_map/strips/pallas_call | solution.py:324
  23.2 3.5 %collective-permute-start.2 = (bf16[4,72,768]{2,1,0:T(8,128)(2,1)}, bf16[4,72,768]{2,1,0:T(8,128)(2,1)S(1)}, u32[]{:S(2)}, u32[]{:S(2)}) collective-permute-start(bf16[4,72,768]{2,1,0:T(8,128)(2,1)} %get-tuple-element.84), channel_id=1, source_target_pairs={{0,1},{1,2},{2,3},{4,5},{5,6},{6,7},{8,9},{9,10},{10,11},{12,13},{... | collective-permute-start | bytes 1327112 | tf_op jit(solution)/shard_map/ppermute | solution.py:1154
  28.7 3.0 %bias_table.2.bias_ref = f32[3,256,256]{2,1,0:T(8,128)} custom-call(f32[12,50]{1,0:T(8,128)} %table.2, s32[16,256]{1,0:T(8,128)} %constant.116.clone.index_ref), custom_call_target="tpu_custom_call" | custom-call | tf_op jit(solution)/shard_map/bias_table/pallas_call | solution.py:229
  31.7 8.1 %qkv_own.1.own_ref.k_ref.v_ref = bf16[4,256,2304]{2,1,0:T(8,128)(2,1)} custom-call(bf16[4,256,768]{2,1,0:T(8,128)(2,1)} %bitcast.45, bf16[768,2304]{1,0:T(8,128)(2,1)} %w_ref.5, f32[16,768]{1,0:T(8,128)} %reshape.110.vec_ref), custom_call_target="tpu_custom_call" | custom-call | flops 3623878656 | bytes 9830400 | tf_op jit(solution)/shard_map/qkv_own/pallas_call | solution.py:288
  41.3 9.6 %qkv_halo.1.hk_ref.hv_ref.cq_ref.hq_ref.cls_ref = bf16[4,288,2304]{2,1,0:T(8,128)(2,1)} custom-call(bf16[4,48,768]{2,1,0:T(8,128)(2,1)} %copy-done.26, bf16[4,48,768]{2,1,0:T(8,128)(2,1)} %copy-done.27, bf16[4,72,768]{2,1,0:T(8,128)(2,1)} %copy-done.47, bf16[4,72,768]{2,1,0:T(8,128)(2,1)} %copy-done.48, bf16[4,16,768]{2,1,0:T(8,128)(2,1)} %broadcast_select_fusion.2.last_ref, ...), custom_call_target="tpu_custom_call" | custom-call | flops 4076863488 | bytes 10616832 | tf_op jit(solution)/shard_map/qkv_halo/pallas_call | solution.py:288
  51.0 11.5 %attend.1 = (bf16[4,256,768]{2,1,0:T(8,128)(2,1)}, f32[4,256,128]{2,1,0:T(8,128)}, bf16[4,3,4,256,256]{4,3,2,1,0:T(8,128)(2,1)}, f32[8,768]{1,0:T(8,128)}) custom-call(bf16[4,256,2304]{2,1,0:T(8,128)(2,1)} %qkv_own.1.own_ref.k_ref.v_ref, bf16[4,288,2304]{2,1,0:T(8,128)(2,1)} %qkv_halo.1.hk_ref.hv_ref.cq_ref.hq_ref.cls_ref, ...), custom_call_target="tpu_custom_call" | custom-call | flops 3221225472 | bytes 16777216 | tf_op jit(solution)/shard_map/attend/pallas_call | solution.py:425
  62.5 32.7 %hidden.1 = (bf16[1024,3072]{1,0:T(8,128)(2,1)}, bf16[1024,3072]{1,0:T(8,128)(2,1)}, bf16[16,384,768]{2,1,0:T(8,128)(2,1)}, f32[8,3072]{1,0:T(8,128)}) custom-call(bf16[1024,768]{1,0:T(8,128)(2,1)} %bitcast.50, bf16[1024,768]{1,0:T(8,128)(2,1)} %bitcast.46, bf16[1024,768]{1,0:T(8,128)(2,1)} %bitcast.59, bf16[768,768]{1,0:T(8,128)(2,1)} %wout_ref.5, ...), custom_call_target="tpu_custom_call" | custom-call | flops 20535312384 | bytes 36175872 | tf_op jit(solution)/shard_map/hidden/pallas_call | solution.py:515
  95.3 23.8 %close.1 = (bf16[1024,768]{1,0:T(8,128)(2,1)}, bf16[1024,896]{1,0:T(8,128)(2,1)}, f32[1024,768]{1,0:T(8,128)}, bf16[1024,768]{1,0:T(8,128)(2,1)}, f32[8,768]{1,0:T(8,128)}) custom-call(bf16[1024,768]{1,0:T(8,128)(2,1)} %bitcast.51, bf16[1024,768]{1,0:T(8,128)(2,1)} %bitcast.47, bf16[1024,768]{1,0:T(8,128)(2,1)} %bitcast.60, f32[1024,128]{1,0:T(8,128)} %bitcast.65, ...), custom_call_target="tpu_custom_call" | custom-call | flops 13287555072 | bytes 34603008 | tf_op jit(solution)/shard_map/close/pallas_call | solution.py:604
  120.4 6.6 %collective-permute-start.6 = (bf16[4,48,896]{2,1,0:T(8,128)(2,1)S(1)}, bf16[4,48,896]{2,1,0:T(8,128)(2,1)S(1)}, u32[]{:S(2)}, u32[]{:S(2)}) collective-permute-start(bf16[4,48,896]{2,1,0:T(8,128)(2,1)S(1)} %get-tuple-element.163), channel_id=1, source_target_pairs={{0,4},{4,8},{8,12},{1,5},{5,9},{9,13},{2,6},{6,10},{10,14},{3,7},{... | collective-permute-start | bytes 1032200 | tf_op jit(solution)/shard_map/ppermute | solution.py:1154
  128.6 3.0 %bias_table.3.bias_ref = f32[3,256,256]{2,1,0:T(8,128)} custom-call(f32[12,50]{1,0:T(8,128)} %table.2, s32[16,256]{1,0:T(8,128)} %constant.118.clone.index_ref), custom_call_target="tpu_custom_call" | custom-call | tf_op jit(solution)/shard_map/bias_table/pallas_call | solution.py:229
  133.1 3.9 %strips.3 = (bf16[4,72,896]{2,1,0:T(8,128)(2,1)}, bf16[4,72,896]{2,1,0:T(8,128)(2,1)}) custom-call(bf16[4,256,896]{2,1,0:T(8,128)(2,1)} %bitcast.40, bf16[4,48,896]{2,1,0:T(8,128)(2,1)} %copy-done.5, bf16[4,48,896]{2,1,0:T(8,128)(2,1)} %copy-done.7), custom_call_target="tpu_custom_call" | custom-call | tf_op jit(solution)/shard_map/strips/pallas_call | solution.py:324
  137.1 4.2 %collective-permute-start.8 = (bf16[4,72,896]{2,1,0:T(8,128)(2,1)}, bf16[4,72,896]{2,1,0:T(8,128)(2,1)S(1)}, u32[]{:S(2)}, u32[]{:S(2)}) collective-permute-start(bf16[4,72,896]{2,1,0:T(8,128)(2,1)} %get-tuple-element.101), channel_id=1, source_target_pairs={{0,1},{1,2},{2,3},{4,5},{5,6},{6,7},{8,9},{9,10},{10,11},{12,13},{... | collective-permute-start | bytes 1548296 | tf_op jit(solution)/shard_map/ppermute | solution.py:1154
  142.6 11.4 %query_grad.1 = (bf16[4,256,768]{2,1,0:T(8,128)(2,1)}, f32[16,128]{1,0:T(8,128)}) custom-call(bf16[4,3,4,256,256]{4,3,2,1,0:T(8,128)(2,1)} %get-tuple-element.92.p_ref, bf16[4,256,2304]{2,1,0:T(8,128)(2,1)} %qkv_own.1.own_ref.k_ref.v_ref, bf16[4,256,2304]{2,1,0:T(8,128)(2,1)} %qkv_own.1.own_ref.k_ref.v_ref, ...), custom_call_target="tpu_custom_call" | custom-call | flops 3221225472 | bytes 20971520 | tf_op jit(solution)/shard_map/query_grad/pallas_call | solution.py:708
  158.4 6.5 %early_weight.1 = (bf16[8,48,1536]{2,1,0:T(8,128)(2,1)S(1)}, bf16[8,48,1536]{2,1,0:T(8,128)(2,1)S(1)}, bf16[768,1024]{1,0:T(8,128)(2,1)S(1)}, f32[8,768]{1,0:T(8,128)S(1)}) custom-call(s32[4]{0:T(128)S(1)} %pad_add_fusion.at_ref, bf16[1024,768]{1,0:T(8,128)(2,1)S(1)} %bitcast.49, bf16[1024,768]{1,0:T(8,128)(2,1)S(1)} %bitcast.52, ...), custom_call_target="tpu_custom_call" | custom-call | flops 2415919104 | bytes 10223616 | tf_op jit(solution)/shard_map/early_weight/pallas_call | solution.py:995
  165.5 6.9 %collective-permute-start.5 = (bf16[8,48,1536]{2,1,0:T(8,128)(2,1)S(1)}, bf16[8,48,1536]{2,1,0:T(8,128)(2,1)S(1)}, u32[]{:S(2)}, u32[]{:S(2)}) collective-permute-start(bf16[8,48,1536]{2,1,0:T(8,128)(2,1)S(1)} %get-tuple-element.97), channel_id=1, source_target_pairs={{0,4},{4,0},{8,12},{12,8},{1,5},{5,1},{9,13},{13,9},{2,6},{6,2},{1... | collective-permute-start | bytes 3538952 | tf_op jit(solution)/shard_map/ppermute | solution.py:1158
  172.4 6.9 %collective-permute-done.9.right_ref = bf16[4,72,896]{2,1,0:T(8,128)(2,1)S(1)} collective-permute-done((bf16[4,72,896]{2,1,0:T(8,128)(2,1)}, bf16[4,72,896]{2,1,0:T(8,128)(2,1)S(1)}, u32[]{:S(2)}, u32[]{:S(2)}) %collective-permute-start.9) | collective-permute-done | bytes 516128 | tf_op jit(solution)/shard_map/ppermute | solution.py:1154
  179.4 2.3 copy-done
  181.8 13.0 %key_grad.1 = (bf16[4,256,768]{2,1,0:T(8,128)(2,1)S(1)}, bf16[4,256,768]{2,1,0:T(8,128)(2,1)S(1)}, bf16[16,1536]{1,0:T(8,128)(2,1)S(1)}) custom-call(bf16[4,256,2304]{2,1,0:T(8,128)(2,1)S(1)} %copy-done, bf16[4,288,2304]{2,1,0:T(8,128)(2,1)S(1)} %bitcast.38, bf16[4,288,2304]{2,1,0:T(8,128)(2,1)S(1)} %bitcast.38, bf16[4,256,896]{2,1,0:T(8,128)(2,1)S(1)} %bitcast.42, ...), custom_call_target="tpu_custom_call" | custom-call | flops 6442450944 | bytes 20971520 | tf_op jit(solution)/shard_map/key_grad/pallas_call | solution.py:812
  194.8 5.3 %late_weight.1 = (bf16[8,48,1536]{2,1,0:T(8,128)(2,1)S(1)}, bf16[8,48,1536]{2,1,0:T(8,128)(2,1)S(1)}, f32[8,768]{1,0:T(8,128)S(1)}) custom-call(s32[4]{0:T(128)S(1)} %pad_add_fusion.at_ref, bf16[768,1024]{1,0:T(8,128)(2,1)S(1)} %get-tuple-element.105.nt_ref, bf16[1024,768]{1,0:T(8,128)(2,1)S(1)} %bitcast.55, bf16[1024,768]{1,0:T(8,128)(2,1)S(1)} %bitcast.57, ...), custom_call_target="tpu_custom_call" | custom-call | flops 2415919104 | bytes 10223616 | tf_op jit(solution)/shard_map/late_weight/pallas_call | solution.py:995
  200.2 5.3 %collective-permute-start.10 = (bf16[8,48,1536]{2,1,0:T(8,128)(2,1)S(1)}, bf16[8,48,1536]{2,1,0:T(8,128)(2,1)S(1)}, u32[]{:S(2)}, u32[]{:S(2)}) collective-permute-start(bf16[8,48,1536]{2,1,0:T(8,128)(2,1)S(1)} %get-tuple-element.115), channel_id=1, source_target_pairs={{0,4},{4,0},{8,12},{12,8},{1,5},{5,1},{9,13},{13,9},{2,6},{6,2},{1... | collective-permute-start | bytes 3538952 | tf_op jit(solution)/shard_map/ppermute | solution.py:1158
  205.5 2.5 collective-permute-done.10.r2_ref
  207.9 1.7 fold.1
  212.6 12.3 %token_grad.1 = (f32[1024,768]{1,0:T(8,128)}, f32[32,768]{1,0:T(8,128)}) custom-call(bf16[1024,768]{1,0:T(8,128)(2,1)} %bitcast.48, bf16[1024,768]{1,0:T(8,128)(2,1)} %bitcast.53, bf16[1024,768]{1,0:T(8,128)(2,1)} %bitcast.56, bf16[1024,768]{1,0:T(8,128)(2,1)} %bitcast.58, f32[1024,768]{1,0:T(8,128)} %get-tuple-element.120.gres_ref, ...), custom_call_target="tpu_custom_call" | custom-call | flops 3623878656 | bytes 16121856 | tf_op jit(solution)/shard_map/token_grad/pallas_call | solution.py:1137
  228.1 2.8 collective-permute-start.15
  233.7 4.4 %collective-permute-done.14 = f32[32,768]{1,0:T(8,128)S(1)} collective-permute-done((f32[32,768]{1,0:T(8,128)}, f32[32,768]{1,0:T(8,128)S(1)}, u32[]{:S(2)}, u32[]{:S(2)}) %collective-permute-start.14) | collective-permute-done | bytes 98336 | tf_op jit(solution)/shard_map/ppermute | solution.py:1158
  243.6 2.6 collective-permute-start.24
  247.2 2.7 collective-permute-done.20
  250.0 6.4 %collective-permute-done.23 = bf16[48,1536]{1,0:T(8,128)(2,1)S(1)} collective-permute-done((bf16[48,1536]{1,0:T(8,128)(2,1)S(1)}, bf16[48,1536]{1,0:T(8,128)(2,1)S(1)}, u32[]{:S(2)}, u32[]{:S(2)}) %collective-permute-start.23) | collective-permute-done | bytes 147488 | tf_op jit(solution)/shard_map/ppermute | solution.py:1158
  261.9 7.5 %class_close.1 = bf16[4,768]{1,0:T(4,128)(2,1)} custom-call(s32[1]{0:T(128)} %bitcast.20.mine_ref, f32[16,8,768]{2,1,0:T(8,128)} %bitcast.62, bf16[4,288,2304]{2,1,0:T(8,128)(2,1)} %qkv_halo.1.hk_ref.hv_ref.cq_ref.hq_ref.cls_ref, bf16[16,768]{1,0:T(8,128)(2,1)} %copy-done.10, bf16[768,128]{1,0:T(8,128)(2,1)} %constant.110.clone.toh_ref, ...), custom_call_target="tpu_custom_call" | custom-call | flops 339738624 | bytes 12582912 | tf_op jit(solution)/shard_map/class_close/pallas_call | solution.py:884
  (205 shorter events, 42.9 us)
Async XLA Ops:
  7.2 250.7 %reduce-scatter.2.cloned.1.call-start = ((), (), s32[]{:S(2)}) async-start(), calls=%async_computation.1 | async-start | bytes 10027008 | tf_op jit(solution)/shard_map/reduce_scatter | solution.py:1233
  11.3 5.4 %collective-permute-start = (bf16[4,48,768]{2,1,0:T(8,128)(2,1)S(1)}, bf16[4,48,768]{2,1,0:T(8,128)(2,1)S(1)}, u32[]{:S(2)}, u32[]{:S(2)}) collective-permute-start(bf16[4,48,768]{2,1,0:T(8,128)(2,1)S(1)} %get-tuple-element.165), channel_id=1, source_target_pairs={{0,4},{4,8},{8,12},{1,5},{5,9},{9,13},{2,6},{6,10},{10,14},{3,7},{... | collective-permute-start | bytes 884744 | tf_op jit(solution)/shard_map/ppermute | solution.py:1154
  13.7 5.6 %collective-permute-start.1 = (bf16[4,48,768]{2,1,0:T(8,128)(2,1)S(1)}, bf16[4,48,768]{2,1,0:T(8,128)(2,1)S(1)}, u32[]{:S(2)}, u32[]{:S(2)}) collective-permute-start(bf16[4,48,768]{2,1,0:T(8,128)(2,1)S(1)} %get-tuple-element.164), channel_id=1, source_target_pairs={{4,0},{8,4},{12,8},{5,1},{9,5},{13,9},{6,2},{10,6},{14,10},{7,3},{... | collective-permute-start | bytes 884744 | tf_op jit(solution)/shard_map/ppermute | solution.py:1154
  23.2 16.6 %collective-permute-start.2 = (bf16[4,72,768]{2,1,0:T(8,128)(2,1)}, bf16[4,72,768]{2,1,0:T(8,128)(2,1)S(1)}, u32[]{:S(2)}, u32[]{:S(2)}) collective-permute-start(bf16[4,72,768]{2,1,0:T(8,128)(2,1)} %get-tuple-element.84), channel_id=1, source_target_pairs={{0,1},{1,2},{2,3},{4,5},{5,6},{6,7},{8,9},{9,10},{10,11},{12,13},{... | collective-permute-start | bytes 1327112 | tf_op jit(solution)/shard_map/ppermute | solution.py:1154
  26.7 13.1 %collective-permute-start.3 = (bf16[4,72,768]{2,1,0:T(8,128)(2,1)}, bf16[4,72,768]{2,1,0:T(8,128)(2,1)S(1)}, u32[]{:S(2)}, u32[]{:S(2)}) collective-permute-start(bf16[4,72,768]{2,1,0:T(8,128)(2,1)} %get-tuple-element.85), channel_id=1, source_target_pairs={{1,0},{2,1},{3,2},{5,4},{6,5},{7,6},{9,8},{10,9},{11,10},{13,12},{... | collective-permute-start | bytes 1327112 | tf_op jit(solution)/shard_map/ppermute | solution.py:1154
  95.3 33.1 %copy-start.29 = (f32[12,50]{1,0:T(8,128)S(1)}, f32[12,50]{1,0:T(8,128)}, u32[]{:S(2)}) copy-start(f32[12,50]{1,0:T(8,128)} %table.2) | copy-start | bytes 7204
  120.4 11.3 %collective-permute-start.6 = (bf16[4,48,896]{2,1,0:T(8,128)(2,1)S(1)}, bf16[4,48,896]{2,1,0:T(8,128)(2,1)S(1)}, u32[]{:S(2)}, u32[]{:S(2)}) collective-permute-start(bf16[4,48,896]{2,1,0:T(8,128)(2,1)S(1)} %get-tuple-element.163), channel_id=1, source_target_pairs={{0,4},{4,8},{8,12},{1,5},{5,9},{9,13},{2,6},{6,10},{10,14},{3,7},{... | collective-permute-start | bytes 1032200 | tf_op jit(solution)/shard_map/ppermute | solution.py:1154
  127.0 4.7 %collective-permute-start.7 = (bf16[4,48,896]{2,1,0:T(8,128)(2,1)S(1)}, bf16[4,48,896]{2,1,0:T(8,128)(2,1)S(1)}, u32[]{:S(2)}, u32[]{:S(2)}) collective-permute-start(bf16[4,48,896]{2,1,0:T(8,128)(2,1)S(1)} %get-tuple-element.162), channel_id=1, source_target_pairs={{4,0},{8,4},{12,8},{5,1},{9,5},{13,9},{6,2},{10,6},{14,10},{7,3},{... | collective-permute-start | bytes 1032200 | tf_op jit(solution)/shard_map/ppermute | solution.py:1154
  128.3 66.5 %copy-start.10 = (bf16[16,768]{1,0:T(8,128)(2,1)}, bf16[16,768]{1,0:T(8,128)(2,1)S(1)}, u32[]{:S(2)}) copy-start(bf16[16,768]{1,0:T(8,128)(2,1)S(1)} %concatenate.27.c_ref.x_ref) | copy-start | bytes 73732
  133.1 46.2 %slice-start = ((s8[5308416]{0:T(1024)(128)(4,1)}), s8[4194304]{0:T(1024)(128)(4,1)S(1)}, s32[]{:S(2)}) async-start(s8[5308416]{0:T(1024)(128)(4,1)} %bitcast.37), calls=%async_computation.2 | async-start | bytes 8388608
  137.1 35.3 %collective-permute-start.8 = (bf16[4,72,896]{2,1,0:T(8,128)(2,1)}, bf16[4,72,896]{2,1,0:T(8,128)(2,1)S(1)}, u32[]{:S(2)}, u32[]{:S(2)}) collective-permute-start(bf16[4,72,896]{2,1,0:T(8,128)(2,1)} %get-tuple-element.101), channel_id=1, source_target_pairs={{0,1},{1,2},{2,3},{4,5},{5,6},{6,7},{8,9},{9,10},{10,11},{12,13},{... | collective-permute-start | bytes 1548296 | tf_op jit(solution)/shard_map/ppermute | solution.py:1154
  141.2 38.0 %collective-permute-start.9 = (bf16[4,72,896]{2,1,0:T(8,128)(2,1)}, bf16[4,72,896]{2,1,0:T(8,128)(2,1)S(1)}, u32[]{:S(2)}, u32[]{:S(2)}) collective-permute-start(bf16[4,72,896]{2,1,0:T(8,128)(2,1)} %get-tuple-element.102), channel_id=1, source_target_pairs={{1,0},{2,1},{3,2},{5,4},{6,5},{7,6},{9,8},{10,9},{11,10},{13,12},{... | collective-permute-start | bytes 1548296 | tf_op jit(solution)/shard_map/ppermute | solution.py:1154
  142.6 36.8 %slice-start.1 = ((s8[5308416]{0:T(1024)(128)(4,1)}), s8[1114112]{0:T(1024)(128)(4,1)S(1)}, s32[]{:S(2)}) async-start(s8[5308416]{0:T(1024)(128)(4,1)} %bitcast.37), calls=%async_computation.3 | async-start | bytes 2228224
  158.3 21.1 %copy-start.11 = (f32[16,768]{1,0:T(8,128)S(1)}, f32[16,768]{1,0:T(8,128)}, u32[]{:S(2)}) copy-start(f32[16,768]{1,0:T(8,128)} %constant.107.clone.hrf_ref) | copy-start | bytes 147460
  158.3 21.1 %copy-start.12 = (bf16[16,256]{1,0:T(8,128)(2,1)S(1)}, bf16[16,256]{1,0:T(8,128)(2,1)}, u32[]{:S(2)}) copy-start(bf16[16,256]{1,0:T(8,128)(2,1)} %constant.105.clone.hm_ref) | copy-start | bytes 24580
  165.5 40.0 %collective-permute-start.5 = (bf16[8,48,1536]{2,1,0:T(8,128)(2,1)S(1)}, bf16[8,48,1536]{2,1,0:T(8,128)(2,1)S(1)}, u32[]{:S(2)}, u32[]{:S(2)}) collective-permute-start(bf16[8,48,1536]{2,1,0:T(8,128)(2,1)S(1)} %get-tuple-element.97), channel_id=1, source_target_pairs={{0,4},{4,0},{8,12},{12,8},{1,5},{5,1},{9,13},{13,9},{2,6},{6,2},{1... | collective-permute-start | bytes 3538952 | tf_op jit(solution)/shard_map/ppermute | solution.py:1158
  200.2 7.7 %collective-permute-start.10 = (bf16[8,48,1536]{2,1,0:T(8,128)(2,1)S(1)}, bf16[8,48,1536]{2,1,0:T(8,128)(2,1)S(1)}, u32[]{:S(2)}, u32[]{:S(2)}) collective-permute-start(bf16[8,48,1536]{2,1,0:T(8,128)(2,1)S(1)} %get-tuple-element.115), channel_id=1, source_target_pairs={{0,4},{4,0},{8,12},{12,8},{1,5},{5,1},{9,13},{13,9},{2,6},{6,2},{1... | collective-permute-start | bytes 3538952 | tf_op jit(solution)/shard_map/ppermute | solution.py:1158
  209.7 15.7 %collective-permute-start.11 = (bf16[4,48,1536]{2,1,0:T(8,128)(2,1)S(1)}, bf16[4,48,1536]{2,1,0:T(8,128)(2,1)S(1)}, u32[]{:S(2)}, u32[]{:S(2)}) collective-permute-start(bf16[4,48,1536]{2,1,0:T(8,128)(2,1)S(1)} %get-tuple-element.116), channel_id=1, source_target_pairs={{0,16},{16,0},{1,17},{17,1},{2,18},{18,2},{3,19},{19,3},{4,20},{20... | collective-permute-start | bytes 1769480 | tf_op jit(solution)/shard_map/ppermute | solution.py:1158
  211.2 15.3 %collective-permute-start.12 = (bf16[4,48,1536]{2,1,0:T(8,128)(2,1)S(1)}, bf16[4,48,1536]{2,1,0:T(8,128)(2,1)S(1)}, u32[]{:S(2)}, u32[]{:S(2)}) collective-permute-start(bf16[4,48,1536]{2,1,0:T(8,128)(2,1)S(1)} %get-tuple-element.117), channel_id=1, source_target_pairs={{0,8},{4,12},{8,0},{12,4},{1,9},{5,13},{9,1},{13,5},{2,10},{6,14},... | collective-permute-start | bytes 1769480 | tf_op jit(solution)/shard_map/ppermute | solution.py:1158
  226.5 7.1 %collective-permute-start.13 = (f32[32,768]{1,0:T(8,128)}, f32[32,768]{1,0:T(8,128)S(1)}, u32[]{:S(2)}, u32[]{:S(2)}) collective-permute-start(f32[32,768]{1,0:T(8,128)} %get-tuple-element.128), channel_id=1, source_target_pairs={{0,1},{1,0},{2,3},{3,2},{4,5},{5,4},{6,7},{7,6},{8,9},{9,8},{10,11... | collective-permute-start | bytes 294920 | tf_op jit(solution)/shard_map/ppermute | solution.py:1158
  228.0 10.0 %collective-permute-start.14 = (f32[32,768]{1,0:T(8,128)}, f32[32,768]{1,0:T(8,128)S(1)}, u32[]{:S(2)}, u32[]{:S(2)}) collective-permute-start(f32[32,768]{1,0:T(8,128)} %get-tuple-element.128), channel_id=1, source_target_pairs={{0,2},{1,3},{2,0},{3,1},{4,6},{5,7},{6,4},{7,5},{8,10},{9,11},{10,... | collective-permute-start | bytes 294920 | tf_op jit(solution)/shard_map/ppermute | solution.py:1158
  228.1 9.9 %collective-permute-start.15 = (f32[32,768]{1,0:T(8,128)}, f32[32,768]{1,0:T(8,128)S(1)}, u32[]{:S(2)}, u32[]{:S(2)}) collective-permute-start(f32[32,768]{1,0:T(8,128)} %get-tuple-element.128), channel_id=1, source_target_pairs={{0,3},{1,2},{2,1},{3,0},{4,7},{5,6},{6,5},{7,4},{8,11},{9,10},{10,... | collective-permute-start | bytes 294920 | tf_op jit(solution)/shard_map/ppermute | solution.py:1158
  231.0 7.4 %collective-permute-start.16 = (bf16[2,48,1536]{2,1,0:T(8,128)(2,1)S(1)}, bf16[2,48,1536]{2,1,0:T(8,128)(2,1)S(1)}, u32[]{:S(2)}, u32[]{:S(2)}) collective-permute-start(bf16[2,48,1536]{2,1,0:T(8,128)(2,1)S(1)} %add_convert_fusion.3), channel_id=1, source_target_pairs={{0,16},{16,0},{1,17},{17,1},{2,18},{18,2},{3,19},{19,3},{4,20},{20... | collective-permute-start | bytes 884744 | tf_op jit(solution)/shard_map/ppermute | solution.py:1158
  232.4 7.1 %collective-permute-start.17 = (bf16[2,48,1536]{2,1,0:T(8,128)(2,1)S(1)}, bf16[2,48,1536]{2,1,0:T(8,128)(2,1)S(1)}, u32[]{:S(2)}, u32[]{:S(2)}) collective-permute-start(bf16[2,48,1536]{2,1,0:T(8,128)(2,1)S(1)} %add_convert_fusion.1), channel_id=1, source_target_pairs={{0,8},{4,12},{8,0},{12,4},{1,9},{5,13},{9,1},{13,5},{2,10},{6,14},... | collective-permute-start | bytes 884744 | tf_op jit(solution)/shard_map/ppermute | solution.py:1158
  239.9 3.7 %collective-permute-start.18 = (f32[56,768]{1,0:T(8,128)S(1)}, f32[56,768]{1,0:T(8,128)S(1)}, u32[]{:S(2)}, u32[]{:S(2)}) collective-permute-start(f32[56,768]{1,0:T(8,128)S(1)} %get-tuple-element.134), channel_id=1, source_target_pairs={{0,4},{4,0},{8,12},{12,8},{1,5},{5,1},{9,13},{13,9},{2,6},{6,2},{1... | collective-permute-start | bytes 516104 | tf_op jit(solution)/shard_map/ppermute | solution.py:1158
  240.0 7.2 %collective-permute-start.19 = (f32[56,768]{1,0:T(8,128)S(1)}, f32[56,768]{1,0:T(8,128)S(1)}, u32[]{:S(2)}, u32[]{:S(2)}) collective-permute-start(f32[56,768]{1,0:T(8,128)S(1)} %get-tuple-element.134), channel_id=1, source_target_pairs={{0,8},{4,12},{8,0},{12,4},{1,9},{5,13},{9,1},{13,5},{2,10},{6,14},... | collective-permute-start | bytes 516104 | tf_op jit(solution)/shard_map/ppermute | solution.py:1158
  241.2 8.7 %collective-permute-start.20 = (f32[56,768]{1,0:T(8,128)S(1)}, f32[56,768]{1,0:T(8,128)S(1)}, u32[]{:S(2)}, u32[]{:S(2)}) collective-permute-start(f32[56,768]{1,0:T(8,128)S(1)} %get-tuple-element.134), channel_id=1, source_target_pairs={{0,12},{4,8},{8,4},{12,0},{1,13},{5,9},{9,5},{13,1},{2,14},{6,10},... | collective-permute-start | bytes 516104 | tf_op jit(solution)/shard_map/ppermute | solution.py:1158
  241.8 8.2 %collective-permute-start.22 = (bf16[48,1536]{1,0:T(8,128)(2,1)S(1)}, bf16[48,1536]{1,0:T(8,128)(2,1)S(1)}, u32[]{:S(2)}, u32[]{:S(2)}) collective-permute-start(bf16[48,1536]{1,0:T(8,128)(2,1)S(1)} %get-tuple-element.135), channel_id=1, source_target_pairs={{0,1},{1,0},{2,3},{3,2},{4,5},{5,4},{6,7},{7,6},{8,9},{9,8},{10,11... | collective-permute-start | bytes 442376 | tf_op jit(solution)/shard_map/ppermute | solution.py:1158
  242.4 14.0 %collective-permute-start.23 = (bf16[48,1536]{1,0:T(8,128)(2,1)S(1)}, bf16[48,1536]{1,0:T(8,128)(2,1)S(1)}, u32[]{:S(2)}, u32[]{:S(2)}) collective-permute-start(bf16[48,1536]{1,0:T(8,128)(2,1)S(1)} %get-tuple-element.136), channel_id=1, source_target_pairs={{0,2},{1,3},{2,0},{3,1},{4,6},{5,7},{6,4},{7,5},{8,10},{9,11},{10,... | collective-permute-start | bytes 442376 | tf_op jit(solution)/shard_map/ppermute | solution.py:1158
  243.6 12.8 %collective-permute-start.24 = (bf16[48,1536]{1,0:T(8,128)(2,1)S(1)}, bf16[48,1536]{1,0:T(8,128)(2,1)S(1)}, u32[]{:S(2)}, u32[]{:S(2)}) collective-permute-start(bf16[48,1536]{1,0:T(8,128)(2,1)S(1)} %get-tuple-element.137), channel_id=1, source_target_pairs={{0,3},{1,2},{2,1},{3,0},{4,7},{5,6},{6,5},{7,4},{8,11},{9,10},{10,... | collective-permute-start | bytes 442376 | tf_op jit(solution)/shard_map/ppermute | solution.py:1158
  256.4 13.0 %collective-permute-start.21 = (f32[20,768]{1,0:T(8,128)S(1)}, f32[20,768]{1,0:T(8,128)S(1)}, u32[]{:S(2)}, u32[]{:S(2)}) collective-permute-start(f32[20,768]{1,0:T(8,128)S(1)} %slice.225), channel_id=1, source_target_pairs={{0,16},{16,0},{1,17},{17,1},{2,18},{18,2},{3,19},{19,3},{4,20},{20... | collective-permute-start | bytes 184328 | tf_op jit(solution)/shard_map/ppermute | solution.py:1158
  259.2 10.3 %collective-permute-start.4 = (bf16[192,768]{1,0:T(8,128)(2,1)S(1)}, bf16[192,768]{1,0:T(8,128)(2,1)S(1)}, u32[]{:S(2)}, u32[]{:S(2)}) collective-permute-start(bf16[192,768]{1,0:T(8,128)(2,1)S(1)} %pad_maximum_fusion), channel_id=1, source_target_pairs={{0,16},{16,0},{1,17},{17,1},{2,18},{18,2},{3,19},{19,3},{4,20},{20... | collective-permute-start | bytes 884744 | tf_op jit(solution)/shard_map/ppermute | solution.py:1158
  (46 other events, 399.4 us)
Sparse Core Ops, SparseCore 0:
  95.4 127.4 reduce-scatter.1
